TPU v7x, 256 devices: a whole 4x4x8 slice. The times are simulated.
256 devices in a mesh: tm: 32 (over z, y), space: 8 (over x, core).
Axes of the slice: x: 4, y: 4, z: 8, core: 2. Of those that a mesh axis runs over, the one named last changes fastest.
Arguments:
- video: bfloat16 [128, 64, 64, 256], P('tm', 'space'), may hold values from -6 to 6
- cotangent: bfloat16 [128, 64, 64, 256], P('tm', 'space'), may hold values from -6 to 6
- frame_count: int32 [32], replicated, may hold values from 1 to 4, 96 in all
- row_count: int32 [8], replicated, may hold values from 1 to 8, 48 in all
- w_conv: bfloat16 [3, 3, 256, 256], replicated, may hold values from -0.125 to 0.125
- w_query: bfloat16 [256, 256], replicated, may hold values from -1 to 1
- w_key: bfloat16 [256, 256], replicated, may hold values from -1 to 1
- w_value: bfloat16 [256, 256], replicated, may hold values from -0.375 to 0.375
- w_out: bfloat16 [256, 256], replicated, may hold values from -0.375 to 0.375
Outputs:
- encoded: bfloat16 [128, 64, 64, 256], P('tm', 'space')
- video_grad: bfloat16 [128, 64, 64, 256], P('tm', 'space')
Inputs may be any that keep to these rules, and one draw needn't show every extreme that they name: `frame_count`: the counts sum to 3 times the number of time blocks, and the largest is 4. `row_count`: the counts sum to 6 times the number of spatial tiles, and the largest is 8.
All inputs are finite; a program needn't handle non-finite values.
Results may differ from a plain program's by a relative error of at most 0.011.
Values may be sent and summed in bfloat16 or wider, within the bound.
No kernel may reach another device: no remote copies, remote signals or barrier semaphores. Data moves between devices by JAX's collectives and lax.ppermute only.
A program may use at most 64 MiB of HBM per device.

v0:
```python
import jax
import jax.numpy as jnp
from jax import lax
from jax.sharding import PartitionSpec as P


def with_halo(cells, sides, width):
    for axis, dim in sides:
        count = lax.axis_size(axis)
        ends = count - 1
        head = lax.slice_in_dim(cells, 0, width, axis=dim)
        tail = lax.slice_in_dim(cells, cells.shape[dim] - width, cells.shape[dim], axis=dim)
        cells = jnp.concatenate(
            [
                lax.ppermute(tail, axis, [(i, (i + 1) % count) for i in range(ends)]),
                cells,
                lax.ppermute(head, axis, [((i + 1) % count, i) for i in range(ends)]),
            ],
            axis=dim,
        )
    return cells


def shift_cols(field):
    zero_col = jnp.zeros_like(field[:, :, :1])
    left = jnp.concatenate([zero_col, field[:, :, :-1]], axis=2)
    right = jnp.concatenate([field[:, :, 1:], zero_col], axis=2)
    return jnp.stack([left, field, right], axis=3)


def convolve(field, weight, rows_here):
    row_slots = field.shape[1]
    edges = jnp.concatenate(
        [field[:, :1], lax.dynamic_slice_in_dim(field, rows_here - 1, 1, axis=1)], axis=1
    )
    extended = with_halo(edges, (("space", 1),), 1)
    above = extended[:, 0:1]
    below = extended[:, 3:4]
    upper = jnp.concatenate([above, field[:, :-1]], axis=1)
    shifted = jnp.concatenate([field[:, 1:], jnp.zeros_like(field[:, :1])], axis=1)
    slot_index = jnp.arange(row_slots, dtype=jnp.int32)[None, :, None, None]
    lower = jnp.where(slot_index == rows_here - 1, below, shifted)
    total = jnp.zeros(field.shape, jnp.float32)
    for offset, view in enumerate((upper, field, lower)):
        total = total + jnp.einsum(
            "frwbc,bcd->frwd", shift_cols(view), weight[offset], preferred_element_type=jnp.float32
        )
    return total


def project(field, weight):
    return jnp.dot(field, weight, preferred_element_type=jnp.float32).astype(jnp.bfloat16)


def back_project(grads, weights):
    total = jnp.einsum("fpd,cd->fpc", grads[0], weights[0], preferred_element_type=jnp.float32)
    total = total + jnp.einsum(
        "fpd,cd->fpc", grads[1], weights[1], preferred_element_type=jnp.float32
    )
    total = total + jnp.einsum(
        "fpd,cd->fpc", grads[2], weights[2], preferred_element_type=jnp.float32
    )
    return total.astype(jnp.bfloat16)


def body(video, cotangent, frame_count, row_count, w_conv, w_query, w_key, w_value, w_out):
    frame_slots, row_slots, columns, channels = video.shape
    frames_here = frame_count[lax.axis_index("tm")]
    rows_here = row_count[lax.axis_index("space")]
    frame_used = jnp.arange(frame_slots, dtype=jnp.int32) < frames_here
    row_used = jnp.arange(row_slots, dtype=jnp.int32) < rows_here
    mask = (frame_used[:, None] & row_used[None, :]).astype(jnp.float32)[:, :, None, None]
    masked = (video.astype(jnp.float32) * mask).astype(jnp.bfloat16)
    hidden = ((masked.astype(jnp.float32) + convolve(masked, w_conv, rows_here)) * mask).astype(
        jnp.bfloat16
    )
    hidden_f = hidden.astype(jnp.float32)
    inv_rms = lax.rsqrt(jnp.mean(hidden_f * hidden_f, axis=-1, keepdims=True) + 1e-06)
    normed = (hidden_f * inv_rms).astype(jnp.bfloat16)
    positions = row_slots * columns
    flat = normed.reshape(frame_slots, positions, channels)
    queries = project(flat, w_query)
    key_rows = project(flat, w_key)
    value_rows = project(flat, w_value)
    queries, key_rows, value_rows = (
        lax.all_to_all(queries, "tm", split_axis=1, concat_axis=0, tiled=True),
        lax.all_to_all(key_rows, "tm", split_axis=1, concat_axis=0, tiled=True),
        lax.all_to_all(value_rows, "tm", split_axis=1, concat_axis=0, tiled=True),
    )
    all_frames = queries.shape[0]
    slot_index = jnp.arange(all_frames, dtype=jnp.int32)
    slot_used = slot_index % frame_slots < jnp.repeat(
        frame_count, frame_slots, total_repeat_length=all_frames
    )
    allowed = (slot_index[None, :] <= slot_index[:, None]) & slot_used[None, :]
    scale = channels ** (-0.5)
    scores = (
        jnp.einsum("fpc,gpc->pfg", queries, key_rows, preferred_element_type=jnp.float32) * scale
    )
    scores = jnp.where(allowed[None], scores, -1e30)
    top = jnp.max(scores, axis=-1, keepdims=True)
    expo = jnp.exp(scores - top)
    probs = expo / jnp.sum(expo, axis=-1, keepdims=True)
    probs_low = probs.astype(jnp.bfloat16)
    attended = jnp.einsum(
        "pfg,gpc->fpc", probs_low, value_rows, preferred_element_type=jnp.float32
    ).astype(jnp.bfloat16)
    attended_home = lax.all_to_all(attended, "tm", split_axis=0, concat_axis=1, tiled=True)
    projected = project(attended_home, w_out)
    projected = projected.reshape(frame_slots, row_slots, columns, channels)
    encoded = ((hidden_f + projected.astype(jnp.float32)) * mask).astype(jnp.bfloat16)
    grad_out = (cotangent.astype(jnp.float32) * mask).astype(jnp.bfloat16)
    grad_home = jnp.einsum(
        "fpd,cd->fpc",
        grad_out.reshape(frame_slots, positions, channels),
        w_out,
        preferred_element_type=jnp.float32,
    ).astype(jnp.bfloat16)
    grad_attended = lax.all_to_all(grad_home, "tm", split_axis=1, concat_axis=0, tiled=True)
    grad_probs = jnp.einsum(
        "fpc,gpc->pfg", grad_attended, value_rows, preferred_element_type=jnp.float32
    )
    delta = jnp.sum(grad_attended.astype(jnp.float32) * attended.astype(jnp.float32), axis=-1).T[
        :, :, None
    ]
    grad_scores = (probs * (grad_probs - delta) * scale).astype(jnp.bfloat16)
    grad_queries = jnp.einsum(
        "pfg,gpc->fpc", grad_scores, key_rows, preferred_element_type=jnp.float32
    ).astype(jnp.bfloat16)
    grad_keys = jnp.einsum(
        "pfg,fpc->gpc", grad_scores, queries, preferred_element_type=jnp.float32
    ).astype(jnp.bfloat16)
    grad_values = jnp.einsum(
        "pfg,fpc->gpc", probs_low, grad_attended, preferred_element_type=jnp.float32
    ).astype(jnp.bfloat16)
    grad_queries, grad_keys, grad_values = (
        lax.all_to_all(grad_queries, "tm", split_axis=0, concat_axis=1, tiled=True),
        lax.all_to_all(grad_keys, "tm", split_axis=0, concat_axis=1, tiled=True),
        lax.all_to_all(grad_values, "tm", split_axis=0, concat_axis=1, tiled=True),
    )
    grad_normed = back_project((grad_queries, grad_keys, grad_values), (w_query, w_key, w_value))
    grad_normed = grad_normed.reshape(frame_slots, row_slots, columns, channels).astype(jnp.float32)
    inner = jnp.mean(grad_normed * hidden_f, axis=-1, keepdims=True)
    grad_hidden = (
        mask
        * (grad_out.astype(jnp.float32) + inv_rms * grad_normed - inv_rms**3 * hidden_f * inner)
    ).astype(jnp.bfloat16)
    flipped = jnp.transpose(jnp.flip(w_conv, (0, 1)), (0, 1, 3, 2))
    video_grad = (
        mask * (grad_hidden.astype(jnp.float32) + convolve(grad_hidden, flipped, rows_here))
    ).astype(jnp.bfloat16)
    return (encoded, video_grad)


def solution(mesh):
    in_specs = (
        P("tm", "space", None, None),
        P("tm", "space", None, None),
        P(),
        P(),
        P(),
        P(),
        P(),
        P(),
        P(),
    )
    out_specs = (P("tm", "space", None, None), P("tm", "space", None, None))
    return jax.shard_map(body, mesh=mesh, in_specs=in_specs, out_specs=out_specs, check_vma=False)
```

profile of v0, /device:TPU:10, one launch (start us, length us, event | category | flops | bytes accessed | tf_op | source)
XLA Modules:
  0.0 320.5 jit_solution(7043034270033585974)
XLA Ops:
  0.6 1.3 dynamic_slice.13
  2.6 1.2 dynamic_slice.12
  5.9 2.5 multiply_convert_fusion
  8.4 1.9 collective-permute-start.1
  10.4 2.4 collective-permute-start
  13.2 1.8 copy.120
  15.0 11.7 %all-to-all-start.4 = ((bf16[4,512,256]{2,0,1:T(4,128)(2,1)}), bf16[4,512,256]{2,0,1:T(4,128)(2,1)S(1)}, u32[]{:S(2)}, u32[]{:S(2)}) async-start(bf16[4,512,256]{2,0,1:T(4,128)(2,1)} %copy.120), calls=%async_computation.4 | async-start | bytes 2097152 | tf_op jit(solution)/shard_map/all_to_all | solution.py:119
  28.7 1.0 fusion.15
  30.4 0.7 fusion.80
  32.8 1.0 fusion.13
  33.8 1.5 fusion.21
  36.7 1.8 copy.114
  38.5 17.0 %all-to-all-done.4 = bf16[4,512,256]{2,0,1:T(4,128)(2,1)S(1)} async-done(((bf16[4,512,256]{2,0,1:T(4,128)(2,1)}), bf16[4,512,256]{2,0,1:T(4,128)(2,1)S(1)}, u32[]{:S(2)}, u32[]{:S(2)}) %all-to-all-start.4) | async-done | bytes 1048608 | tf_op jit(solution)/shard_map/all_to_all | solution.py:119
  55.5 6.2 %all-to-all-start.2 = ((bf16[4,512,256]{2,0,1:T(4,128)(2,1)}), bf16[4,512,256]{2,0,1:T(4,128)(2,1)}, u32[]{:S(2)}, u32[]{:S(2)}) async-start(bf16[4,512,256]{2,0,1:T(4,128)(2,1)} %copy.114), calls=%async_computation.2 | async-start | bytes 2097152 | tf_op jit(solution)/shard_map/all_to_all | solution.py:87
  62.2 1.8 copy.109
  63.9 25.6 %all-to-all-done.2 = bf16[4,512,256]{2,0,1:T(4,128)(2,1)} async-done(((bf16[4,512,256]{2,0,1:T(4,128)(2,1)}), bf16[4,512,256]{2,0,1:T(4,128)(2,1)}, u32[]{:S(2)}, u32[]{:S(2)}) %all-to-all-start.2) | async-done | bytes 1048608 | tf_op jit(solution)/shard_map/all_to_all | solution.py:87
  89.5 5.6 %all-to-all-start = ((bf16[4,512,256]{2,0,1:T(4,128)(2,1)}), bf16[4,512,256]{2,0,1:T(4,128)(2,1)}, u32[]{:S(2)}, u32[]{:S(2)}) async-start(bf16[4,512,256]{2,0,1:T(4,128)(2,1)} %copy.109), calls=%async_computation | async-start | bytes 2097152 | tf_op jit(solution)/shard_map/all_to_all | solution.py:88
  95.6 1.8 copy.112
  97.4 24.6 %all-to-all-done = bf16[4,512,256]{2,0,1:T(4,128)(2,1)} async-done(((bf16[4,512,256]{2,0,1:T(4,128)(2,1)}), bf16[4,512,256]{2,0,1:T(4,128)(2,1)}, u32[]{:S(2)}, u32[]{:S(2)}) %all-to-all-start) | async-done | bytes 1048608 | tf_op jit(solution)/shard_map/all_to_all | solution.py:88
  122.0 5.6 %all-to-all-start.1 = ((bf16[4,512,256]{2,0,1:T(4,128)(2,1)}), bf16[4,512,256]{2,0,1:T(4,128)(2,1)}, u32[]{:S(2)}, u32[]{:S(2)}) async-start(bf16[4,512,256]{2,0,1:T(4,128)(2,1)} %copy.112), calls=%async_computation.1 | async-start | bytes 2097152 | tf_op jit(solution)/shard_map/all_to_all | solution.py:86
  127.7 1.2 gather_fusion
  129.3 1.7 copy.125
  131.0 1.7 copy.187
  133.0 1.4 copy.110
  134.4 1.1 copy.111
  135.5 18.7 %all-to-all-done.1 = bf16[4,512,256]{2,0,1:T(4,128)(2,1)} async-done(((bf16[4,512,256]{2,0,1:T(4,128)(2,1)}), bf16[4,512,256]{2,0,1:T(4,128)(2,1)}, u32[]{:S(2)}, u32[]{:S(2)}) %all-to-all-start.1) | async-done | bytes 1048608 | tf_op jit(solution)/shard_map/all_to_all | solution.py:86
  154.2 2.7 copy.188
  156.8 1.3 all_to_all.111
  158.6 1.0 copy-done.2
  159.6 1.2 fusion.81
  160.8 4.0 %multiply_reduce_fusion = (f32[128,16]{0,1:T(8,128)S(1)}, bf16[128,16,256]{0,2,1:T(8,128)(2,1)}) fusion(bf16[128,16,256]{0,2,1:T(8,128)(2,1)} %copy.125, f32[16,128]{1,0:T(8,128)S(1)} %get-tuple-element.42, f32[16,128,128]{1,2,0:T(8,128)} %copy-done.2, bf16[128,16,256]{2,1,0:T(8,128)(2,1)} %bitcast.228), kind=kOutput, calls=%fused_computation.50 | convolution fusion | flops 137625728 | bytes 4210688 | tf_op jit(solution)/shard_map/pfg,gpc->fpc/dot_general | solution.py:105
  164.8 2.5 fusion.44
  167.3 0.8 copy-done.10
  168.1 1.5 fusion.41
  169.5 2.7 copy.129
  172.2 5.6 %all-to-all-start.5 = ((bf16[128,16,256]{2,1,0:T(8,128)(2,1)}), bf16[128,16,256]{2,1,0:T(8,128)(2,1)S(1)}, u32[]{:S(2)}, u32[]{:S(2)}) async-start(bf16[128,16,256]{2,1,0:T(8,128)(2,1)} %copy.129), calls=%async_computation.5 | async-start | bytes 2097152 | tf_op jit(solution)/shard_map/all_to_all | solution.py:137
  177.8 2.5 fusion.42
  180.3 2.6 copy.133
  182.9 21.4 %all-to-all-done.5 = bf16[128,16,256]{2,1,0:T(8,128)(2,1)S(1)} async-done(((bf16[128,16,256]{2,1,0:T(8,128)(2,1)}), bf16[128,16,256]{2,1,0:T(8,128)(2,1)S(1)}, u32[]{:S(2)}, u32[]{:S(2)}) %all-to-all-start.5) | async-done | bytes 1048608 | tf_op jit(solution)/shard_map/all_to_all | solution.py:137
  204.3 5.6 %all-to-all-start.6 = ((bf16[128,16,256]{2,1,0:T(8,128)(2,1)}), bf16[128,16,256]{2,1,0:T(8,128)(2,1)S(1)}, u32[]{:S(2)}, u32[]{:S(2)}) async-start(bf16[128,16,256]{2,1,0:T(8,128)(2,1)} %copy.133), calls=%async_computation.6 | async-start | bytes 2097152 | tf_op jit(solution)/shard_map/all_to_all | solution.py:138
  209.9 3.3 %fusion.43 = bf16[128,16,256]{0,2,1:T(8,128)(2,1)} fusion(bf16[128,16,256]{0,2,1:T(8,128)(2,1)} %copy.125, f32[16,128]{1,0:T(8,128)S(1)} %get-tuple-element.42, f32[16,128,128]{1,2,0:T(8,128)} %copy-done.2), kind=kOutput, calls=%fused_computation.78 | convolution fusion | flops 135530624 | bytes 3153920 | tf_op jit(solution)/shard_map/pfg,fpc->gpc/dot_general | solution.py:133
  213.2 2.7 copy.137
  215.9 20.5 %all-to-all-done.6 = bf16[128,16,256]{2,1,0:T(8,128)(2,1)S(1)} async-done(((bf16[128,16,256]{2,1,0:T(8,128)(2,1)}), bf16[128,16,256]{2,1,0:T(8,128)(2,1)S(1)}, u32[]{:S(2)}, u32[]{:S(2)}) %all-to-all-start.6) | async-done | bytes 1048608 | tf_op jit(solution)/shard_map/all_to_all | solution.py:138
  236.4 5.6 %all-to-all-start.7 = ((bf16[128,16,256]{2,1,0:T(8,128)(2,1)}), bf16[128,16,256]{2,1,0:T(8,128)(2,1)S(1)}, u32[]{:S(2)}, u32[]{:S(2)}) async-start(bf16[128,16,256]{2,1,0:T(8,128)(2,1)} %copy.137), calls=%async_computation.7 | async-start | bytes 2097152 | tf_op jit(solution)/shard_map/all_to_all | solution.py:139
  242.0 2.7 copy.118
  244.7 23.8 %all-to-all-done.7 = bf16[128,16,256]{2,1,0:T(8,128)(2,1)S(1)} async-done(((bf16[128,16,256]{2,1,0:T(8,128)(2,1)}), bf16[128,16,256]{2,1,0:T(8,128)(2,1)S(1)}, u32[]{:S(2)}, u32[]{:S(2)}) %all-to-all-start.7) | async-done | bytes 1048608 | tf_op jit(solution)/shard_map/all_to_all | solution.py:139
  268.5 1.0 copy-done.7
  269.5 5.6 %all-to-all-start.3 = ((bf16[128,16,256]{2,1,0:T(8,128)(2,1)}), bf16[128,16,256]{2,1,0:T(8,128)(2,1)}, u32[]{:S(2)}, u32[]{:S(2)}) async-start(bf16[128,16,256]{2,1,0:T(8,128)(2,1)} %copy.118), calls=%async_computation.3 | async-start | bytes 2097152 | tf_op jit(solution)/shard_map/all_to_all | solution.py:108
  275.1 1.7 copy.139
  276.8 1.1 reverse_bitcast_fusion
  278.5 0.7 copy-done.8
  281.5 20.1 %all-to-all-done.3 = bf16[128,16,256]{2,1,0:T(8,128)(2,1)} async-done(((bf16[128,16,256]{2,1,0:T(8,128)(2,1)}), bf16[128,16,256]{2,1,0:T(8,128)(2,1)}, u32[]{:S(2)}, u32[]{:S(2)}) %all-to-all-start.3) | async-done | bytes 1048608 | tf_op jit(solution)/shard_map/all_to_all | solution.py:108
  301.7 1.4 copy.119
  303.5 2.2 fusion.20
  306.4 1.9 collective-permute-start.3
  308.5 0.7 pad_bitcast_fusion.3
  309.2 2.4 collective-permute-start.2
  311.6 1.0 fusion.9
  313.5 0.7 fusion.77
  314.4 0.7 pad_bitcast_fusion.1
  315.9 0.7 pad_bitcast_fusion.5
  316.6 1.0 fusion.7
  317.7 1.0 fusion.11
  318.8 1.8 fusion.29
  (94 shorter events, 15.4 us)
Async XLA Ops:
  0.6 94.5 %copy-start = (bf16[256,256]{1,0:T(8,128)(2,1)S(1)}, bf16[256,256]{1,0:T(8,128)(2,1)}, u32[]{:S(2)}) copy-start(bf16[256,256]{1,0:T(8,128)(2,1)} %param.16) | copy-start | bytes 393220
  5.9 27.9 %copy-start.19 = (f32[4,8]{1,0:T(4,128)}, f32[4,8]{1,0:T(4,128)S(1)}, u32[]{:S(2)}) copy-start(f32[4,8]{1,0:T(4,128)S(1)} %and_convert_fusion) | copy-start | bytes 388
  5.9 6.9 %copy-start.16 = (bf16[256,256]{1,0:T(8,128)(2,1)S(1)}, bf16[256,256]{1,0:T(8,128)(2,1)}, u32[]{:S(2)}) copy-start(bf16[256,256]{1,0:T(8,128)(2,1)} %param.19) | copy-start | bytes 393220
  8.4 21.5 %collective-permute-start.1 = (bf16[4,1,64,256]{3,2,1,0:T(8,128)(2,1)S(1)}, bf16[4,1,64,256]{3,2,1,0:T(8,128)(2,1)S(1)}, u32[]{:S(2)}, u32[]{:S(2)}) collective-permute-start(bf16[4,1,64,256]{3,2,1,0:T(8,128)(2,1)S(1)} %get-tuple-element.31), channel_id=1, source_target_pairs={{1,0},{2,1},{3,2},{4,3},{5,4},{6,5},{7,6},{9,8},{10,9},{11,10},{12... | collective-permute-start | bytes 393224 | tf_op jit(solution)/shard_map/ppermute | solution.py:17
  10.4 21.4 %collective-permute-start = (bf16[4,1,64,256]{3,2,1,0:T(8,128)(2,1)S(1)}, bf16[4,1,64,256]{3,2,1,0:T(8,128)(2,1)S(1)}, u32[]{:S(2)}, u32[]{:S(2)}) collective-permute-start(bf16[4,1,64,256]{3,2,1,0:T(8,128)(2,1)S(1)} %get-tuple-element.30), channel_id=1, source_target_pairs={{0,1},{1,2},{2,3},{3,4},{4,5},{5,6},{6,7},{8,9},{9,10},{10,11},{11... | collective-permute-start | bytes 393224 | tf_op jit(solution)/shard_map/ppermute | solution.py:15
  15.0 40.5 %all-to-all-start.4 = ((bf16[4,512,256]{2,0,1:T(4,128)(2,1)}), bf16[4,512,256]{2,0,1:T(4,128)(2,1)S(1)}, u32[]{:S(2)}, u32[]{:S(2)}) async-start(bf16[4,512,256]{2,0,1:T(4,128)(2,1)} %copy.120), calls=%async_computation.4 | async-start | bytes 2097152 | tf_op jit(solution)/shard_map/all_to_all | solution.py:119
  27.4 1.3 copy-start.11
  29.9 0.5 copy-start.21
  35.3 1.0 copy-start.13
  36.7 25.1 %copy-start.14 = (bf16[256,256]{1,0:T(8,128)(2,1)S(1)}, bf16[256,256]{1,0:T(8,128)(2,1)}, u32[]{:S(2)}) copy-start(bf16[256,256]{1,0:T(8,128)(2,1)} %param.18) | copy-start | bytes 393220
  55.5 34.0 %all-to-all-start.2 = ((bf16[4,512,256]{2,0,1:T(4,128)(2,1)}), bf16[4,512,256]{2,0,1:T(4,128)(2,1)}, u32[]{:S(2)}, u32[]{:S(2)}) async-start(bf16[4,512,256]{2,0,1:T(4,128)(2,1)} %copy.114), calls=%async_computation.2 | async-start | bytes 2097152 | tf_op jit(solution)/shard_map/all_to_all | solution.py:87
  89.5 32.5 %all-to-all-start = ((bf16[4,512,256]{2,0,1:T(4,128)(2,1)}), bf16[4,512,256]{2,0,1:T(4,128)(2,1)}, u32[]{:S(2)}, u32[]{:S(2)}) async-start(bf16[4,512,256]{2,0,1:T(4,128)(2,1)} %copy.109), calls=%async_computation | async-start | bytes 2097152 | tf_op jit(solution)/shard_map/all_to_all | solution.py:88
  95.6 32.0 %copy-start.23 = (s32[128]{0:T(128)S(1)}, s32[128]{0:T(128)}, u32[]{:S(2)}) copy-start(s32[128]{0:T(128)} %constant.159) | copy-start | bytes 1540
  95.6 32.0 %copy-start.1 = (s32[32]{0:T(128)S(1)}, s32[32]{0:T(128)}, u32[]{:S(2)}) copy-start(s32[32]{0:T(128)} %param.13) | copy-start | bytes 388
  122.0 32.2 %all-to-all-start.1 = ((bf16[4,512,256]{2,0,1:T(4,128)(2,1)}), bf16[4,512,256]{2,0,1:T(4,128)(2,1)}, u32[]{:S(2)}, u32[]{:S(2)}) async-start(bf16[4,512,256]{2,0,1:T(4,128)(2,1)} %copy.112), calls=%async_computation.1 | async-start | bytes 2097152 | tf_op jit(solution)/shard_map/all_to_all | solution.py:86
  158.6 1.0 copy-start.2
  167.3 0.8 copy-start.10
  172.2 32.1 %all-to-all-start.5 = ((bf16[128,16,256]{2,1,0:T(8,128)(2,1)}), bf16[128,16,256]{2,1,0:T(8,128)(2,1)S(1)}, u32[]{:S(2)}, u32[]{:S(2)}) async-start(bf16[128,16,256]{2,1,0:T(8,128)(2,1)} %copy.129), calls=%async_computation.5 | async-start | bytes 2097152 | tf_op jit(solution)/shard_map/all_to_all | solution.py:137
  204.3 8.9 %copy-start.3 = (bf16[128,16,256]{2,1,0:T(8,128)(2,1)}, bf16[128,16,256]{2,1,0:T(8,128)(2,1)S(1)}, u32[]{:S(2)}) copy-start(bf16[128,16,256]{2,1,0:T(8,128)(2,1)S(1)} %all-to-all-done.5) | copy-start | bytes 3145732
  204.3 32.1 %all-to-all-start.6 = ((bf16[128,16,256]{2,1,0:T(8,128)(2,1)}), bf16[128,16,256]{2,1,0:T(8,128)(2,1)S(1)}, u32[]{:S(2)}, u32[]{:S(2)}) async-start(bf16[128,16,256]{2,1,0:T(8,128)(2,1)} %copy.133), calls=%async_computation.6 | async-start | bytes 2097152 | tf_op jit(solution)/shard_map/all_to_all | solution.py:138
  236.4 8.3 %copy-start.5 = (bf16[128,16,256]{2,1,0:T(8,128)(2,1)}, bf16[128,16,256]{2,1,0:T(8,128)(2,1)S(1)}, u32[]{:S(2)}) copy-start(bf16[128,16,256]{2,1,0:T(8,128)(2,1)S(1)} %all-to-all-done.6) | copy-start | bytes 3145732
  236.4 32.1 %all-to-all-start.7 = ((bf16[128,16,256]{2,1,0:T(8,128)(2,1)}), bf16[128,16,256]{2,1,0:T(8,128)(2,1)S(1)}, u32[]{:S(2)}, u32[]{:S(2)}) async-start(bf16[128,16,256]{2,1,0:T(8,128)(2,1)} %copy.137), calls=%async_computation.7 | async-start | bytes 2097152 | tf_op jit(solution)/shard_map/all_to_all | solution.py:139
  268.5 1.0 copy-start.7
  269.5 32.2 %all-to-all-start.3 = ((bf16[128,16,256]{2,1,0:T(8,128)(2,1)}), bf16[128,16,256]{2,1,0:T(8,128)(2,1)}, u32[]{:S(2)}, u32[]{:S(2)}) async-start(bf16[128,16,256]{2,1,0:T(8,128)(2,1)} %copy.118), calls=%async_computation.3 | async-start | bytes 2097152 | tf_op jit(solution)/shard_map/all_to_all | solution.py:108
  275.1 2.8 copy-start.4
  276.8 1.7 copy-start.6
  277.9 1.3 copy-start.8
  279.8 0.9 copy-start.15
  281.2 21.9 %copy-start.17 = (bf16[256,256]{1,0:T(8,128)(2,1)S(1)}, bf16[256,256]{1,0:T(8,128)(2,1)}, u32[]{:S(2)}) copy-start(bf16[256,256]{1,0:T(8,128)(2,1)} %param.19) | copy-start | bytes 393220
  301.6 1.9 copy-start.9
  301.6 1.9 copy-start.18
  301.6 1.9 copy-start.20
  306.4 6.4 %collective-permute-start.3 = (bf16[4,1,64,256]{3,2,1,0:T(8,128)(2,1)S(1)}, bf16[4,1,64,256]{3,2,1,0:T(8,128)(2,1)S(1)}, u32[]{:S(2)}, u32[]{:S(2)}) collective-permute-start(bf16[4,1,64,256]{3,2,1,0:T(8,128)(2,1)S(1)} %get-tuple-element.21), channel_id=1, source_target_pairs={{1,0},{2,1},{3,2},{4,3},{5,4},{6,5},{7,6},{9,8},{10,9},{11,10},{12... | collective-permute-start | bytes 393224 | tf_op jit(solution)/shard_map/ppermute | solution.py:17
  308.4 3.2 %copy-start.12 = (bf16[3,3,256,256]{3,2,1,0:T(8,128)(2,1)S(1)}, bf16[3,3,256,256]{3,2,1,0:T(8,128)(2,1)}, u32[]{:S(2)}) copy-start(bf16[3,3,256,256]{3,2,1,0:T(8,128)(2,1)} %reverse_bitcast_fusion) | copy-start | bytes 3538948
  309.2 6.3 %collective-permute-start.2 = (bf16[4,1,64,256]{3,2,1,0:T(8,128)(2,1)S(1)}, bf16[4,1,64,256]{3,2,1,0:T(8,128)(2,1)S(1)}, u32[]{:S(2)}, u32[]{:S(2)}) collective-permute-start(bf16[4,1,64,256]{3,2,1,0:T(8,128)(2,1)S(1)} %get-tuple-element.20), channel_id=1, source_target_pairs={{0,1},{1,2},{2,3},{3,4},{4,5},{5,6},{6,7},{8,9},{9,10},{10,11},{11... | collective-permute-start | bytes 393224 | tf_op jit(solution)/shard_map/ppermute | solution.py:15
  312.6 0.6 copy-start.22
where the time goes:
time: 324 us; the launch traced here: 321 us
  waiting for transfers between devices  172 us (53%)
  starting transfers between devices  60.1 us (19%)
  local copies, waits for them, and re-layouts  49.5 us (15%)
  matrix products  24.2 us (7%)
  other arithmetic  11.9 us (4%)
    all_to_all x1, waiting for transfers between devices, body(): lax.all_to_all(key_rows, 'tm', split_axis=1, concat_axis=0, tiled=True)  25.6 us
    all_to_all x1, waiting for transfers between devices, body(): lax.all_to_all(value_rows, 'tm', split_axis=1, concat_axis=0, tiled=True)  24.6 us
    all_to_all x1, waiting for transfers between devices, body(): lax.all_to_all(grad_values, 'tm', split_axis=0, concat_axis=1, tiled=True)  23.8 us
    all_to_all x1, waiting for transfers between devices, body(): lax.all_to_all(grad_queries, 'tm', split_axis=0, concat_axis=1, tiled=True)  21.4 us
    all_to_all x1, waiting for transfers between devices, body(): lax.all_to_all(grad_keys, 'tm', split_axis=0, concat_axis=1, tiled=True)  20.5 us
    all_to_all x1, waiting for transfers between devices, body(): lax.all_to_all(attended, 'tm', split_axis=0, concat_axis=1, tiled=True)  20.1 us
    all_to_all x1, waiting for transfers between devices, body(): lax.all_to_all(queries, 'tm', split_axis=1, concat_axis=0, tiled=True)  18.7 us
    all_to_all x1, waiting for transfers between devices, body(): lax.all_to_all(grad_home, 'tm', split_axis=1, concat_axis=0, tiled=True)  17 us
  transfers between devices with their start and end apart: 12, of which 9 were waited for; matrix products, arithmetic and copies ran while one was open for 15% of the time, Pallas kernels for 0%

commit v1 on v0

v1 whole, which is shorter than its diff:
```python
import functools

import jax
import jax.numpy as jnp
from jax import lax
from jax.experimental import pallas as pl
from jax.experimental.pallas import tpu as pltpu
from jax.sharding import PartitionSpec as P

BF16 = jnp.bfloat16
F32 = jnp.float32
GROUP = 4
LANES = 128
VMEM = pltpu.VMEM
SMEM = pltpu.SMEM


def dot(a, b, contract=(1, 0)):
    return lax.dot_general(
        a, b, (((contract[0],), (contract[1],)), ((), ())), preferred_element_type=F32
    )


def specs(*spaces):
    return [pl.BlockSpec(memory_space=space) for space in spaces]


def cost(flops, moved):
    return pl.CostEstimate(flops=flops, bytes_accessed=moved, transcendentals=0)


def edges_kernel(row_count, field, head, tail, sems):
    rows_here = row_count[lax.axis_index("space")]
    first = pltpu.make_async_copy(field.at[:, 0], head, sems.at[0])
    last = pltpu.make_async_copy(field.at[:, rows_here - 1], tail, sems.at[1])
    first.start()
    last.start()
    first.wait()
    last.wait()


def fill_halo(extended, field, above, below, rows_here):
    slots = field.shape[1]
    extended[:, 1 : 1 + slots] = field[...]
    extended[:, 0] = above[...]
    extended[:, 1 + rows_here] = below[...]


def convolve_frame(extended, weight, frame, flipped):
    _, padded, columns, channels = extended.shape
    tokens = (padded - 2) * columns
    column = lax.broadcasted_iota(jnp.int32, (tokens, channels), 0) % columns
    total = None
    for b in range(3):
        part = None
        for a in range(3):
            view = extended[frame, a : a + padded - 2].reshape(tokens, channels)
            if flipped:
                term = dot(view, weight[2 - a, 2 - b], (1, 1))
            else:
                term = dot(view, weight[a, b])
            part = term if part is None else part + term
        if b == 0:
            part = jnp.where(column == 0, 0.0, pltpu.roll(part, 1, 0))
        elif b == 2:
            part = jnp.where(column == columns - 1, 0.0, pltpu.roll(part, tokens - 1, 0))
        total = part if total is None else total + part
    return total


def token_mask(frame, frames_here, rows_here, columns, shape):
    row = lax.broadcasted_iota(jnp.int32, shape, 0) // columns
    return (row < rows_here) & (frame < frames_here)


def inverse_rms(hidden):
    return lax.rsqrt(jnp.mean(hidden * hidden, axis=-1, keepdims=True) + 1e-06)


def hidden_kernel(
    frame_count, row_count, field, above, below, weight, hidden_out, normed_out, extended
):
    frames_here = frame_count[lax.axis_index("tm")]
    rows_here = row_count[lax.axis_index("space")]
    frames, slots, columns, channels = field.shape
    tokens = slots * columns
    fill_halo(extended, field, above, below, rows_here)

    def step(frame, carry):
        total = convolve_frame(extended, weight, frame, False)
        used = token_mask(frame, frames_here, rows_here, columns, total.shape)
        center = field[frame].reshape(tokens, channels).astype(F32)
        hidden = jnp.where(used, center + total, 0.0).astype(BF16)
        hidden_out[:, frame] = hidden.reshape(hidden_out.shape[0], -1, channels)
        hidden_f = hidden.astype(F32)
        normed = (hidden_f * inverse_rms(hidden_f)).astype(BF16)
        normed_out[:, frame] = normed.reshape(normed_out.shape[0], -1, channels)
        return carry

    lax.fori_loop(0, frames, step, 0)


def by_position(source, spread, target, scale=None):
    frames, positions, channels = source.shape
    for h in range(channels // LANES):
        lanes = slice(h * LANES, (h + 1) * LANES)
        part = source[:, :, lanes].astype(F32)
        spread[h] = part.reshape(frames * positions, LANES)
        for p in range(positions):
            rows = spread[h, pl.ds(p, frames, stride=positions), :]
            if scale is not None:
                rows = rows * scale
            target[p, :, lanes] = rows.astype(BF16)


def scatter_position(spread, position, positions, rows):
    for h in range(spread.shape[0]):
        part = rows[:, h * LANES : (h + 1) * LANES]
        spread[h, pl.ds(position, rows.shape[0], stride=positions), :] = part


def gather_frames(spread, target):
    for h in range(spread.shape[0]):
        part = spread[h].reshape(target.shape[0], target.shape[1], LANES)
        target[:, :, h * LANES : (h + 1) * LANES] = part.astype(BF16)


def grads_kernel(cotangent, used, w_out, grad_out, spread, ordered):
    by_position(cotangent, spread, ordered, used[...])
    positions, frames, channels = ordered.shape

    def step(i, carry):
        rows = ordered[pl.ds(i * GROUP, GROUP)].reshape(GROUP * frames, channels)
        grads = dot(rows, w_out[...], (1, 1)).astype(BF16)
        grad_out[pl.ds(i * GROUP, GROUP)] = grads.reshape(GROUP, frames, channels)
        return carry

    lax.fori_loop(0, positions // GROUP, step, 0)


def attention_kernel(
    normed, grads, used, w_query, w_key, w_value, attended, grad_normed,
    spread, ordered, query_s, key_s, value_s, dq_s, dk_s, dv_s,
):
    all_frames, positions, channels = normed.shape
    by_position(normed, spread, ordered)
    tile = (all_frames, all_frames)
    source = lax.broadcasted_iota(jnp.int32, tile, 0)
    reader = lax.broadcasted_iota(jnp.int32, tile, 1)
    allowed = (source <= reader) & (used[...] > 0.0)
    scale = channels ** (-0.5)

    def step(i, carry):
        rows = ordered[pl.ds(i * GROUP, GROUP)].reshape(GROUP * all_frames, channels)
        query_s[...] = dot(rows, w_query[...]).astype(BF16)
        key_s[...] = dot(rows, w_key[...]).astype(BF16)
        value_s[...] = dot(rows, w_value[...]).astype(BF16)
        for j in range(GROUP):
            here = pl.ds(j * all_frames, all_frames)
            query, key, value = query_s[here], key_s[here], value_s[here]
            grad = grads[i * GROUP + j]
            scores = jnp.where(allowed, dot(key, query, (1, 1)) * scale, -1e30)
            expo = jnp.exp(scores - jnp.max(scores, axis=0, keepdims=True))
            probs = expo * (1.0 / jnp.sum(expo, axis=0, keepdims=True))
            low = probs.astype(BF16)
            attended[i * GROUP + j] = dot(low, value, (0, 0)).astype(BF16)
            grad_probs = dot(value, grad, (1, 1))
            delta = jnp.sum(low.astype(F32) * grad_probs, axis=0, keepdims=True)
            grad_scores = (probs * (grad_probs - delta) * scale).astype(BF16)
            dv_s[here] = dot(low, grad).astype(BF16)
            dk_s[here] = dot(grad_scores, query).astype(BF16)
            dq_s[here] = dot(grad_scores, key, (0, 0)).astype(BF16)
        total = dot(dq_s[...], w_query[...], (1, 1))
        total = total + dot(dk_s[...], w_key[...], (1, 1))
        total = total + dot(dv_s[...], w_value[...], (1, 1))
        total = total.astype(BF16).astype(F32)
        for j in range(GROUP):
            rows = total[j * all_frames : (j + 1) * all_frames]
            scatter_position(spread, i * GROUP + j, positions, rows)
        return carry

    lax.fori_loop(0, positions // GROUP, step, 0)
    gather_frames(spread, grad_normed)


def project_kernel(attended, w_out, projected, spread):
    positions, frames, channels = attended.shape

    def step(i, carry):
        rows = attended[pl.ds(i * GROUP, GROUP)].reshape(GROUP * frames, channels)
        total = dot(rows, w_out[...]).astype(BF16).astype(F32)
        for j in range(GROUP):
            part = total[j * frames : (j + 1) * frames]
            scatter_position(spread, i * GROUP + j, positions, part)
        return carry

    lax.fori_loop(0, positions // GROUP, step, 0)
    gather_frames(spread, projected)


def encode_kernel(frame_count, row_count, hidden, projected, encoded):
    frames_here = frame_count[lax.axis_index("tm")]
    rows_here = row_count[lax.axis_index("space")]
    frames, slots, columns, channels = encoded.shape
    tokens = slots * columns

    def step(frame, carry):
        total = hidden[:, frame].astype(F32) + projected[:, frame].astype(F32)
        total = total.reshape(tokens, channels)
        used = token_mask(frame, frames_here, rows_here, columns, total.shape)
        total = jnp.where(used, total, 0.0).astype(BF16)
        encoded[frame] = total.reshape(slots, columns, channels)
        return carry

    lax.fori_loop(0, frames, step, 0)


def grad_hidden_kernel(
    frame_count, row_count, cotangent, hidden, grad_normed, grad_hidden, head, tail
):
    frames_here = frame_count[lax.axis_index("tm")]
    rows_here = row_count[lax.axis_index("space")]
    frames, slots, columns, channels = cotangent.shape
    tokens = slots * columns

    def step(frame, carry):
        hid = hidden[:, frame].astype(F32).reshape(tokens, channels)
        grad = grad_normed[:, frame].astype(F32).reshape(tokens, channels)
        outer = cotangent[frame].astype(F32).reshape(tokens, channels)
        inv = inverse_rms(hid)
        inner = jnp.mean(grad * hid, axis=-1, keepdims=True)
        total = outer + inv * grad - (inv * inv * inv * inner) * hid
        used = token_mask(frame, frames_here, rows_here, columns, total.shape)
        total = jnp.where(used, total, 0.0).astype(BF16)
        grad_hidden[frame] = total.reshape(slots, columns, channels)
        return carry

    lax.fori_loop(0, frames, step, 0)
    head[...] = grad_hidden[:, 0]
    tail[...] = grad_hidden[:, rows_here - 1]


def video_grad_kernel(frame_count, row_count, field, above, below, weight, out, extended):
    frames_here = frame_count[lax.axis_index("tm")]
    rows_here = row_count[lax.axis_index("space")]
    frames, slots, columns, channels = field.shape
    tokens = slots * columns
    fill_halo(extended, field, above, below, rows_here)

    def step(frame, carry):
        total = convolve_frame(extended, weight, frame, True)
        used = token_mask(frame, frames_here, rows_here, columns, total.shape)
        center = field[frame].reshape(tokens, channels).astype(F32)
        total = jnp.where(used, center + total, 0.0).astype(BF16)
        out[frame] = total.reshape(slots, columns, channels)
        return carry

    lax.fori_loop(0, frames, step, 0)


def share_rows(head, tail):
    ends = lax.axis_size("space") - 1
    above = lax.ppermute(tail, "space", [(i, i + 1) for i in range(ends)])
    below = lax.ppermute(head, "space", [(i + 1, i) for i in range(ends)])
    return above, below


def exchange(blocks):
    return lax.all_to_all(blocks, "tm", split_axis=0, concat_axis=0, tiled=True)


def body(video, cotangent, frame_count, row_count, w_conv, w_query, w_key, w_value, w_out):
    frames, slots, columns, channels = video.shape
    blocks = lax.axis_size("tm")
    positions = slots * columns // blocks
    all_frames = frames * blocks
    shaped = jax.ShapeDtypeStruct
    home = (frames, slots, columns, channels)
    sent = (blocks, frames, positions, channels)
    spread = (all_frames, positions, channels)
    ordered = (positions, all_frames, channels)
    edge = (frames, columns, channels)
    padded = (frames, slots + 2, columns, channels)
    size = 2 * frames * slots * columns * channels
    product = 2 * frames * slots * columns * channels * channels
    inner = 2 * positions * all_frames * all_frames * channels

    outgoing = cotangent.reshape(frames, blocks, positions, channels).transpose(1, 0, 2, 3)
    grads_in = exchange(outgoing).reshape(spread)
    head, tail = pl.pallas_call(
        edges_kernel,
        out_shape=[shaped(edge, BF16)] * 2,
        in_specs=specs(SMEM, pl.ANY),
        out_specs=specs(VMEM, VMEM),
        scratch_shapes=[pltpu.SemaphoreType.DMA((2,))],
        cost_estimate=cost(0, size // 2),
        name="edges",
    )(row_count, video)
    above, below = share_rows(head, tail)
    hidden, normed = pl.pallas_call(
        hidden_kernel,
        out_shape=[shaped(sent, BF16)] * 2,
        in_specs=specs(SMEM, SMEM, VMEM, VMEM, VMEM, VMEM),
        out_specs=specs(VMEM, VMEM),
        scratch_shapes=[VMEM(padded, BF16)],
        cost_estimate=cost(9 * product, 4 * size),
        name="hidden",
    )(frame_count, row_count, video, above, below, w_conv)
    slot = lax.broadcasted_iota(jnp.int32, (blocks, frames, all_frames), 1)
    used = (slot < frame_count[:, None, None]).astype(F32).reshape(all_frames, all_frames)
    grads = pl.pallas_call(
        grads_kernel,
        out_shape=shaped(ordered, BF16),
        in_specs=specs(VMEM, VMEM, VMEM),
        out_specs=pl.BlockSpec(memory_space=VMEM),
        scratch_shapes=[VMEM((channels // LANES, all_frames * positions, LANES), F32), VMEM(ordered, BF16)],
        cost_estimate=cost(product, 2 * size),
        name="grads",
    )(grads_in, used, w_out)
    normed_in = exchange(normed).reshape(spread)
    group = (GROUP * all_frames, channels)
    attended, grad_normed = pl.pallas_call(
        attention_kernel,
        out_shape=[shaped(ordered, BF16), shaped(spread, BF16)],
        in_specs=specs(*[VMEM] * 6),
        out_specs=specs(VMEM, VMEM),
        scratch_shapes=[VMEM((channels // LANES, all_frames * positions, LANES), F32), VMEM(ordered, BF16)]
        + [VMEM(group, BF16)] * 6,
        cost_estimate=cost(6 * product + 6 * inner, 4 * size),
        name="attention",
    )(normed_in, grads, used, w_query, w_key, w_value)
    grad_home = exchange(grad_normed.reshape(sent))
    projected = pl.pallas_call(
        project_kernel,
        out_shape=shaped(spread, BF16),
        in_specs=specs(VMEM, VMEM),
        out_specs=pl.BlockSpec(memory_space=VMEM),
        scratch_shapes=[VMEM((channels // LANES, all_frames * positions, LANES), F32)],
        cost_estimate=cost(product, 2 * size),
        name="project",
    )(attended, w_out)
    grad_hidden, head, tail = pl.pallas_call(
        grad_hidden_kernel,
        out_shape=[shaped(home, BF16), shaped(edge, BF16), shaped(edge, BF16)],
        in_specs=specs(SMEM, SMEM, VMEM, VMEM, VMEM),
        out_specs=specs(VMEM, VMEM, VMEM),
        cost_estimate=cost(0, 5 * size),
        name="grad_hidden",
    )(frame_count, row_count, cotangent, hidden, grad_home)
    projected_home = exchange(projected.reshape(sent))
    above, below = share_rows(head, tail)
    video_grad = pl.pallas_call(
        video_grad_kernel,
        out_shape=shaped(home, BF16),
        in_specs=specs(SMEM, SMEM, VMEM, VMEM, VMEM, VMEM),
        out_specs=pl.BlockSpec(memory_space=VMEM),
        scratch_shapes=[VMEM(padded, BF16)],
        cost_estimate=cost(9 * product, 3 * size),
        name="video_grad",
    )(frame_count, row_count, grad_hidden, above, below, w_conv)
    encoded = pl.pallas_call(
        encode_kernel,
        out_shape=shaped(home, BF16),
        in_specs=specs(SMEM, SMEM, VMEM, VMEM),
        out_specs=pl.BlockSpec(memory_space=VMEM),
        cost_estimate=cost(0, 3 * size),
        name="encode",
    )(frame_count, row_count, hidden, projected_home)
    return encoded, video_grad


def solution(mesh):
    field = P("tm", "space", None, None)
    in_specs = (field, field) + (P(),) * 7
    return jax.shard_map(
        body, mesh=mesh, in_specs=in_specs, out_specs=(field, field), check_vma=False
    )
```

time: 324 us -> 165 us (0.51)
  waiting for transfers between devices: 172 us -> 74.1 us
  Pallas kernels: 0 us -> 43.6 us
  local copies, waits for them, and re-layouts: 49.5 us -> 6.48 us
  matrix products: 24.2 us -> 0 us
  starting transfers between devices: 60.1 us -> 39.5 us
  other arithmetic: 11.9 us -> 0.07 us
    all_to_all x8 -> x4, waiting for transfers between devices: 172 us -> 71.3 us  [exchange(): return lax.all_to_all(blocks, 'tm', split_axis=0, concat_axis=0, tiled=True)]
    pallas_call x0 -> x8, Pallas kernels: none -> 43.6 us  [the longest x1 13.2 us: body(): pl.pallas_call(attention_kernel, out_shape=[shaped(ordered, BF16), shaped...]
    dot_general x20 -> x0, matrix products: 24.2 us -> none  [the longest x6 6.49 us: convolve(): jnp.einsum('frwbc,bcd->frwd', shift_cols(view), weight[offset], preferred...]
    all_to_all x8 -> x4, starting transfers between devices: 51.5 us -> 28.4 us  [exchange(): return lax.all_to_all(blocks, 'tm', split_axis=0, concat_axis=0, tiled=True)]
    convert_element_type x8 -> x1, local copies, waits for them, and re-layouts: 17.8 us -> 0.11 us  [body(): (slot < frame_count[:, None, None]).astype(F32)]
    all_to_all x13 -> x0, local copies, waits for them, and re-layouts: 12.1 us -> none  [the longest x2 4.03 us: body(): lax.all_to_all(queries, 'tm', split_axis=1, concat_axis=0, tiled=True)]
    convert_element_type x5 -> x1, other arithmetic: 6.94 us -> 0.07 us  [body(): (slot < frame_count[:, None, None]).astype(F32)]
    another operation x9 -> x0, local copies, waits for them, and re-layouts: 4.22 us -> none  [shift_cols(): return jnp.stack([left, field, right], axis=3)]
  transfers between devices with their start and end apart: 12 -> 8, of which waited for: 9 -> 6; matrix products, arithmetic and copies ran while one was open for 15% -> 1% of each run, Pallas kernels for 0% -> 15%
where the time goes in v1:
time: 165 us; the launch traced here: 164 us
  waiting for transfers between devices  74.1 us (45%)
  Pallas kernels  43.6 us (26%)
  starting transfers between devices  39.5 us (24%)
  local copies, waits for them, and re-layouts  6.48 us (4%)
    all_to_all x4, waiting for transfers between devices, exchange(): return lax.all_to_all(blocks, 'tm', split_axis=0, concat_axis=0, tiled=True)  71.3 us
    all_to_all x4, starting transfers between devices, exchange(): return lax.all_to_all(blocks, 'tm', split_axis=0, concat_axis=0, tiled=True)  28.4 us
    pallas_call x1, Pallas kernels, body(): pl.pallas_call(attention_kernel, out_shape=[shaped(ordered, BF16), shaped...  13.2 us
    ppermute x2, starting transfers between devices, share_rows(): below = lax.ppermute(head, 'space', [(i + 1, i) for i in range(ends)])  7.28 us
    pallas_call x1, Pallas kernels, body(): pl.pallas_call(hidden_kernel, out_shape=[shaped(sent, BF16)] * 2, in_spec...  6.85 us
    pallas_call x1, Pallas kernels, body(): pl.pallas_call(video_grad_kernel, out_shape=shaped(home, BF16), in_specs=...  6.09 us
    pallas_call x1, Pallas kernels, body(): pl.pallas_call(grads_kernel, out_shape=shaped(ordered, BF16), in_specs=sp...  4.24 us
    pallas_call x1, Pallas kernels, body(): pl.pallas_call(grad_hidden_kernel, out_shape=[shaped(home, BF16), shaped(...  4.2 us
  transfers between devices with their start and end apart: 8, of which 6 were waited for; matrix products, arithmetic and copies ran while one was open for 1% of the time, Pallas kernels for 15%

profile of v1, /device:TPU:10, one launch (start us, length us, event | category | flops | bytes accessed | tf_op | source)
XLA Modules:
  0.0 164.5 jit_solution(11542902494323610950)
XLA Ops:
  0.6 2.4 %copy.14 = bf16[4,32,16,256]{3,2,0,1:T(8,128)(2,1)} copy(bf16[4,32,16,256]{3,2,1,0:T(8,128)(2,1)} %bitcast.8) | data formatting | bytes 2097152 | tf_op jit(solution)/shard_map/reshape | solution.py:288
  3.0 11.7 %all-to-all-start.1 = ((bf16[32,4,16,256]{3,2,1,0:T(8,128)(2,1)}), bf16[32,4,16,256]{3,2,1,0:T(8,128)(2,1)S(1)}, u32[]{:S(2)}, u32[]{:S(2)}) async-start(bf16[32,4,16,256]{3,2,1,0:T(8,128)(2,1)} %bitcast.7), calls=%async_computation.1 | async-start | bytes 2097152 | tf_op jit(solution)/shard_map/all_to_all | solution.py:269
  14.7 2.4 %edges.1 = (bf16[4,64,256]{2,1,0:T(8,128)(2,1)}, bf16[4,64,256]{2,1,0:T(8,128)(2,1)}) custom-call(s32[8]{0:T(128)} %row_count.9, bf16[4,8,64,256]{3,2,1,0:T(8,128)(2,1)} %field.3), custom_call_target="tpu_custom_call" | custom-call | bytes 524288 | tf_op jit(solution)/shard_map/edges/pallas_call | solution.py:290
  17.0 1.9 %collective-permute-start = (bf16[4,64,256]{2,1,0:T(8,128)(2,1)}, bf16[4,64,256]{2,1,0:T(8,128)(2,1)S(1)}, u32[]{:S(2)}, u32[]{:S(2)}) collective-permute-start(bf16[4,64,256]{2,1,0:T(8,128)(2,1)} %get-tuple-element.11), channel_id=1, source_target_pairs={{0,1},{1,2},{2,3},{3,4},{4,5},{5,6},{6,7},{8,9},{9,10},{10,11},{11... | collective-permute-start | bytes 393224 | tf_op jit(solution)/shard_map/ppermute | solution.py:263
  19.0 3.6 %collective-permute-start.1 = (bf16[4,64,256]{2,1,0:T(8,128)(2,1)}, bf16[4,64,256]{2,1,0:T(8,128)(2,1)S(1)}, u32[]{:S(2)}, u32[]{:S(2)}) collective-permute-start(bf16[4,64,256]{2,1,0:T(8,128)(2,1)} %get-tuple-element.12), channel_id=1, source_target_pairs={{1,0},{2,1},{3,2},{4,3},{5,4},{6,5},{7,6},{9,8},{10,9},{11,10},{12... | collective-permute-start | bytes 393224 | tf_op jit(solution)/shard_map/ppermute | solution.py:264
  22.6 0.9 collective-permute-done.above
  23.5 0.0 copy-start.7
  23.5 1.9 %collective-permute-done.1.below = bf16[4,64,256]{2,1,0:T(8,128)(2,1)S(1)} collective-permute-done((bf16[4,64,256]{2,1,0:T(8,128)(2,1)}, bf16[4,64,256]{2,1,0:T(8,128)(2,1)S(1)}, u32[]{:S(2)}, u32[]{:S(2)}) %collective-permute-start.1) | collective-permute-done | bytes 131104 | tf_op jit(solution)/shard_map/ppermute | solution.py:264
  25.4 0.0 copy-done.7
  25.4 0.0 copy-start.8
  25.4 0.6 copy-done.8
  26.1 6.9 %hidden.1 = (bf16[32,4,16,256]{3,2,1,0:T(8,128)(2,1)}, bf16[32,4,16,256]{3,2,1,0:T(8,128)(2,1)}) custom-call(s32[32]{0:T(128)} %frame_count.7, s32[8]{0:T(128)} %row_count.9, bf16[4,8,64,256]{3,2,1,0:T(8,128)(2,1)} %field.3, bf16[4,64,256]{2,1,0:T(8,128)(2,1)} %copy-done.7, bf16[4,64,256]{2,1,0:T(8,128)(2,1)} %copy-done.8, bf16[3,3,256,256]{3,2,1,0:T(8,128)(2,1)} %weight.3), custom_call_target="tpu_custom_call" | custom-call | flops 2415919104 | bytes 4194304 | tf_op jit(solution)/shard_map/hidden/pallas_call | solution.py:300
  32.9 0.0 copy-start.4
  33.0 9.8 %all-to-all-done.1 = bf16[32,4,16,256]{3,2,1,0:T(8,128)(2,1)S(1)} async-done(((bf16[32,4,16,256]{3,2,1,0:T(8,128)(2,1)}), bf16[32,4,16,256]{3,2,1,0:T(8,128)(2,1)S(1)}, u32[]{:S(2)}, u32[]{:S(2)}) %all-to-all-start.1) | async-done | bytes 1048608 | tf_op jit(solution)/shard_map/all_to_all | solution.py:269
  42.8 0.0 copy-start
  42.8 5.6 %all-to-all-start = ((bf16[32,4,16,256]{3,2,1,0:T(8,128)(2,1)}), bf16[32,4,16,256]{3,2,1,0:T(8,128)(2,1)S(1)}, u32[]{:S(2)}, u32[]{:S(2)}) async-start(bf16[32,4,16,256]{3,2,1,0:T(8,128)(2,1)} %get-tuple-element.14), calls=%async_computation | async-start | bytes 2097152 | tf_op jit(solution)/shard_map/all_to_all | solution.py:269
  48.3 0.0 copy-done.4
  48.3 0.1 fusion
  48.4 0.1 reshape.31
  48.5 0.7 iota.10.used
  49.2 0.0 copy-done
  49.3 4.2 %grads.1 = bf16[16,128,256]{2,1,0:T(8,128)(2,1)} custom-call(bf16[128,16,256]{2,1,0:T(8,128)(2,1)} %bitcast.9, f32[128,128]{1,0:T(8,128)} %iota.10.used, bf16[256,256]{1,0:T(8,128)(2,1)} %w_out.3), custom_call_target="tpu_custom_call" | custom-call | flops 268435456 | bytes 2097152 | tf_op jit(solution)/shard_map/grads/pallas_call | solution.py:311
  53.5 21.8 %all-to-all-done = bf16[32,4,16,256]{3,2,1,0:T(8,128)(2,1)S(1)} async-done(((bf16[32,4,16,256]{3,2,1,0:T(8,128)(2,1)}), bf16[32,4,16,256]{3,2,1,0:T(8,128)(2,1)S(1)}, u32[]{:S(2)}, u32[]{:S(2)}) %all-to-all-start) | async-done | bytes 1048608 | tf_op jit(solution)/shard_map/all_to_all | solution.py:269
  75.3 0.0 copy-start.3
  75.3 1.0 copy-done.3
  76.3 13.2 %attention.1 = (bf16[16,128,256]{2,1,0:T(8,128)(2,1)}, bf16[128,16,256]{2,1,0:T(8,128)(2,1)}) custom-call(bf16[128,16,256]{2,1,0:T(8,128)(2,1)} %bitcast.11, bf16[16,128,256]{2,1,0:T(8,128)(2,1)} %grads.1, f32[128,128]{1,0:T(8,128)} %iota.10.used, bf16[256,256]{1,0:T(8,128)(2,1)} %w_query.1, bf16[256,256]{1,0:T(8,128)(2,1)} %w_key.1, bf16[256,256]{1,0:T(8,128)(2,1)} %w_value.1), custom_call_target="tpu_custom_call" | custom-call | flops 2415919104 | bytes 4194304 | tf_op jit(solution)/shard_map/attention/pallas_call | solution.py:322
  89.5 5.6 %all-to-all-start.3 = ((bf16[32,4,16,256]{3,2,1,0:T(8,128)(2,1)}), bf16[32,4,16,256]{3,2,1,0:T(8,128)(2,1)S(1)}, u32[]{:S(2)}, u32[]{:S(2)}) async-start(bf16[32,4,16,256]{3,2,1,0:T(8,128)(2,1)} %bitcast.12), calls=%async_computation.3 | async-start | bytes 2097152 | tf_op jit(solution)/shard_map/all_to_all | solution.py:269
  95.1 3.7 %project.1 = bf16[128,16,256]{2,1,0:T(8,128)(2,1)} custom-call(bf16[16,128,256]{2,1,0:T(8,128)(2,1)} %get-tuple-element.15.attended, bf16[256,256]{1,0:T(8,128)(2,1)} %w_out.3), custom_call_target="tpu_custom_call" | custom-call | flops 268435456 | bytes 2097152 | tf_op jit(solution)/shard_map/project/pallas_call | solution.py:333
  98.8 22.9 %all-to-all-done.3.grad_normed = bf16[32,4,16,256]{3,2,1,0:T(8,128)(2,1)S(1)} async-done(((bf16[32,4,16,256]{3,2,1,0:T(8,128)(2,1)}), bf16[32,4,16,256]{3,2,1,0:T(8,128)(2,1)S(1)}, u32[]{:S(2)}, u32[]{:S(2)}) %all-to-all-start.3) | async-done | bytes 1048608 | tf_op jit(solution)/shard_map/all_to_all | solution.py:269
  121.7 0.0 copy-start.2
  121.7 5.6 %all-to-all-start.2 = ((bf16[32,4,16,256]{3,2,1,0:T(8,128)(2,1)}), bf16[32,4,16,256]{3,2,1,0:T(8,128)(2,1)S(1)}, u32[]{:S(2)}, u32[]{:S(2)}) async-start(bf16[32,4,16,256]{3,2,1,0:T(8,128)(2,1)} %bitcast.10), calls=%async_computation.2 | async-start | bytes 2097152 | tf_op jit(solution)/shard_map/all_to_all | solution.py:269
  127.3 0.0 copy-done.2
  127.3 4.2 %grad_hidden.1 = (bf16[4,8,64,256]{3,2,1,0:T(8,128)(2,1)}, bf16[4,64,256]{2,1,0:T(8,128)(2,1)}, bf16[4,64,256]{2,1,0:T(8,128)(2,1)}) custom-call(s32[32]{0:T(128)} %frame_count.7, s32[8]{0:T(128)} %row_count.9, bf16[4,8,64,256]{3,2,1,0:T(8,128)(2,1)} %cotangent.1, bf16[32,4,16,256]{3,2,1,0:T(8,128)(2,1)} %get-tuple-element.13.hidden, ...), custom_call_target="tpu_custom_call" | custom-call | bytes 5242880 | tf_op jit(solution)/shard_map/grad_hidden/pallas_call | solution.py:342
  131.5 1.9 %collective-permute-start.2 = (bf16[4,64,256]{2,1,0:T(8,128)(2,1)}, bf16[4,64,256]{2,1,0:T(8,128)(2,1)S(1)}, u32[]{:S(2)}, u32[]{:S(2)}) collective-permute-start(bf16[4,64,256]{2,1,0:T(8,128)(2,1)} %get-tuple-element.18), channel_id=1, source_target_pairs={{0,1},{1,2},{2,3},{3,4},{4,5},{5,6},{6,7},{8,9},{9,10},{10,11},{11... | collective-permute-start | bytes 393224 | tf_op jit(solution)/shard_map/ppermute | solution.py:263
  133.4 3.6 %collective-permute-start.3 = (bf16[4,64,256]{2,1,0:T(8,128)(2,1)}, bf16[4,64,256]{2,1,0:T(8,128)(2,1)S(1)}, u32[]{:S(2)}, u32[]{:S(2)}) collective-permute-start(bf16[4,64,256]{2,1,0:T(8,128)(2,1)} %get-tuple-element.19), channel_id=1, source_target_pairs={{1,0},{2,1},{3,2},{4,3},{5,4},{6,5},{7,6},{9,8},{10,9},{11,10},{12... | collective-permute-start | bytes 393224 | tf_op jit(solution)/shard_map/ppermute | solution.py:264
  137.0 16.7 %all-to-all-done.2.projected = bf16[32,4,16,256]{3,2,1,0:T(8,128)(2,1)S(1)} async-done(((bf16[32,4,16,256]{3,2,1,0:T(8,128)(2,1)}), bf16[32,4,16,256]{3,2,1,0:T(8,128)(2,1)S(1)}, u32[]{:S(2)}, u32[]{:S(2)}) %all-to-all-start.2) | async-done | bytes 1048608 | tf_op jit(solution)/shard_map/all_to_all | solution.py:269
  153.8 0.0 copy-start.1
  153.8 1.0 copy-done.1
  154.7 3.0 %encode.1 = bf16[4,8,64,256]{3,2,1,0:T(8,128)(2,1)} custom-call(s32[32]{0:T(128)} %frame_count.7, s32[8]{0:T(128)} %row_count.9, bf16[32,4,16,256]{3,2,1,0:T(8,128)(2,1)} %get-tuple-element.13.hidden, bf16[32,4,16,256]{3,2,1,0:T(8,128)(2,1)} %copy-done.1), custom_call_target="tpu_custom_call" | custom-call | bytes 3145728 | tf_op jit(solution)/shard_map/encode/pallas_call | solution.py:361
  157.7 0.0 collective-permute-done.2.above
  157.7 0.0 copy-start.5
  157.7 0.0 collective-permute-done.3.below
  157.7 0.0 copy-start.6
  157.7 0.6 copy-done.5
  158.4 0.0 copy-done.6
  158.4 6.1 %video_grad.1 = bf16[4,8,64,256]{3,2,1,0:T(8,128)(2,1)} custom-call(s32[32]{0:T(128)} %frame_count.7, s32[8]{0:T(128)} %row_count.9, bf16[4,8,64,256]{3,2,1,0:T(8,128)(2,1)} %get-tuple-element.17.field, bf16[4,64,256]{2,1,0:T(8,128)(2,1)} %copy-done.5, bf16[4,64,256]{2,1,0:T(8,128)(2,1)} %copy-done.6, bf16[3,3,256,256]{3,2,1,0:T(8,128)(2,1)} %weight.3), custom_call_target="tpu_custom_call" | custom-call | flops 2415919104 | bytes 3145728 | tf_op jit(solution)/shard_map/video_grad/pallas_call | solution.py:352
Async XLA Ops:
  3.0 39.8 %all-to-all-start.1 = ((bf16[32,4,16,256]{3,2,1,0:T(8,128)(2,1)}), bf16[32,4,16,256]{3,2,1,0:T(8,128)(2,1)S(1)}, u32[]{:S(2)}, u32[]{:S(2)}) async-start(bf16[32,4,16,256]{3,2,1,0:T(8,128)(2,1)} %bitcast.7), calls=%async_computation.1 | async-start | bytes 2097152 | tf_op jit(solution)/shard_map/all_to_all | solution.py:269
  17.0 6.5 %collective-permute-start = (bf16[4,64,256]{2,1,0:T(8,128)(2,1)}, bf16[4,64,256]{2,1,0:T(8,128)(2,1)S(1)}, u32[]{:S(2)}, u32[]{:S(2)}) collective-permute-start(bf16[4,64,256]{2,1,0:T(8,128)(2,1)} %get-tuple-element.11), channel_id=1, source_target_pairs={{0,1},{1,2},{2,3},{3,4},{4,5},{5,6},{6,7},{8,9},{9,10},{10,11},{11... | collective-permute-start | bytes 393224 | tf_op jit(solution)/shard_map/ppermute | solution.py:263
  19.0 6.5 %collective-permute-start.1 = (bf16[4,64,256]{2,1,0:T(8,128)(2,1)}, bf16[4,64,256]{2,1,0:T(8,128)(2,1)S(1)}, u32[]{:S(2)}, u32[]{:S(2)}) collective-permute-start(bf16[4,64,256]{2,1,0:T(8,128)(2,1)} %get-tuple-element.12), channel_id=1, source_target_pairs={{1,0},{2,1},{3,2},{4,3},{5,4},{6,5},{7,6},{9,8},{10,9},{11,10},{12... | collective-permute-start | bytes 393224 | tf_op jit(solution)/shard_map/ppermute | solution.py:264
  23.5 1.9 %copy-start.7 = (bf16[4,64,256]{2,1,0:T(8,128)(2,1)}, bf16[4,64,256]{2,1,0:T(8,128)(2,1)S(1)}, u32[]{:S(2)}) copy-start(bf16[4,64,256]{2,1,0:T(8,128)(2,1)S(1)} %collective-permute-done.above) | copy-start | bytes 393220
  25.4 0.6 copy-start.8
  32.9 15.4 %copy-start.4 = (s32[32]{0:T(128)S(1)}, s32[32]{0:T(128)}, u32[]{:S(2)}) copy-start(s32[32]{0:T(128)} %frame_count.7) | copy-start | bytes 388
  42.8 6.5 %copy-start = (bf16[32,4,16,256]{3,2,1,0:T(8,128)(2,1)}, bf16[32,4,16,256]{3,2,1,0:T(8,128)(2,1)S(1)}, u32[]{:S(2)}) copy-start(bf16[32,4,16,256]{3,2,1,0:T(8,128)(2,1)S(1)} %all-to-all-done.1) | copy-start | bytes 3145732
  42.8 32.6 %all-to-all-start = ((bf16[32,4,16,256]{3,2,1,0:T(8,128)(2,1)}), bf16[32,4,16,256]{3,2,1,0:T(8,128)(2,1)S(1)}, u32[]{:S(2)}, u32[]{:S(2)}) async-start(bf16[32,4,16,256]{3,2,1,0:T(8,128)(2,1)} %get-tuple-element.14), calls=%async_computation | async-start | bytes 2097152 | tf_op jit(solution)/shard_map/all_to_all | solution.py:269
  75.3 1.0 copy-start.3
  89.5 32.2 %all-to-all-start.3 = ((bf16[32,4,16,256]{3,2,1,0:T(8,128)(2,1)}), bf16[32,4,16,256]{3,2,1,0:T(8,128)(2,1)S(1)}, u32[]{:S(2)}, u32[]{:S(2)}) async-start(bf16[32,4,16,256]{3,2,1,0:T(8,128)(2,1)} %bitcast.12), calls=%async_computation.3 | async-start | bytes 2097152 | tf_op jit(solution)/shard_map/all_to_all | solution.py:269
  121.7 5.6 %copy-start.2 = (bf16[32,4,16,256]{3,2,1,0:T(8,128)(2,1)}, bf16[32,4,16,256]{3,2,1,0:T(8,128)(2,1)S(1)}, u32[]{:S(2)}) copy-start(bf16[32,4,16,256]{3,2,1,0:T(8,128)(2,1)S(1)} %all-to-all-done.3.grad_normed) | copy-start | bytes 3145732
  121.7 32.1 %all-to-all-start.2 = ((bf16[32,4,16,256]{3,2,1,0:T(8,128)(2,1)}), bf16[32,4,16,256]{3,2,1,0:T(8,128)(2,1)S(1)}, u32[]{:S(2)}, u32[]{:S(2)}) async-start(bf16[32,4,16,256]{3,2,1,0:T(8,128)(2,1)} %bitcast.10), calls=%async_computation.2 | async-start | bytes 2097152 | tf_op jit(solution)/shard_map/all_to_all | solution.py:269
  131.5 26.2 %collective-permute-start.2 = (bf16[4,64,256]{2,1,0:T(8,128)(2,1)}, bf16[4,64,256]{2,1,0:T(8,128)(2,1)S(1)}, u32[]{:S(2)}, u32[]{:S(2)}) collective-permute-start(bf16[4,64,256]{2,1,0:T(8,128)(2,1)} %get-tuple-element.18), channel_id=1, source_target_pairs={{0,1},{1,2},{2,3},{3,4},{4,5},{5,6},{6,7},{8,9},{9,10},{10,11},{11... | collective-permute-start | bytes 393224 | tf_op jit(solution)/shard_map/ppermute | solution.py:263
  133.4 24.3 %collective-permute-start.3 = (bf16[4,64,256]{2,1,0:T(8,128)(2,1)}, bf16[4,64,256]{2,1,0:T(8,128)(2,1)S(1)}, u32[]{:S(2)}, u32[]{:S(2)}) collective-permute-start(bf16[4,64,256]{2,1,0:T(8,128)(2,1)} %get-tuple-element.19), channel_id=1, source_target_pairs={{1,0},{2,1},{3,2},{4,3},{5,4},{6,5},{7,6},{9,8},{10,9},{11,10},{12... | collective-permute-start | bytes 393224 | tf_op jit(solution)/shard_map/ppermute | solution.py:264
  153.8 1.0 copy-start.1
  157.7 0.7 copy-start.5
  157.7 0.7 copy-start.6

commit v2 on v1

v2 whole, which is shorter than its diff:
```python
import jax
import jax.numpy as jnp
from jax import lax
from jax.experimental import pallas as pl
from jax.experimental.pallas import tpu as pltpu
from jax.sharding import PartitionSpec as P


BF16 = jnp.bfloat16
F32 = jnp.float32
GROUP = 4
LANES = 128
VMEM = pltpu.VMEM
SMEM = pltpu.SMEM
HBM = pltpu.HBM
ON_CHIP = object()


def dot(a, b, contract=(1, 0)):
    return lax.dot_general(
        a, b, (((contract[0],), (contract[1],)), ((), ())), preferred_element_type=F32
    )


def specs(*spaces):
    return [pl.BlockSpec(memory_space=space) for space in spaces]


def cost(flops, moved):
    return pl.CostEstimate(flops=flops, bytes_accessed=moved, transcendentals=0)


def edges_kernel(row_count, field, head, tail, sems):
    rows_here = row_count[lax.axis_index("space")]
    first = pltpu.make_async_copy(field.at[:, 0], head, sems.at[0])
    last = pltpu.make_async_copy(field.at[:, rows_here - 1], tail, sems.at[1])
    first.start()
    last.start()
    first.wait()
    last.wait()


def fill_halo(extended, field, above, below, rows_here):
    slots = field.shape[1]
    extended[:, 1 : 1 + slots] = field[...]
    extended[:, 0] = above[...]
    extended[:, 1 + rows_here] = below[...]


def convolve_frame(extended, weight, frame, flipped):
    _, padded, columns, channels = extended.shape
    tokens = (padded - 2) * columns
    column = lax.broadcasted_iota(jnp.int32, (tokens, channels), 0) % columns
    total = None
    for b in range(3):
        part = None
        for a in range(3):
            view = extended[frame, a : a + padded - 2].reshape(tokens, channels)
            if flipped:
                term = dot(view, weight[2 - a, 2 - b], (1, 1))
            else:
                term = dot(view, weight[a, b])
            part = term if part is None else part + term
        if b == 0:
            part = jnp.where(column == 0, 0.0, pltpu.roll(part, 1, 0))
        elif b == 2:
            part = jnp.where(column == columns - 1, 0.0, pltpu.roll(part, tokens - 1, 0))
        total = part if total is None else total + part
    return total


def token_mask(frame, frames_here, rows_here, columns, shape):
    row = lax.broadcasted_iota(jnp.int32, shape, 0) // columns
    return (row < rows_here) & (frame < frames_here)


def inverse_rms(hidden):
    return lax.rsqrt(jnp.mean(hidden * hidden, axis=-1, keepdims=True) + 1e-06)


def hidden_kernel(
    frame_count, row_count, field, above, below, weight, hidden_out, normed_out, extended
):
    frames_here = frame_count[lax.axis_index("tm")]
    rows_here = row_count[lax.axis_index("space")]
    frames, slots, columns, channels = field.shape
    tokens = slots * columns
    fill_halo(extended, field, above, below, rows_here)

    def step(frame, carry):
        total = convolve_frame(extended, weight, frame, False)
        used = token_mask(frame, frames_here, rows_here, columns, total.shape)
        center = field[frame].reshape(tokens, channels).astype(F32)
        hidden = jnp.where(used, center + total, 0.0).astype(BF16)
        hidden_out[:, frame] = hidden.reshape(hidden_out.shape[0], -1, channels)
        hidden_f = hidden.astype(F32)
        normed = (hidden_f * inverse_rms(hidden_f)).astype(BF16)
        normed_out[:, frame] = normed.reshape(normed_out.shape[0], -1, channels)
        return carry

    lax.fori_loop(0, frames, step, 0)


def load_position(spread, position, positions, scale=None):
    parts = []
    for h in range(spread.shape[0]):
        rows = spread[h, pl.ds(position, spread.shape[1] // positions, stride=positions), :]
        parts.append((rows if scale is None else rows * scale).astype(BF16))
    return jnp.concatenate(parts, axis=1)


def store_position(spread, position, positions, rows):
    for h in range(spread.shape[0]):
        part = rows[:, h * LANES : (h + 1) * LANES]
        spread[h, pl.ds(position, rows.shape[0], stride=positions), :] = part


def widen(source, spread):
    for h in range(spread.shape[0]):
        part = source[:, :, h * LANES : (h + 1) * LANES].astype(F32)
        spread[h] = part.reshape(spread.shape[1], LANES)


def narrow(spread, held, target, sems):
    frames, positions, _ = held.shape
    pieces = 4
    size = frames // pieces
    copies = []
    for i in range(pieces):
        here = slice(i * size, (i + 1) * size)
        for h in range(spread.shape[0]):
            part = spread[h, i * size * positions : (i + 1) * size * positions]
            part = part.reshape(size, positions, LANES)
            held[here, :, h * LANES : (h + 1) * LANES] = part.astype(BF16)
        copy = pltpu.make_async_copy(held.at[here], target.at[here], sems.at[i])
        copy.start()
        copies.append(copy)
    for copy in copies:
        copy.wait()


def send_kernel(field, out, held, sems):
    frames = field.shape[0]
    arrive = [
        pltpu.make_async_copy(field.at[f], held.at[f], sems.at[0, f]) for f in range(frames)
    ]
    leave = [
        pltpu.make_async_copy(held.at[f], out.at[:, f], sems.at[1, f]) for f in range(frames)
    ]
    for copy in arrive:
        copy.start()
    for f in range(frames):
        arrive[f].wait()
        leave[f].start()
    for copy in leave:
        copy.wait()


def grads_kernel(cotangent, used, w_out, grad_out, spread, ordered):
    all_frames, positions, channels = cotangent.shape
    widen(cotangent, spread)
    for first in range(0, positions, GROUP):
        for p in range(first, first + GROUP):
            here = slice(p * all_frames, (p + 1) * all_frames)
            ordered[here] = load_position(spread, p, positions, used[...])
        here = slice(first * all_frames, (first + GROUP) * all_frames)
        grads = dot(ordered[here], w_out[...], (1, 1)).astype(BF16)
        grad_out[first : first + GROUP] = grads.reshape(GROUP, all_frames, channels)


def softmax_probs(query, key, allowed, scale):
    scores = jnp.where(allowed, dot(key, query, (1, 1)) * scale, -1e30)
    expo = jnp.exp(scores - jnp.max(scores, axis=0, keepdims=True))
    return expo * (1.0 / jnp.sum(expo, axis=0, keepdims=True))


def allowed_pairs(used):
    tile = (used.shape[0], used.shape[0])
    source = lax.broadcasted_iota(jnp.int32, tile, 0)
    reader = lax.broadcasted_iota(jnp.int32, tile, 1)
    return (source <= reader) & (used[...] > 0.0)


def attention_kernel(
    normed, grads_in, used, w_query, w_key, w_value, grad_normed, kept,
    grads, weights, spread, result, out, ordered, query_s, key_s, value_s, dq_s, dk_s, dv_s, sems,
):
    loads = [
        pltpu.make_async_copy(w, weights.at[i], sems.at[i])
        for i, w in enumerate((w_query, w_key, w_value))
    ]
    loads.append(pltpu.make_async_copy(grads_in, grads, sems.at[3]))
    for copy in loads:
        copy.start()
    all_frames, positions, channels = normed.shape
    widen(normed, spread)
    allowed = allowed_pairs(used)
    scale = channels ** (-0.5)
    for copy in loads[:3]:
        copy.wait()
    keeps = []

    for first in range(0, positions, GROUP):
        group = slice(first * all_frames, (first + GROUP) * all_frames)
        for p in range(first, first + GROUP):
            ordered[p * all_frames : (p + 1) * all_frames] = load_position(spread, p, positions)
        rows = ordered[group]
        keep = pltpu.make_async_copy(
            ordered.at[group], kept.at[group], sems.at[4 + first // GROUP]
        )
        keep.start()
        keeps.append(keep)
        query_s[group] = dot(rows, weights[0]).astype(BF16)
        key_s[group] = dot(rows, weights[1]).astype(BF16)
        value_s[group] = dot(rows, weights[2]).astype(BF16)
        if first == 0:
            loads[3].wait()
        for p in range(first, first + GROUP):
            here = slice(p * all_frames, (p + 1) * all_frames)
            query, key, value, grad = query_s[here], key_s[here], value_s[here], grads[p]
            probs = softmax_probs(query, key, allowed, scale)
            low = probs.astype(BF16)
            grad_probs = dot(value, grad, (1, 1))
            delta = jnp.sum(low.astype(F32) * grad_probs, axis=0, keepdims=True)
            grad_scores = (probs * (grad_probs - delta) * scale).astype(BF16)
            dv_s[here] = dot(low, grad).astype(BF16)
            dk_s[here] = dot(grad_scores, query).astype(BF16)
            dq_s[here] = dot(grad_scores, key, (0, 0)).astype(BF16)
        total = dot(dq_s[group], weights[0], (1, 1))
        total = total + dot(dk_s[group], weights[1], (1, 1))
        total = total + dot(dv_s[group], weights[2], (1, 1))
        total = total.astype(BF16).astype(F32)
        for j in range(GROUP):
            part = total[j * all_frames : (j + 1) * all_frames]
            store_position(result, first + j, positions, part)
    narrow(result, out, grad_normed, sems)
    for copy in keeps:
        copy.wait()


def project_kernel(
    ordered, used, w_query, w_key, w_value, w_out, projected,
    spread, query_s, key_s, value_s, attended,
):
    all_frames, positions, channels = projected.shape
    allowed = allowed_pairs(used)
    scale = channels ** (-0.5)

    def step(i, carry):
        first = pl.multiple_of(i * GROUP * all_frames, GROUP * all_frames)
        rows = ordered[pl.ds(first, GROUP * all_frames)]
        query_s[...] = dot(rows, w_query[...]).astype(BF16)
        key_s[...] = dot(rows, w_key[...]).astype(BF16)
        value_s[...] = dot(rows, w_value[...]).astype(BF16)
        for j in range(GROUP):
            here = slice(j * all_frames, (j + 1) * all_frames)
            low = softmax_probs(query_s[here], key_s[here], allowed, scale).astype(BF16)
            attended[here] = dot(low, value_s[here], (0, 0)).astype(BF16)
        total = dot(attended[...], w_out[...]).astype(BF16).astype(F32)
        for j in range(GROUP):
            part = total[j * all_frames : (j + 1) * all_frames]
            store_position(spread, i * GROUP + j, positions, part)
        return carry

    lax.fori_loop(0, positions // GROUP, step, 0)
    for h in range(spread.shape[0]):
        part = spread[h].reshape(all_frames, positions, LANES)
        projected[:, :, h * LANES : (h + 1) * LANES] = part.astype(BF16)


def encode_kernel(frame_count, row_count, hidden, projected, encoded, held, sems):
    frames_here = frame_count[lax.axis_index("tm")]
    rows_here = row_count[lax.axis_index("space")]
    frames, slots, columns, channels = encoded.shape
    tokens = slots * columns
    copies = []
    for frame in range(frames):
        total = hidden[:, frame].astype(F32) + projected[:, frame].astype(F32)
        total = total.reshape(tokens, channels)
        used = token_mask(frame, frames_here, rows_here, columns, total.shape)
        total = jnp.where(used, total, 0.0).astype(BF16)
        held[frame] = total.reshape(slots, columns, channels)
        copy = pltpu.make_async_copy(held.at[frame], encoded.at[frame], sems.at[frame])
        copy.start()
        copies.append(copy)
    for copy in copies:
        copy.wait()


def grad_hidden_kernel(
    frame_count, row_count, cotangent, hidden, grad_normed, grad_hidden, head, tail
):
    frames_here = frame_count[lax.axis_index("tm")]
    rows_here = row_count[lax.axis_index("space")]
    frames, slots, columns, channels = cotangent.shape
    tokens = slots * columns

    def step(frame, carry):
        hid = hidden[:, frame].astype(F32).reshape(tokens, channels)
        grad = grad_normed[:, frame].astype(F32).reshape(tokens, channels)
        outer = cotangent[frame].astype(F32).reshape(tokens, channels)
        inv = inverse_rms(hid)
        inner = jnp.mean(grad * hid, axis=-1, keepdims=True)
        total = outer + inv * grad - (inv * inv * inv * inner) * hid
        used = token_mask(frame, frames_here, rows_here, columns, total.shape)
        total = jnp.where(used, total, 0.0).astype(BF16)
        grad_hidden[frame] = total.reshape(slots, columns, channels)
        return carry

    lax.fori_loop(0, frames, step, 0)
    head[...] = grad_hidden[:, 0]
    tail[...] = grad_hidden[:, rows_here - 1]


def video_grad_kernel(frame_count, row_count, field, above, below, weight, out, extended):
    frames_here = frame_count[lax.axis_index("tm")]
    rows_here = row_count[lax.axis_index("space")]
    frames, slots, columns, channels = field.shape
    tokens = slots * columns
    fill_halo(extended, field, above, below, rows_here)

    def step(frame, carry):
        total = convolve_frame(extended, weight, frame, True)
        used = token_mask(frame, frames_here, rows_here, columns, total.shape)
        center = field[frame].reshape(tokens, channels).astype(F32)
        total = jnp.where(used, center + total, 0.0).astype(BF16)
        out[frame] = total.reshape(slots, columns, channels)
        return carry

    lax.fori_loop(0, frames, step, 0)


def share_rows(head, tail):
    ends = lax.axis_size("space") - 1
    above = lax.ppermute(tail, "space", [(i, i + 1) for i in range(ends)])
    below = lax.ppermute(head, "space", [(i + 1, i) for i in range(ends)])
    return above, below


def exchange(blocks):
    return lax.all_to_all(blocks, "tm", split_axis=0, concat_axis=0, tiled=True)


def body(video, cotangent, frame_count, row_count, w_conv, w_query, w_key, w_value, w_out):
    frames, slots, columns, channels = video.shape
    blocks = lax.axis_size("tm")
    positions = slots * columns // blocks
    all_frames = frames * blocks
    shaped = jax.ShapeDtypeStruct
    home = (frames, slots, columns, channels)
    sent = (blocks, frames, positions, channels)
    spread = (all_frames, positions, channels)
    ordered = (positions, all_frames, channels)
    edge = (frames, columns, channels)
    padded = (frames, slots + 2, columns, channels)
    size = 2 * frames * slots * columns * channels
    product = 2 * frames * slots * columns * channels * channels
    inner = 2 * positions * all_frames * all_frames * channels

    def call(kernel, outs, ins, args, scratch, flops, moved, out_spaces=None):
        args = [
            pltpu.with_memory_space_constraint(x, VMEM) if space is ON_CHIP else x
            for x, space in zip(args, ins)
        ]
        ins = [VMEM if space is ON_CHIP else space for space in ins]
        return pl.pallas_call(
            kernel,
            out_shape=outs,
            in_specs=specs(*ins),
            out_specs=specs(*(out_spaces or [VMEM] * len(outs))),
            scratch_shapes=scratch,
            cost_estimate=cost(flops, moved),
        )(*args)

    dma = pltpu.SemaphoreType.DMA
    wide = VMEM((channels // LANES, all_frames * positions, LANES), F32)
    flat = VMEM((all_frames * positions, channels), BF16)
    part = VMEM((GROUP * all_frames, channels), BF16)
    chunked = (frames, blocks, positions, channels)

    (outgoing,) = call(
        send_kernel, [shaped(sent, BF16)], [HBM], [cotangent.reshape(chunked)],
        [VMEM(chunked, BF16), dma((2, frames))], 0, size, [HBM],
    )
    grads_in = exchange(outgoing).reshape(spread)
    head, tail = call(
        edges_kernel, [VMEM(edge, BF16)] * 2, [SMEM, HBM], [row_count, video],
        [dma((2,))], 0, size // 4,
    )
    above, below = share_rows(head, tail)
    hidden, normed = call(
        hidden_kernel, [shaped(sent, BF16)] * 2, [SMEM, SMEM, VMEM, ON_CHIP, ON_CHIP, VMEM],
        [frame_count, row_count, video, above, below, w_conv], [VMEM(padded, BF16)],
        9 * product, 4 * size,
    )
    normed_in = exchange(normed).reshape(spread)
    slot = lax.broadcasted_iota(jnp.int32, (blocks, frames, LANES), 1)
    used = (slot < frame_count[:, None, None]).astype(F32).reshape(all_frames, LANES)
    (grads,) = call(
        grads_kernel, [shaped(ordered, BF16)], [ON_CHIP, ON_CHIP, VMEM], [grads_in, used, w_out],
        [wide, flat], product, 2 * size,
    )
    grad_normed, kept = call(
        attention_kernel,
        [shaped(spread, BF16), shaped((all_frames * positions, channels), BF16)],
        [ON_CHIP, HBM, ON_CHIP, HBM, HBM, HBM],
        [normed_in, grads, used, w_query, w_key, w_value],
        [VMEM(ordered, BF16), VMEM((3, channels, channels), BF16), wide, wide, VMEM(spread, BF16)]
        + [flat] * 7 + [dma((4 + positions // GROUP,))],
        6 * product + 5 * inner, 4 * size, [HBM, HBM],
    )
    grad_home = exchange(grad_normed.reshape(sent))
    (projected,) = call(
        project_kernel, [shaped(spread, BF16)], [VMEM, ON_CHIP] + [VMEM] * 4,
        [kept, used, w_query, w_key, w_value, w_out],
        [wide] + [part] * 4, 4 * product + 2 * inner, 2 * size,
    )
    projected_home = exchange(projected.reshape(sent))
    grad_hidden, head, tail = call(
        grad_hidden_kernel, [shaped(home, BF16), shaped(edge, BF16), shaped(edge, BF16)],
        [SMEM, SMEM, VMEM, VMEM, ON_CHIP],
        [frame_count, row_count, cotangent, hidden, grad_home], [], 0, 5 * size,
    )
    above, below = share_rows(head, tail)
    (video_grad,) = call(
        video_grad_kernel, [shaped(home, BF16)], [SMEM, SMEM, VMEM, ON_CHIP, ON_CHIP, VMEM],
        [frame_count, row_count, grad_hidden, above, below, w_conv], [VMEM(padded, BF16)],
        9 * product, 3 * size,
    )
    (encoded,) = call(
        encode_kernel, [shaped(home, BF16)], [SMEM, SMEM, ON_CHIP, ON_CHIP],
        [frame_count, row_count, hidden, projected_home],
        [VMEM(home, BF16), dma((frames,))], 0, 3 * size, [HBM],
    )
    return encoded, video_grad


def solution(mesh):
    field = P("tm", "space", None, None)
    in_specs = (field, field) + (P(),) * 7

    return jax.shard_map(
        body, mesh=mesh, in_specs=in_specs, out_specs=(field, field), check_vma=False
    )
```

time: 165 us -> 159 us (0.964)
  local copies, waits for them, and re-layouts: 6.48 us -> 1.16 us
    reshape x1 -> x0, local copies, waits for them, and re-layouts: 2.36 us -> none  [body(): cotangent.reshape(frames, blocks, positions, channels).transpose(1, 0, 2, 3)]
    unnamed x18 -> x8, local copies, waits for them, and re-layouts: 3.29 us -> 0.98 us
    pallas_call x8 -> x9, Pallas kernels: 43.6 us -> 42.6 us  [call(): pl.pallas_call(kernel, out_shape=outs, in_specs=specs(*ins), out_specs=sp...]
  transfers between devices with their start and end apart: 8 -> 8, of which waited for: 6 -> 6; matrix products, arithmetic and copies ran while one was open for 1% -> 0% of each run, Pallas kernels for 15% -> 16%
where the time goes in v2:
time: 159 us; the launch traced here: 158 us
  waiting for transfers between devices  74 us (47%)
  Pallas kernels  42.6 us (27%)
  starting transfers between devices  39.7 us (25%)
    all_to_all x4, waiting for transfers between devices, exchange(): return lax.all_to_all(blocks, 'tm', split_axis=0, concat_axis=0, tiled=True)  71.5 us
    pallas_call x9, Pallas kernels, call(): pl.pallas_call(kernel, out_shape=outs, in_specs=specs(*ins), out_specs=sp...  42.6 us
    all_to_all x4, starting transfers between devices, exchange(): return lax.all_to_all(blocks, 'tm', split_axis=0, concat_axis=0, tiled=True)  28.5 us
    ppermute x2, starting transfers between devices, share_rows(): below = lax.ppermute(head, 'space', [(i + 1, i) for i in range(ends)])  7.28 us
    ppermute x2, starting transfers between devices, share_rows(): above = lax.ppermute(tail, 'space', [(i, i + 1) for i in range(ends)])  3.83 us
  transfers between devices with their start and end apart: 8, of which 6 were waited for; matrix products, arithmetic and copies ran while one was open for 0% of the time, Pallas kernels for 16%

profile of v2, /device:TPU:10, one launch (start us, length us, event | category | flops | bytes accessed | tf_op | source)
XLA Modules:
  0.0 158.2 jit_solution(9485132659716226158)
XLA Ops:
  0.6 2.0 %shard_map.106 = bf16[32,4,16,256]{3,2,1,0:T(8,128)(2,1)} custom-call(bf16[4,32,16,256]{3,2,1,0:T(8,128)(2,1)} %bitcast.7), custom_call_target="tpu_custom_call" | custom-call | bytes 1048576 | tf_op jit(solution)/shard_map/pallas_call | solution.py:366
  2.7 11.7 %all-to-all-start.1 = ((bf16[32,4,16,256]{3,2,1,0:T(8,128)(2,1)}), bf16[32,4,16,256]{3,2,1,0:T(8,128)(2,1)S(1)}, u32[]{:S(2)}, u32[]{:S(2)}) async-start(bf16[32,4,16,256]{3,2,1,0:T(8,128)(2,1)} %shard_map.106), calls=%async_computation.1 | async-start | bytes 2097152 | tf_op jit(solution)/shard_map/all_to_all | solution.py:341
  14.4 1.7 %shard_map.104 = (bf16[4,64,256]{2,1,0:T(8,128)(2,1)S(1)}, bf16[4,64,256]{2,1,0:T(8,128)(2,1)S(1)}) custom-call(s32[8]{0:T(128)} %row_count.9, bf16[4,8,64,256]{3,2,1,0:T(8,128)(2,1)} %field.3), custom_call_target="tpu_custom_call" | custom-call | bytes 262144 | tf_op jit(solution)/shard_map/pallas_call | solution.py:366
  16.0 1.9 %collective-permute-start = (bf16[4,64,256]{2,1,0:T(8,128)(2,1)S(1)}, bf16[4,64,256]{2,1,0:T(8,128)(2,1)S(1)}, u32[]{:S(2)}, u32[]{:S(2)}) collective-permute-start(bf16[4,64,256]{2,1,0:T(8,128)(2,1)S(1)} %get-tuple-element.11), channel_id=1, source_target_pairs={{0,1},{1,2},{2,3},{3,4},{4,5},{5,6},{6,7},{8,9},{9,10},{10,11},{11... | collective-permute-start | bytes 393224 | tf_op jit(solution)/shard_map/ppermute | solution.py:335
  18.0 3.6 %collective-permute-start.1 = (bf16[4,64,256]{2,1,0:T(8,128)(2,1)S(1)}, bf16[4,64,256]{2,1,0:T(8,128)(2,1)S(1)}, u32[]{:S(2)}, u32[]{:S(2)}) collective-permute-start(bf16[4,64,256]{2,1,0:T(8,128)(2,1)S(1)} %get-tuple-element.12), channel_id=1, source_target_pairs={{1,0},{2,1},{3,2},{4,3},{5,4},{6,5},{7,6},{9,8},{10,9},{11,10},{12... | collective-permute-start | bytes 393224 | tf_op jit(solution)/shard_map/ppermute | solution.py:336
  21.6 0.7 collective-permute-done.above
  22.3 1.8 %collective-permute-done.1.below = bf16[4,64,256]{2,1,0:T(8,128)(2,1)S(1)} collective-permute-done((bf16[4,64,256]{2,1,0:T(8,128)(2,1)S(1)}, bf16[4,64,256]{2,1,0:T(8,128)(2,1)S(1)}, u32[]{:S(2)}, u32[]{:S(2)}) %collective-permute-start.1) | collective-permute-done | bytes 131104 | tf_op jit(solution)/shard_map/ppermute | solution.py:336
  24.1 6.7 %shard_map.105 = (bf16[32,4,16,256]{3,2,1,0:T(8,128)(2,1)}, bf16[32,4,16,256]{3,2,1,0:T(8,128)(2,1)}) custom-call(s32[32]{0:T(128)} %frame_count.7, s32[8]{0:T(128)} %row_count.9, bf16[4,8,64,256]{3,2,1,0:T(8,128)(2,1)} %field.3, bf16[4,64,256]{2,1,0:T(8,128)(2,1)S(1)} %collective-permute-done.above, bf16[4,64,256]{2,1,0:T(8,128)(2,1)S(1)} %collective-permute-done.1.below, ...), custom_call_target="tpu_custom_call" | custom-call | flops 2415919104 | bytes 4194304 | tf_op jit(solution)/shard_map/pallas_call | solution.py:366
  30.8 0.0 copy-start.3
  30.9 11.6 %all-to-all-done.1 = bf16[32,4,16,256]{3,2,1,0:T(8,128)(2,1)S(1)} async-done(((bf16[32,4,16,256]{3,2,1,0:T(8,128)(2,1)}), bf16[32,4,16,256]{3,2,1,0:T(8,128)(2,1)S(1)}, u32[]{:S(2)}, u32[]{:S(2)}) %all-to-all-start.1) | async-done | bytes 1048608 | tf_op jit(solution)/shard_map/all_to_all | solution.py:341
  42.4 5.6 %all-to-all-start = ((bf16[32,4,16,256]{3,2,1,0:T(8,128)(2,1)}), bf16[32,4,16,256]{3,2,1,0:T(8,128)(2,1)S(1)}, u32[]{:S(2)}, u32[]{:S(2)}) async-start(bf16[32,4,16,256]{3,2,1,0:T(8,128)(2,1)} %get-tuple-element.14), calls=%async_computation | async-start | bytes 2097152 | tf_op jit(solution)/shard_map/all_to_all | solution.py:341
  48.0 0.0 copy-done.3
  48.0 0.1 fusion
  48.1 0.1 reshape.31
  48.2 0.1 iota.10.used
  48.3 2.8 %shard_map.107.grads_in = bf16[16,128,256]{2,1,0:T(8,128)(2,1)} custom-call(bf16[128,16,256]{2,1,0:T(8,128)(2,1)S(1)} %bitcast.5, f32[128,128]{1,0:T(8,128)S(1)} %iota.10.used, bf16[256,256]{1,0:T(8,128)(2,1)} %w_out.3), custom_call_target="tpu_custom_call" | custom-call | flops 268435456 | bytes 2097152 | tf_op jit(solution)/shard_map/pallas_call | solution.py:366
  51.1 24.0 %all-to-all-done = bf16[32,4,16,256]{3,2,1,0:T(8,128)(2,1)S(1)} async-done(((bf16[32,4,16,256]{3,2,1,0:T(8,128)(2,1)}), bf16[32,4,16,256]{3,2,1,0:T(8,128)(2,1)S(1)}, u32[]{:S(2)}, u32[]{:S(2)}) %all-to-all-start) | async-done | bytes 1048608 | tf_op jit(solution)/shard_map/all_to_all | solution.py:341
  75.0 10.0 %shard_map.108 = (bf16[128,16,256]{2,1,0:T(8,128)(2,1)}, bf16[2048,256]{1,0:T(8,128)(2,1)}) custom-call(bf16[128,16,256]{2,1,0:T(8,128)(2,1)S(1)} %bitcast.6, bf16[16,128,256]{2,1,0:T(8,128)(2,1)} %shard_map.107.grads_in, f32[128,128]{1,0:T(8,128)S(1)} %iota.10.used, bf16[256,256]{1,0:T(8,128)(2,1)} %w_query.3, bf16[256,256]{1,0:T(8,128)(2,1)} %w_key.3, ...), custom_call_target="tpu_custom_call" | custom-call | flops 2281701376 | bytes 4194304 | tf_op jit(solution)/shard_map/pallas_call | solution.py:366
  85.1 5.6 %all-to-all-start.3 = ((bf16[32,4,16,256]{3,2,1,0:T(8,128)(2,1)}), bf16[32,4,16,256]{3,2,1,0:T(8,128)(2,1)S(1)}, u32[]{:S(2)}, u32[]{:S(2)}) async-start(bf16[32,4,16,256]{3,2,1,0:T(8,128)(2,1)} %bitcast.9), calls=%async_computation.3 | async-start | bytes 2097152 | tf_op jit(solution)/shard_map/all_to_all | solution.py:341
  90.6 7.6 %shard_map.109 = bf16[128,16,256]{2,1,0:T(8,128)(2,1)} custom-call(bf16[2048,256]{1,0:T(8,128)(2,1)} %get-tuple-element.15.ordered, f32[128,128]{1,0:T(8,128)S(1)} %iota.10.used, bf16[256,256]{1,0:T(8,128)(2,1)} %w_query.3, bf16[256,256]{1,0:T(8,128)(2,1)} %w_key.3, bf16[256,256]{1,0:T(8,128)(2,1)} %w_value.3, bf16[256,256]{1,0:T(8,128)(2,1)} %w_out.3), custom_call_target="tpu_custom_call" | custom-call | flops 1342177280 | bytes 2097152 | tf_op jit(solution)/shard_map/pallas_call | solution.py:366
  98.3 19.0 %all-to-all-done.3.grad_normed = bf16[32,4,16,256]{3,2,1,0:T(8,128)(2,1)S(1)} async-done(((bf16[32,4,16,256]{3,2,1,0:T(8,128)(2,1)}), bf16[32,4,16,256]{3,2,1,0:T(8,128)(2,1)S(1)}, u32[]{:S(2)}, u32[]{:S(2)}) %all-to-all-start.3) | async-done | bytes 1048608 | tf_op jit(solution)/shard_map/all_to_all | solution.py:341
  117.3 0.0 copy-start.1
  117.3 1.0 copy-done.1
  118.2 0.0 copy-start.2
  118.2 5.7 %all-to-all-start.2 = ((bf16[32,4,16,256]{3,2,1,0:T(8,128)(2,1)}), bf16[32,4,16,256]{3,2,1,0:T(8,128)(2,1)S(1)}, u32[]{:S(2)}, u32[]{:S(2)}) async-start(bf16[32,4,16,256]{3,2,1,0:T(8,128)(2,1)} %bitcast.8), calls=%async_computation.2 | async-start | bytes 2097152 | tf_op jit(solution)/shard_map/all_to_all | solution.py:341
  123.9 0.0 copy-done.2
  124.0 0.0 copy-start
  124.0 4.0 %shard_map.111 = (bf16[4,8,64,256]{3,2,1,0:T(8,128)(2,1)}, bf16[4,64,256]{2,1,0:T(8,128)(2,1)}, bf16[4,64,256]{2,1,0:T(8,128)(2,1)}) custom-call(s32[32]{0:T(128)} %frame_count.7, s32[8]{0:T(128)} %row_count.9, bf16[4,8,64,256]{3,2,1,0:T(8,128)(2,1)} %cotangent.1, bf16[32,4,16,256]{3,2,1,0:T(8,128)(2,1)} %get-tuple-element.13.hidden, ...), custom_call_target="tpu_custom_call" | custom-call | bytes 5242880 | tf_op jit(solution)/shard_map/pallas_call | solution.py:366
  127.9 1.9 %collective-permute-start.2 = (bf16[4,64,256]{2,1,0:T(8,128)(2,1)}, bf16[4,64,256]{2,1,0:T(8,128)(2,1)S(1)}, u32[]{:S(2)}, u32[]{:S(2)}) collective-permute-start(bf16[4,64,256]{2,1,0:T(8,128)(2,1)} %get-tuple-element.18), channel_id=1, source_target_pairs={{0,1},{1,2},{2,3},{3,4},{4,5},{5,6},{6,7},{8,9},{9,10},{10,11},{11... | collective-permute-start | bytes 393224 | tf_op jit(solution)/shard_map/ppermute | solution.py:335
  129.8 3.6 %collective-permute-start.3 = (bf16[4,64,256]{2,1,0:T(8,128)(2,1)}, bf16[4,64,256]{2,1,0:T(8,128)(2,1)S(1)}, u32[]{:S(2)}, u32[]{:S(2)}) collective-permute-start(bf16[4,64,256]{2,1,0:T(8,128)(2,1)} %get-tuple-element.19), channel_id=1, source_target_pairs={{1,0},{2,1},{3,2},{4,3},{5,4},{6,5},{7,6},{9,8},{10,9},{11,10},{12... | collective-permute-start | bytes 393224 | tf_op jit(solution)/shard_map/ppermute | solution.py:336
  133.5 16.9 %all-to-all-done.2.projected = bf16[32,4,16,256]{3,2,1,0:T(8,128)(2,1)S(1)} async-done(((bf16[32,4,16,256]{3,2,1,0:T(8,128)(2,1)}), bf16[32,4,16,256]{3,2,1,0:T(8,128)(2,1)S(1)}, u32[]{:S(2)}, u32[]{:S(2)}) %all-to-all-start.2) | async-done | bytes 1048608 | tf_op jit(solution)/shard_map/all_to_all | solution.py:341
  150.4 0.0 copy-done
  150.4 1.8 %shard_map.110 = bf16[4,8,64,256]{3,2,1,0:T(8,128)(2,1)} custom-call(s32[32]{0:T(128)} %frame_count.7, s32[8]{0:T(128)} %row_count.9, bf16[32,4,16,256]{3,2,1,0:T(8,128)(2,1)S(1)} %copy-done, bf16[32,4,16,256]{3,2,1,0:T(8,128)(2,1)S(1)} %all-to-all-done.2.projected), custom_call_target="tpu_custom_call" | custom-call | bytes 3145728 | tf_op jit(solution)/shard_map/pallas_call | solution.py:366
  152.2 0.0 collective-permute-done.2.above
  152.2 0.0 collective-permute-done.3.below
  152.2 6.0 %shard_map.112 = bf16[4,8,64,256]{3,2,1,0:T(8,128)(2,1)} custom-call(s32[32]{0:T(128)} %frame_count.7, s32[8]{0:T(128)} %row_count.9, bf16[4,8,64,256]{3,2,1,0:T(8,128)(2,1)} %get-tuple-element.17.field, bf16[4,64,256]{2,1,0:T(8,128)(2,1)S(1)} %collective-permute-done.2.above, bf16[4,64,256]{2,1,0:T(8,128)(2,1)S(1)} %collective-permute-done.3.below, ...), custom_call_target="tpu_custom_call" | custom-call | flops 2415919104 | bytes 3145728 | tf_op jit(solution)/shard_map/pallas_call | solution.py:366
Async XLA Ops:
  2.7 39.8 %all-to-all-start.1 = ((bf16[32,4,16,256]{3,2,1,0:T(8,128)(2,1)}), bf16[32,4,16,256]{3,2,1,0:T(8,128)(2,1)S(1)}, u32[]{:S(2)}, u32[]{:S(2)}) async-start(bf16[32,4,16,256]{3,2,1,0:T(8,128)(2,1)} %shard_map.106), calls=%async_computation.1 | async-start | bytes 2097152 | tf_op jit(solution)/shard_map/all_to_all | solution.py:341
  16.0 6.3 %collective-permute-start = (bf16[4,64,256]{2,1,0:T(8,128)(2,1)S(1)}, bf16[4,64,256]{2,1,0:T(8,128)(2,1)S(1)}, u32[]{:S(2)}, u32[]{:S(2)}) collective-permute-start(bf16[4,64,256]{2,1,0:T(8,128)(2,1)S(1)} %get-tuple-element.11), channel_id=1, source_target_pairs={{0,1},{1,2},{2,3},{3,4},{4,5},{5,6},{6,7},{8,9},{9,10},{10,11},{11... | collective-permute-start | bytes 393224 | tf_op jit(solution)/shard_map/ppermute | solution.py:335
  18.0 6.1 %collective-permute-start.1 = (bf16[4,64,256]{2,1,0:T(8,128)(2,1)S(1)}, bf16[4,64,256]{2,1,0:T(8,128)(2,1)S(1)}, u32[]{:S(2)}, u32[]{:S(2)}) collective-permute-start(bf16[4,64,256]{2,1,0:T(8,128)(2,1)S(1)} %get-tuple-element.12), channel_id=1, source_target_pairs={{1,0},{2,1},{3,2},{4,3},{5,4},{6,5},{7,6},{9,8},{10,9},{11,10},{12... | collective-permute-start | bytes 393224 | tf_op jit(solution)/shard_map/ppermute | solution.py:336
  30.8 17.2 %copy-start.3 = (s32[32]{0:T(128)S(1)}, s32[32]{0:T(128)}, u32[]{:S(2)}) copy-start(s32[32]{0:T(128)} %frame_count.7) | copy-start | bytes 388
  42.4 32.6 %all-to-all-start = ((bf16[32,4,16,256]{3,2,1,0:T(8,128)(2,1)}), bf16[32,4,16,256]{3,2,1,0:T(8,128)(2,1)S(1)}, u32[]{:S(2)}, u32[]{:S(2)}) async-start(bf16[32,4,16,256]{3,2,1,0:T(8,128)(2,1)} %get-tuple-element.14), calls=%async_computation | async-start | bytes 2097152 | tf_op jit(solution)/shard_map/all_to_all | solution.py:341
  85.1 32.2 %all-to-all-start.3 = ((bf16[32,4,16,256]{3,2,1,0:T(8,128)(2,1)}), bf16[32,4,16,256]{3,2,1,0:T(8,128)(2,1)S(1)}, u32[]{:S(2)}, u32[]{:S(2)}) async-start(bf16[32,4,16,256]{3,2,1,0:T(8,128)(2,1)} %bitcast.9), calls=%async_computation.3 | async-start | bytes 2097152 | tf_op jit(solution)/shard_map/all_to_all | solution.py:341
  117.3 1.0 copy-start.1
  118.2 5.7 %copy-start.2 = (bf16[32,4,16,256]{3,2,1,0:T(8,128)(2,1)S(1)}, bf16[32,4,16,256]{3,2,1,0:T(8,128)(2,1)}, u32[]{:S(2)}) copy-start(bf16[32,4,16,256]{3,2,1,0:T(8,128)(2,1)} %copy-done.1) | copy-start | bytes 3145732
  118.2 32.2 %all-to-all-start.2 = ((bf16[32,4,16,256]{3,2,1,0:T(8,128)(2,1)}), bf16[32,4,16,256]{3,2,1,0:T(8,128)(2,1)S(1)}, u32[]{:S(2)}, u32[]{:S(2)}) async-start(bf16[32,4,16,256]{3,2,1,0:T(8,128)(2,1)} %bitcast.8), calls=%async_computation.2 | async-start | bytes 2097152 | tf_op jit(solution)/shard_map/all_to_all | solution.py:341
  124.0 26.5 %copy-start = (bf16[32,4,16,256]{3,2,1,0:T(8,128)(2,1)S(1)}, bf16[32,4,16,256]{3,2,1,0:T(8,128)(2,1)}, u32[]{:S(2)}) copy-start(bf16[32,4,16,256]{3,2,1,0:T(8,128)(2,1)} %get-tuple-element.13.hidden) | copy-start | bytes 3145732
  127.9 24.3 %collective-permute-start.2 = (bf16[4,64,256]{2,1,0:T(8,128)(2,1)}, bf16[4,64,256]{2,1,0:T(8,128)(2,1)S(1)}, u32[]{:S(2)}, u32[]{:S(2)}) collective-permute-start(bf16[4,64,256]{2,1,0:T(8,128)(2,1)} %get-tuple-element.18), channel_id=1, source_target_pairs={{0,1},{1,2},{2,3},{3,4},{4,5},{5,6},{6,7},{8,9},{9,10},{10,11},{11... | collective-permute-start | bytes 393224 | tf_op jit(solution)/shard_map/ppermute | solution.py:335
  129.8 22.4 %collective-permute-start.3 = (bf16[4,64,256]{2,1,0:T(8,128)(2,1)}, bf16[4,64,256]{2,1,0:T(8,128)(2,1)S(1)}, u32[]{:S(2)}, u32[]{:S(2)}) collective-permute-start(bf16[4,64,256]{2,1,0:T(8,128)(2,1)} %get-tuple-element.19), channel_id=1, source_target_pairs={{1,0},{2,1},{3,2},{4,3},{5,4},{6,5},{7,6},{9,8},{10,9},{11,10},{12... | collective-permute-start | bytes 393224 | tf_op jit(solution)/shard_map/ppermute | solution.py:336

commit v3 on v2

--- a/solution.py
+++ b/solution.py
@@ -183,56 +183,88 @@
 
 def attention_kernel(
     normed, grads_in, used, w_query, w_key, w_value, grad_normed, kept,
-    grads, weights, spread, result, out, ordered, query_s, key_s, value_s, dq_s, dk_s, dv_s, sems,
+    grads, weights, bias, spread, result, out, ordered, fields, scores, grad_probs,
+    probs_low, grad_scores, backs, sems,
 ):
+    all_frames, positions, channels = normed.shape
     loads = [
-        pltpu.make_async_copy(w, weights.at[i], sems.at[i])
+        pltpu.make_async_copy(w, weights.at[:, i * channels : (i + 1) * channels], sems.at[i])
         for i, w in enumerate((w_query, w_key, w_value))
     ]
     loads.append(pltpu.make_async_copy(grads_in, grads, sems.at[3]))
     for copy in loads:
         copy.start()
-    all_frames, positions, channels = normed.shape
     widen(normed, spread)
-    allowed = allowed_pairs(used)
     scale = channels ** (-0.5)
-    for copy in loads[:3]:
-        copy.wait()
+    bias[...] = jnp.where(allowed_pairs(used), 0.0, -1e30)
     keeps = []
 
-    for first in range(0, positions, GROUP):
+    def rows_of(p):
+        return slice(p * all_frames, (p + 1) * all_frames)
+
+    def lanes_of(i):
+        return slice(i * channels, (i + 1) * channels)
+
+    def project_group(first):
         group = slice(first * all_frames, (first + GROUP) * all_frames)
         for p in range(first, first + GROUP):
-            ordered[p * all_frames : (p + 1) * all_frames] = load_position(spread, p, positions)
-        rows = ordered[group]
+            ordered[rows_of(p)] = load_position(spread, p, positions)
         keep = pltpu.make_async_copy(
             ordered.at[group], kept.at[group], sems.at[4 + first // GROUP]
         )
         keep.start()
         keeps.append(keep)
-        query_s[group] = dot(rows, weights[0]).astype(BF16)
-        key_s[group] = dot(rows, weights[1]).astype(BF16)
-        value_s[group] = dot(rows, weights[2]).astype(BF16)
-        if first == 0:
-            loads[3].wait()
-        for p in range(first, first + GROUP):
-            here = slice(p * all_frames, (p + 1) * all_frames)
-            query, key, value, grad = query_s[here], key_s[here], value_s[here], grads[p]
-            probs = softmax_probs(query, key, allowed, scale)
-            low = probs.astype(BF16)
-            grad_probs = dot(value, grad, (1, 1))
-            delta = jnp.sum(low.astype(F32) * grad_probs, axis=0, keepdims=True)
-            grad_scores = (probs * (grad_probs - delta) * scale).astype(BF16)
-            dv_s[here] = dot(low, grad).astype(BF16)
-            dk_s[here] = dot(grad_scores, query).astype(BF16)
-            dq_s[here] = dot(grad_scores, key, (0, 0)).astype(BF16)
-        total = dot(dq_s[group], weights[0], (1, 1))
-        total = total + dot(dk_s[group], weights[1], (1, 1))
-        total = total + dot(dv_s[group], weights[2], (1, 1))
-        total = total.astype(BF16).astype(F32)
+        for i in range(3):
+            product = dot(ordered[group], weights[:, lanes_of(i)])
+            fields[group, lanes_of(i)] = product.astype(BF16)
+
+    def pair_products(p):
+        here = rows_of(p)
+        scores[p] = dot(fields[here, lanes_of(1)], fields[here, lanes_of(0)], (1, 1))
+        grad_probs[p] = dot(fields[here, lanes_of(2)], grads[p], (1, 1))
+
+    def softmax(p):
+        logits = scores[p] * scale + bias[...]
+        expo = jnp.exp(logits - jnp.max(logits, axis=0, keepdims=True))
+        probs = expo * (1.0 / jnp.sum(expo, axis=0, keepdims=True))
+        low = probs.astype(BF16)
+        probs_low[p] = low
+        grad = grad_probs[p]
+        delta = jnp.sum(low.astype(F32) * grad, axis=0, keepdims=True)
+        grad_scores[p] = (probs * (grad - delta) * scale).astype(BF16)
+
+    def back_products(p):
+        here = rows_of(p)
+        backs[here, lanes_of(0)] = dot(
+            grad_scores[p], fields[here, lanes_of(1)], (0, 0)
+        ).astype(BF16)
+        backs[here, lanes_of(1)] = dot(grad_scores[p], fields[here, lanes_of(0)]).astype(BF16)
+        backs[here, lanes_of(2)] = dot(probs_low[p], grads[p]).astype(BF16)
+
+    def back_group(first):
+        group = slice(first * all_frames, (first + GROUP) * all_frames)
+        total = dot(backs[group], weights[...], (1, 1)).astype(BF16).astype(F32)
         for j in range(GROUP):
             part = total[j * all_frames : (j + 1) * all_frames]
             store_position(result, first + j, positions, part)
+
+    for copy in loads[:3]:
+        copy.wait()
+    project_group(0)
+    loads[3].wait()
+    for first in range(0, positions, GROUP):
+        group = range(first, first + GROUP)
+        for p in group:
+            pair_products(p)
+        if first + GROUP < positions:
+            project_group(first + GROUP)
+        for p in group:
+            softmax(p)
+        if first > 0:
+            back_group(first - GROUP)
+        for p in group:
+            back_products(p)
+    back_group(positions - GROUP)
     narrow(result, out, grad_normed, sems)
     for copy in keeps:
         copy.wait()
@@ -376,6 +408,8 @@
     wide = VMEM((channels // LANES, all_frames * positions, LANES), F32)
     flat = VMEM((all_frames * positions, channels), BF16)
     part = VMEM((GROUP * all_frames, channels), BF16)
+    triple = VMEM((all_frames * positions, 3 * channels), BF16)
+    pairs = (all_frames, all_frames)
     chunked = (frames, blocks, positions, channels)
 
     (outgoing,) = call(
@@ -405,8 +439,12 @@
         [shaped(spread, BF16), shaped((all_frames * positions, channels), BF16)],
         [ON_CHIP, HBM, ON_CHIP, HBM, HBM, HBM],
         [normed_in, grads, used, w_query, w_key, w_value],
-        [VMEM(ordered, BF16), VMEM((3, channels, channels), BF16), wide, wide, VMEM(spread, BF16)]
-        + [flat] * 7 + [dma((4 + positions // GROUP,))],
+        [
+            VMEM(ordered, BF16), VMEM((channels, 3 * channels), BF16), VMEM(pairs, F32), wide, wide,
+            VMEM(spread, BF16), flat, triple, VMEM((positions, *pairs), F32),
+            VMEM((positions, *pairs), F32), VMEM((positions, *pairs), BF16),
+            VMEM((positions, *pairs), BF16), triple, dma((4 + positions // GROUP,)),
+        ],
         6 * product + 5 * inner, 4 * size, [HBM, HBM],
     )
     grad_home = exchange(grad_normed.reshape(sent))

time: 159 us -> 156 us (0.981)
  Pallas kernels: 42.6 us -> 39.7 us
    pallas_call x9, Pallas kernels: 42.6 us -> 39.7 us  [call(): pl.pallas_call(kernel, out_shape=outs, in_specs=specs(*ins), out_specs=sp...]
where the time goes in v3:
time: 156 us; the launch traced here: 155 us
  waiting for transfers between devices  74 us (47%)
  Pallas kernels  39.7 us (25%)
  starting transfers between devices  39.7 us (25%)
    all_to_all x4, waiting for transfers between devices, exchange(): return lax.all_to_all(blocks, 'tm', split_axis=0, concat_axis=0, tiled=True)  71.5 us
    pallas_call x9, Pallas kernels, call(): pl.pallas_call(kernel, out_shape=outs, in_specs=specs(*ins), out_specs=sp...  39.7 us
    all_to_all x4, starting transfers between devices, exchange(): return lax.all_to_all(blocks, 'tm', split_axis=0, concat_axis=0, tiled=True)  28.5 us
    ppermute x2, starting transfers between devices, share_rows(): below = lax.ppermute(head, 'space', [(i + 1, i) for i in range(ends)])  7.28 us
    ppermute x2, starting transfers between devices, share_rows(): above = lax.ppermute(tail, 'space', [(i, i + 1) for i in range(ends)])  3.83 us
  transfers between devices with their start and end apart: 8, of which 6 were waited for; matrix products, arithmetic and copies ran while one was open for 0% of the time, Pallas kernels for 16%

profile of v3, /device:TPU:10, one launch (start us, length us, event | category | flops | bytes accessed | tf_op | source)
XLA Modules:
  0.0 155.3 jit_solution(10544347890815835593)
XLA Ops:
  0.6 2.0 %shard_map.106 = bf16[32,4,16,256]{3,2,1,0:T(8,128)(2,1)} custom-call(bf16[4,32,16,256]{3,2,1,0:T(8,128)(2,1)} %bitcast.7), custom_call_target="tpu_custom_call" | custom-call | bytes 1048576 | tf_op jit(solution)/shard_map/pallas_call | solution.py:398
  2.7 11.7 %all-to-all-start.1 = ((bf16[32,4,16,256]{3,2,1,0:T(8,128)(2,1)}), bf16[32,4,16,256]{3,2,1,0:T(8,128)(2,1)S(1)}, u32[]{:S(2)}, u32[]{:S(2)}) async-start(bf16[32,4,16,256]{3,2,1,0:T(8,128)(2,1)} %shard_map.106), calls=%async_computation.1 | async-start | bytes 2097152 | tf_op jit(solution)/shard_map/all_to_all | solution.py:373
  14.4 1.7 %shard_map.104 = (bf16[4,64,256]{2,1,0:T(8,128)(2,1)S(1)}, bf16[4,64,256]{2,1,0:T(8,128)(2,1)S(1)}) custom-call(s32[8]{0:T(128)} %row_count.9, bf16[4,8,64,256]{3,2,1,0:T(8,128)(2,1)} %field.3), custom_call_target="tpu_custom_call" | custom-call | bytes 262144 | tf_op jit(solution)/shard_map/pallas_call | solution.py:398
  16.0 1.9 %collective-permute-start = (bf16[4,64,256]{2,1,0:T(8,128)(2,1)S(1)}, bf16[4,64,256]{2,1,0:T(8,128)(2,1)S(1)}, u32[]{:S(2)}, u32[]{:S(2)}) collective-permute-start(bf16[4,64,256]{2,1,0:T(8,128)(2,1)S(1)} %get-tuple-element.11), channel_id=1, source_target_pairs={{0,1},{1,2},{2,3},{3,4},{4,5},{5,6},{6,7},{8,9},{9,10},{10,11},{11... | collective-permute-start | bytes 393224 | tf_op jit(solution)/shard_map/ppermute | solution.py:367
  18.0 3.6 %collective-permute-start.1 = (bf16[4,64,256]{2,1,0:T(8,128)(2,1)S(1)}, bf16[4,64,256]{2,1,0:T(8,128)(2,1)S(1)}, u32[]{:S(2)}, u32[]{:S(2)}) collective-permute-start(bf16[4,64,256]{2,1,0:T(8,128)(2,1)S(1)} %get-tuple-element.12), channel_id=1, source_target_pairs={{1,0},{2,1},{3,2},{4,3},{5,4},{6,5},{7,6},{9,8},{10,9},{11,10},{12... | collective-permute-start | bytes 393224 | tf_op jit(solution)/shard_map/ppermute | solution.py:368
  21.6 0.7 collective-permute-done.above
  22.3 1.8 %collective-permute-done.1.below = bf16[4,64,256]{2,1,0:T(8,128)(2,1)S(1)} collective-permute-done((bf16[4,64,256]{2,1,0:T(8,128)(2,1)S(1)}, bf16[4,64,256]{2,1,0:T(8,128)(2,1)S(1)}, u32[]{:S(2)}, u32[]{:S(2)}) %collective-permute-start.1) | collective-permute-done | bytes 131104 | tf_op jit(solution)/shard_map/ppermute | solution.py:368
  24.1 6.7 %shard_map.105 = (bf16[32,4,16,256]{3,2,1,0:T(8,128)(2,1)}, bf16[32,4,16,256]{3,2,1,0:T(8,128)(2,1)}) custom-call(s32[32]{0:T(128)} %frame_count.7, s32[8]{0:T(128)} %row_count.9, bf16[4,8,64,256]{3,2,1,0:T(8,128)(2,1)} %field.3, bf16[4,64,256]{2,1,0:T(8,128)(2,1)S(1)} %collective-permute-done.above, bf16[4,64,256]{2,1,0:T(8,128)(2,1)S(1)} %collective-permute-done.1.below, ...), custom_call_target="tpu_custom_call" | custom-call | flops 2415919104 | bytes 4194304 | tf_op jit(solution)/shard_map/pallas_call | solution.py:398
  30.8 0.0 copy-start.3
  30.9 11.6 %all-to-all-done.1 = bf16[32,4,16,256]{3,2,1,0:T(8,128)(2,1)S(1)} async-done(((bf16[32,4,16,256]{3,2,1,0:T(8,128)(2,1)}), bf16[32,4,16,256]{3,2,1,0:T(8,128)(2,1)S(1)}, u32[]{:S(2)}, u32[]{:S(2)}) %all-to-all-start.1) | async-done | bytes 1048608 | tf_op jit(solution)/shard_map/all_to_all | solution.py:373
  42.4 5.6 %all-to-all-start = ((bf16[32,4,16,256]{3,2,1,0:T(8,128)(2,1)}), bf16[32,4,16,256]{3,2,1,0:T(8,128)(2,1)S(1)}, u32[]{:S(2)}, u32[]{:S(2)}) async-start(bf16[32,4,16,256]{3,2,1,0:T(8,128)(2,1)} %get-tuple-element.14), calls=%async_computation | async-start | bytes 2097152 | tf_op jit(solution)/shard_map/all_to_all | solution.py:373
  48.0 0.0 copy-done.3
  48.0 0.1 fusion
  48.1 0.1 reshape.31
  48.2 0.1 iota.10.used
  48.3 2.8 %shard_map.107.grads_in = bf16[16,128,256]{2,1,0:T(8,128)(2,1)} custom-call(bf16[128,16,256]{2,1,0:T(8,128)(2,1)S(1)} %bitcast.5, f32[128,128]{1,0:T(8,128)S(1)} %iota.10.used, bf16[256,256]{1,0:T(8,128)(2,1)} %w_out.3), custom_call_target="tpu_custom_call" | custom-call | flops 268435456 | bytes 2097152 | tf_op jit(solution)/shard_map/pallas_call | solution.py:398
  51.1 24.0 %all-to-all-done = bf16[32,4,16,256]{3,2,1,0:T(8,128)(2,1)S(1)} async-done(((bf16[32,4,16,256]{3,2,1,0:T(8,128)(2,1)}), bf16[32,4,16,256]{3,2,1,0:T(8,128)(2,1)S(1)}, u32[]{:S(2)}, u32[]{:S(2)}) %all-to-all-start) | async-done | bytes 1048608 | tf_op jit(solution)/shard_map/all_to_all | solution.py:373
  75.0 7.1 %shard_map.108 = (bf16[128,16,256]{2,1,0:T(8,128)(2,1)}, bf16[2048,256]{1,0:T(8,128)(2,1)}) custom-call(bf16[128,16,256]{2,1,0:T(8,128)(2,1)S(1)} %bitcast.6, bf16[16,128,256]{2,1,0:T(8,128)(2,1)} %shard_map.107.grads_in, f32[128,128]{1,0:T(8,128)S(1)} %iota.10.used, bf16[256,256]{1,0:T(8,128)(2,1)} %w_query.3, bf16[256,256]{1,0:T(8,128)(2,1)} %w_key.3, ...), custom_call_target="tpu_custom_call" | custom-call | flops 2281701376 | bytes 4194304 | tf_op jit(solution)/shard_map/pallas_call | solution.py:398
  82.2 5.6 %all-to-all-start.3 = ((bf16[32,4,16,256]{3,2,1,0:T(8,128)(2,1)}), bf16[32,4,16,256]{3,2,1,0:T(8,128)(2,1)S(1)}, u32[]{:S(2)}, u32[]{:S(2)}) async-start(bf16[32,4,16,256]{3,2,1,0:T(8,128)(2,1)} %bitcast.9), calls=%async_computation.3 | async-start | bytes 2097152 | tf_op jit(solution)/shard_map/all_to_all | solution.py:373
  87.8 7.6 %shard_map.109 = bf16[128,16,256]{2,1,0:T(8,128)(2,1)} custom-call(bf16[2048,256]{1,0:T(8,128)(2,1)} %get-tuple-element.15.ordered, f32[128,128]{1,0:T(8,128)S(1)} %iota.10.used, bf16[256,256]{1,0:T(8,128)(2,1)} %w_query.3, bf16[256,256]{1,0:T(8,128)(2,1)} %w_key.3, bf16[256,256]{1,0:T(8,128)(2,1)} %w_value.3, bf16[256,256]{1,0:T(8,128)(2,1)} %w_out.3), custom_call_target="tpu_custom_call" | custom-call | flops 1342177280 | bytes 2097152 | tf_op jit(solution)/shard_map/pallas_call | solution.py:398
  95.4 19.0 %all-to-all-done.3.grad_normed = bf16[32,4,16,256]{3,2,1,0:T(8,128)(2,1)S(1)} async-done(((bf16[32,4,16,256]{3,2,1,0:T(8,128)(2,1)}), bf16[32,4,16,256]{3,2,1,0:T(8,128)(2,1)S(1)}, u32[]{:S(2)}, u32[]{:S(2)}) %all-to-all-start.3) | async-done | bytes 1048608 | tf_op jit(solution)/shard_map/all_to_all | solution.py:373
  114.4 0.0 copy-start.1
  114.4 1.0 copy-done.1
  115.4 0.0 copy-start.2
  115.4 5.7 %all-to-all-start.2 = ((bf16[32,4,16,256]{3,2,1,0:T(8,128)(2,1)}), bf16[32,4,16,256]{3,2,1,0:T(8,128)(2,1)S(1)}, u32[]{:S(2)}, u32[]{:S(2)}) async-start(bf16[32,4,16,256]{3,2,1,0:T(8,128)(2,1)} %bitcast.8), calls=%async_computation.2 | async-start | bytes 2097152 | tf_op jit(solution)/shard_map/all_to_all | solution.py:373
  121.1 0.0 copy-done.2
  121.1 0.0 copy-start
  121.1 4.0 %shard_map.111 = (bf16[4,8,64,256]{3,2,1,0:T(8,128)(2,1)}, bf16[4,64,256]{2,1,0:T(8,128)(2,1)}, bf16[4,64,256]{2,1,0:T(8,128)(2,1)}) custom-call(s32[32]{0:T(128)} %frame_count.7, s32[8]{0:T(128)} %row_count.9, bf16[4,8,64,256]{3,2,1,0:T(8,128)(2,1)} %cotangent.1, bf16[32,4,16,256]{3,2,1,0:T(8,128)(2,1)} %get-tuple-element.13.hidden, ...), custom_call_target="tpu_custom_call" | custom-call | bytes 5242880 | tf_op jit(solution)/shard_map/pallas_call | solution.py:398
  125.1 1.9 %collective-permute-start.2 = (bf16[4,64,256]{2,1,0:T(8,128)(2,1)}, bf16[4,64,256]{2,1,0:T(8,128)(2,1)S(1)}, u32[]{:S(2)}, u32[]{:S(2)}) collective-permute-start(bf16[4,64,256]{2,1,0:T(8,128)(2,1)} %get-tuple-element.18), channel_id=1, source_target_pairs={{0,1},{1,2},{2,3},{3,4},{4,5},{5,6},{6,7},{8,9},{9,10},{10,11},{11... | collective-permute-start | bytes 393224 | tf_op jit(solution)/shard_map/ppermute | solution.py:367
  127.0 3.6 %collective-permute-start.3 = (bf16[4,64,256]{2,1,0:T(8,128)(2,1)}, bf16[4,64,256]{2,1,0:T(8,128)(2,1)S(1)}, u32[]{:S(2)}, u32[]{:S(2)}) collective-permute-start(bf16[4,64,256]{2,1,0:T(8,128)(2,1)} %get-tuple-element.19), channel_id=1, source_target_pairs={{1,0},{2,1},{3,2},{4,3},{5,4},{6,5},{7,6},{9,8},{10,9},{11,10},{12... | collective-permute-start | bytes 393224 | tf_op jit(solution)/shard_map/ppermute | solution.py:368
  130.6 16.9 %all-to-all-done.2.projected = bf16[32,4,16,256]{3,2,1,0:T(8,128)(2,1)S(1)} async-done(((bf16[32,4,16,256]{3,2,1,0:T(8,128)(2,1)}), bf16[32,4,16,256]{3,2,1,0:T(8,128)(2,1)S(1)}, u32[]{:S(2)}, u32[]{:S(2)}) %all-to-all-start.2) | async-done | bytes 1048608 | tf_op jit(solution)/shard_map/all_to_all | solution.py:373
  147.6 0.0 copy-done
  147.6 1.8 %shard_map.110 = bf16[4,8,64,256]{3,2,1,0:T(8,128)(2,1)} custom-call(s32[32]{0:T(128)} %frame_count.7, s32[8]{0:T(128)} %row_count.9, bf16[32,4,16,256]{3,2,1,0:T(8,128)(2,1)S(1)} %copy-done, bf16[32,4,16,256]{3,2,1,0:T(8,128)(2,1)S(1)} %all-to-all-done.2.projected), custom_call_target="tpu_custom_call" | custom-call | bytes 3145728 | tf_op jit(solution)/shard_map/pallas_call | solution.py:398
  149.3 0.0 collective-permute-done.2.above
  149.3 0.0 collective-permute-done.3.below
  149.4 6.0 %shard_map.112 = bf16[4,8,64,256]{3,2,1,0:T(8,128)(2,1)} custom-call(s32[32]{0:T(128)} %frame_count.7, s32[8]{0:T(128)} %row_count.9, bf16[4,8,64,256]{3,2,1,0:T(8,128)(2,1)} %get-tuple-element.17.field, bf16[4,64,256]{2,1,0:T(8,128)(2,1)S(1)} %collective-permute-done.2.above, bf16[4,64,256]{2,1,0:T(8,128)(2,1)S(1)} %collective-permute-done.3.below, ...), custom_call_target="tpu_custom_call" | custom-call | flops 2415919104 | bytes 3145728 | tf_op jit(solution)/shard_map/pallas_call | solution.py:398
Async XLA Ops:
  2.7 39.8 %all-to-all-start.1 = ((bf16[32,4,16,256]{3,2,1,0:T(8,128)(2,1)}), bf16[32,4,16,256]{3,2,1,0:T(8,128)(2,1)S(1)}, u32[]{:S(2)}, u32[]{:S(2)}) async-start(bf16[32,4,16,256]{3,2,1,0:T(8,128)(2,1)} %shard_map.106), calls=%async_computation.1 | async-start | bytes 2097152 | tf_op jit(solution)/shard_map/all_to_all | solution.py:373
  16.0 6.3 %collective-permute-start = (bf16[4,64,256]{2,1,0:T(8,128)(2,1)S(1)}, bf16[4,64,256]{2,1,0:T(8,128)(2,1)S(1)}, u32[]{:S(2)}, u32[]{:S(2)}) collective-permute-start(bf16[4,64,256]{2,1,0:T(8,128)(2,1)S(1)} %get-tuple-element.11), channel_id=1, source_target_pairs={{0,1},{1,2},{2,3},{3,4},{4,5},{5,6},{6,7},{8,9},{9,10},{10,11},{11... | collective-permute-start | bytes 393224 | tf_op jit(solution)/shard_map/ppermute | solution.py:367
  18.0 6.1 %collective-permute-start.1 = (bf16[4,64,256]{2,1,0:T(8,128)(2,1)S(1)}, bf16[4,64,256]{2,1,0:T(8,128)(2,1)S(1)}, u32[]{:S(2)}, u32[]{:S(2)}) collective-permute-start(bf16[4,64,256]{2,1,0:T(8,128)(2,1)S(1)} %get-tuple-element.12), channel_id=1, source_target_pairs={{1,0},{2,1},{3,2},{4,3},{5,4},{6,5},{7,6},{9,8},{10,9},{11,10},{12... | collective-permute-start | bytes 393224 | tf_op jit(solution)/shard_map/ppermute | solution.py:368
  30.8 17.2 %copy-start.3 = (s32[32]{0:T(128)S(1)}, s32[32]{0:T(128)}, u32[]{:S(2)}) copy-start(s32[32]{0:T(128)} %frame_count.7) | copy-start | bytes 388
  42.4 32.6 %all-to-all-start = ((bf16[32,4,16,256]{3,2,1,0:T(8,128)(2,1)}), bf16[32,4,16,256]{3,2,1,0:T(8,128)(2,1)S(1)}, u32[]{:S(2)}, u32[]{:S(2)}) async-start(bf16[32,4,16,256]{3,2,1,0:T(8,128)(2,1)} %get-tuple-element.14), calls=%async_computation | async-start | bytes 2097152 | tf_op jit(solution)/shard_map/all_to_all | solution.py:373
  82.2 32.2 %all-to-all-start.3 = ((bf16[32,4,16,256]{3,2,1,0:T(8,128)(2,1)}), bf16[32,4,16,256]{3,2,1,0:T(8,128)(2,1)S(1)}, u32[]{:S(2)}, u32[]{:S(2)}) async-start(bf16[32,4,16,256]{3,2,1,0:T(8,128)(2,1)} %bitcast.9), calls=%async_computation.3 | async-start | bytes 2097152 | tf_op jit(solution)/shard_map/all_to_all | solution.py:373
  114.4 1.0 copy-start.1
  115.4 5.7 %copy-start.2 = (bf16[32,4,16,256]{3,2,1,0:T(8,128)(2,1)S(1)}, bf16[32,4,16,256]{3,2,1,0:T(8,128)(2,1)}, u32[]{:S(2)}) copy-start(bf16[32,4,16,256]{3,2,1,0:T(8,128)(2,1)} %copy-done.1) | copy-start | bytes 3145732
  115.4 32.2 %all-to-all-start.2 = ((bf16[32,4,16,256]{3,2,1,0:T(8,128)(2,1)}), bf16[32,4,16,256]{3,2,1,0:T(8,128)(2,1)S(1)}, u32[]{:S(2)}, u32[]{:S(2)}) async-start(bf16[32,4,16,256]{3,2,1,0:T(8,128)(2,1)} %bitcast.8), calls=%async_computation.2 | async-start | bytes 2097152 | tf_op jit(solution)/shard_map/all_to_all | solution.py:373
  121.1 26.5 %copy-start = (bf16[32,4,16,256]{3,2,1,0:T(8,128)(2,1)S(1)}, bf16[32,4,16,256]{3,2,1,0:T(8,128)(2,1)}, u32[]{:S(2)}) copy-start(bf16[32,4,16,256]{3,2,1,0:T(8,128)(2,1)} %get-tuple-element.13.hidden) | copy-start | bytes 3145732
  125.1 24.3 %collective-permute-start.2 = (bf16[4,64,256]{2,1,0:T(8,128)(2,1)}, bf16[4,64,256]{2,1,0:T(8,128)(2,1)S(1)}, u32[]{:S(2)}, u32[]{:S(2)}) collective-permute-start(bf16[4,64,256]{2,1,0:T(8,128)(2,1)} %get-tuple-element.18), channel_id=1, source_target_pairs={{0,1},{1,2},{2,3},{3,4},{4,5},{5,6},{6,7},{8,9},{9,10},{10,11},{11... | collective-permute-start | bytes 393224 | tf_op jit(solution)/shard_map/ppermute | solution.py:367
  127.0 22.4 %collective-permute-start.3 = (bf16[4,64,256]{2,1,0:T(8,128)(2,1)}, bf16[4,64,256]{2,1,0:T(8,128)(2,1)S(1)}, u32[]{:S(2)}, u32[]{:S(2)}) collective-permute-start(bf16[4,64,256]{2,1,0:T(8,128)(2,1)} %get-tuple-element.19), channel_id=1, source_target_pairs={{1,0},{2,1},{3,2},{4,3},{5,4},{6,5},{7,6},{9,8},{10,9},{11,10},{12... | collective-permute-start | bytes 393224 | tf_op jit(solution)/shard_map/ppermute | solution.py:368

commit v4 on v3

--- a/solution.py
+++ b/solution.py
@@ -156,16 +156,20 @@
         copy.wait()
 
 
-def grads_kernel(cotangent, used, w_out, grad_out, spread, ordered):
+def grads_kernel(
+    cotangent, used, w_out, w_query, w_key, w_value, folded, mixed, spread, ordered, attended
+):
     all_frames, positions, channels = cotangent.shape
+    mixed[...] = (dot(w_query[...], w_key[...], (1, 1)) * channels ** (-0.5)).astype(BF16)
     widen(cotangent, spread)
     for first in range(0, positions, GROUP):
         for p in range(first, first + GROUP):
             here = slice(p * all_frames, (p + 1) * all_frames)
             ordered[here] = load_position(spread, p, positions, used[...])
         here = slice(first * all_frames, (first + GROUP) * all_frames)
-        grads = dot(ordered[here], w_out[...], (1, 1)).astype(BF16)
-        grad_out[first : first + GROUP] = grads.reshape(GROUP, all_frames, channels)
+        attended[here] = dot(ordered[here], w_out[...], (1, 1)).astype(BF16)
+        grads = dot(attended[here], w_value[...], (1, 1)).astype(BF16)
+        folded[first : first + GROUP] = grads.reshape(GROUP, all_frames, channels)
 
 
 def softmax_probs(query, key, allowed, scale):
@@ -182,76 +186,68 @@
 
 
 def attention_kernel(
-    normed, grads_in, used, w_query, w_key, w_value, grad_normed, kept,
-    grads, weights, bias, spread, result, out, ordered, fields, scores, grad_probs,
-    probs_low, grad_scores, backs, sems,
+    normed, folded, used, mixed, grad_normed, kept,
+    weights, bias, spread, result, out, ordered, sides, products, mix, inner, direct, sems,
 ):
     all_frames, positions, channels = normed.shape
+    pieces = positions // GROUP
     loads = [
-        pltpu.make_async_copy(w, weights.at[:, i * channels : (i + 1) * channels], sems.at[i])
-        for i, w in enumerate((w_query, w_key, w_value))
+        pltpu.make_async_copy(mixed, weights, sems.at[0]),
+        pltpu.make_async_copy(folded, sides.at[:, all_frames:], sems.at[1]),
     ]
-    loads.append(pltpu.make_async_copy(grads_in, grads, sems.at[3]))
     for copy in loads:
         copy.start()
     widen(normed, spread)
-    scale = channels ** (-0.5)
     bias[...] = jnp.where(allowed_pairs(used), 0.0, -1e30)
     keeps = []
 
     def rows_of(p):
         return slice(p * all_frames, (p + 1) * all_frames)
 
-    def lanes_of(i):
-        return slice(i * channels, (i + 1) * channels)
+    def group_of(first):
+        return slice(first * all_frames, (first + GROUP) * all_frames)
 
     def project_group(first):
-        group = slice(first * all_frames, (first + GROUP) * all_frames)
+        group = group_of(first)
         for p in range(first, first + GROUP):
             ordered[rows_of(p)] = load_position(spread, p, positions)
         keep = pltpu.make_async_copy(
-            ordered.at[group], kept.at[group], sems.at[4 + first // GROUP]
+            ordered.at[group], kept.at[group], sems.at[pieces + first // GROUP]
         )
         keep.start()
         keeps.append(keep)
-        for i in range(3):
-            product = dot(ordered[group], weights[:, lanes_of(i)])
-            fields[group, lanes_of(i)] = product.astype(BF16)
+        queries = dot(ordered[group], weights[...]).astype(BF16)
+        sides[first : first + GROUP, :all_frames] = queries.reshape(GROUP, all_frames, channels)
 
     def pair_products(p):
-        here = rows_of(p)
-        scores[p] = dot(fields[here, lanes_of(1)], fields[here, lanes_of(0)], (1, 1))
-        grad_probs[p] = dot(fields[here, lanes_of(2)], grads[p], (1, 1))
+        products[p] = dot(ordered[rows_of(p)], sides[p], (1, 1))
 
     def softmax(p):
-        logits = scores[p] * scale + bias[...]
+        logits = products[p, :, :all_frames] + bias[...]
         expo = jnp.exp(logits - jnp.max(logits, axis=0, keepdims=True))
         probs = expo * (1.0 / jnp.sum(expo, axis=0, keepdims=True))
         low = probs.astype(BF16)
-        probs_low[p] = low
-        grad = grad_probs[p]
+        grad = products[p, :, all_frames:]
         delta = jnp.sum(low.astype(F32) * grad, axis=0, keepdims=True)
-        grad_scores[p] = (probs * (grad - delta) * scale).astype(BF16)
+        mix[p, :, :all_frames] = (probs * (grad - delta)).astype(BF16)
+        mix[p, :, all_frames:] = low
 
     def back_products(p):
         here = rows_of(p)
-        backs[here, lanes_of(0)] = dot(
-            grad_scores[p], fields[here, lanes_of(1)], (0, 0)
-        ).astype(BF16)
-        backs[here, lanes_of(1)] = dot(grad_scores[p], fields[here, lanes_of(0)]).astype(BF16)
-        backs[here, lanes_of(2)] = dot(probs_low[p], grads[p]).astype(BF16)
+        direct[here] = dot(mix[p], sides[p])
+        inner[here] = dot(mix[p, :, :all_frames], ordered[here], (0, 0)).astype(BF16)
 
     def back_group(first):
-        group = slice(first * all_frames, (first + GROUP) * all_frames)
-        total = dot(backs[group], weights[...], (1, 1)).astype(BF16).astype(F32)
+        group = group_of(first)
+        total = dot(inner[group], weights[...], (1, 1)) + direct[group]
+        total = total.astype(BF16).astype(F32)
         for j in range(GROUP):
             part = total[j * all_frames : (j + 1) * all_frames]
             store_position(result, first + j, positions, part)
 
-    for copy in loads[:3]:
-        copy.wait()
+    loads[0].wait()
     project_group(0)
-    loads[3].wait()
+    loads[1].wait()
     for first in range(0, positions, GROUP):
         group = range(first, first + GROUP)
         for p in group:
@@ -408,8 +404,6 @@
     wide = VMEM((channels // LANES, all_frames * positions, LANES), F32)
     flat = VMEM((all_frames * positions, channels), BF16)
     part = VMEM((GROUP * all_frames, channels), BF16)
-    triple = VMEM((all_frames * positions, 3 * channels), BF16)
-    pairs = (all_frames, all_frames)
     chunked = (frames, blocks, positions, channels)
 
     (outgoing,) = call(
@@ -430,22 +424,24 @@
     normed_in = exchange(normed).reshape(spread)
     slot = lax.broadcasted_iota(jnp.int32, (blocks, frames, LANES), 1)
     used = (slot < frame_count[:, None, None]).astype(F32).reshape(all_frames, LANES)
-    (grads,) = call(
-        grads_kernel, [shaped(ordered, BF16)], [ON_CHIP, ON_CHIP, VMEM], [grads_in, used, w_out],
-        [wide, flat], product, 2 * size,
-    )
+    folded, mixed = call(
+        grads_kernel, [shaped(ordered, BF16), shaped((channels, channels), BF16)],
+        [ON_CHIP, ON_CHIP] + [VMEM] * 4, [grads_in, used, w_out, w_query, w_key, w_value],
+        [wide, flat, flat], 2 * product, 2 * size,
+    )
+    pairs = (all_frames, all_frames)
+    double = (positions, 2 * all_frames, channels)
     grad_normed, kept = call(
         attention_kernel,
         [shaped(spread, BF16), shaped((all_frames * positions, channels), BF16)],
-        [ON_CHIP, HBM, ON_CHIP, HBM, HBM, HBM],
-        [normed_in, grads, used, w_query, w_key, w_value],
+        [ON_CHIP, HBM, ON_CHIP, HBM], [normed_in, folded, used, mixed],
         [
-            VMEM(ordered, BF16), VMEM((channels, 3 * channels), BF16), VMEM(pairs, F32), wide, wide,
-            VMEM(spread, BF16), flat, triple, VMEM((positions, *pairs), F32),
-            VMEM((positions, *pairs), F32), VMEM((positions, *pairs), BF16),
-            VMEM((positions, *pairs), BF16), triple, dma((4 + positions // GROUP,)),
+            VMEM((channels, channels), BF16), VMEM(pairs, F32), wide, wide, VMEM(spread, BF16),
+            flat, VMEM(double, BF16), VMEM((positions, all_frames, 2 * all_frames), F32),
+            VMEM((positions, all_frames, 2 * all_frames), BF16), flat,
+            VMEM((all_frames * positions, channels), F32), dma((2 * positions // GROUP,)),
         ],
-        6 * product + 5 * inner, 4 * size, [HBM, HBM],
+        2 * product + 5 * inner, 4 * size, [HBM, HBM],
     )
     grad_home = exchange(grad_normed.reshape(sent))
     (projected,) = call(

time: 156 us -> 155 us (level)
  no operation moved by 1% of the time
where the time goes in v4:
time: 155 us; the launch traced here: 154 us
  waiting for transfers between devices  73.3 us (47%)
  starting transfers between devices  39.7 us (26%)
  Pallas kernels  39 us (25%)
    all_to_all x4, waiting for transfers between devices, exchange(): return lax.all_to_all(blocks, 'tm', split_axis=0, concat_axis=0, tiled=True)  70.8 us
    pallas_call x9, Pallas kernels, call(): pl.pallas_call(kernel, out_shape=outs, in_specs=specs(*ins), out_specs=sp...  39 us
    all_to_all x4, starting transfers between devices, exchange(): return lax.all_to_all(blocks, 'tm', split_axis=0, concat_axis=0, tiled=True)  28.5 us
    ppermute x2, starting transfers between devices, share_rows(): below = lax.ppermute(head, 'space', [(i + 1, i) for i in range(ends)])  7.28 us
    ppermute x2, starting transfers between devices, share_rows(): above = lax.ppermute(tail, 'space', [(i, i + 1) for i in range(ends)])  3.83 us
  transfers between devices with their start and end apart: 8, of which 6 were waited for; matrix products, arithmetic and copies ran while one was open for 0% of the time, Pallas kernels for 16%

profile of v4, /device:TPU:10, one launch (start us, length us, event | category | flops | bytes accessed | tf_op | source)
XLA Modules:
  0.0 154.0 jit_solution(3226190532220586614)
XLA Ops:
  0.6 2.0 %shard_map.106 = bf16[32,4,16,256]{3,2,1,0:T(8,128)(2,1)} custom-call(bf16[4,32,16,256]{3,2,1,0:T(8,128)(2,1)} %bitcast.7), custom_call_target="tpu_custom_call" | custom-call | bytes 1048576 | tf_op jit(solution)/shard_map/pallas_call | solution.py:394
  2.6 11.7 %all-to-all-start.1 = ((bf16[32,4,16,256]{3,2,1,0:T(8,128)(2,1)}), bf16[32,4,16,256]{3,2,1,0:T(8,128)(2,1)S(1)}, u32[]{:S(2)}, u32[]{:S(2)}) async-start(bf16[32,4,16,256]{3,2,1,0:T(8,128)(2,1)} %shard_map.106), calls=%async_computation.1 | async-start | bytes 2097152 | tf_op jit(solution)/shard_map/all_to_all | solution.py:369
  14.4 1.7 %shard_map.104 = (bf16[4,64,256]{2,1,0:T(8,128)(2,1)S(1)}, bf16[4,64,256]{2,1,0:T(8,128)(2,1)S(1)}) custom-call(s32[8]{0:T(128)} %row_count.9, bf16[4,8,64,256]{3,2,1,0:T(8,128)(2,1)} %field.3), custom_call_target="tpu_custom_call" | custom-call | bytes 262144 | tf_op jit(solution)/shard_map/pallas_call | solution.py:394
  16.0 1.9 %collective-permute-start = (bf16[4,64,256]{2,1,0:T(8,128)(2,1)S(1)}, bf16[4,64,256]{2,1,0:T(8,128)(2,1)S(1)}, u32[]{:S(2)}, u32[]{:S(2)}) collective-permute-start(bf16[4,64,256]{2,1,0:T(8,128)(2,1)S(1)} %get-tuple-element.13), channel_id=1, source_target_pairs={{0,1},{1,2},{2,3},{3,4},{4,5},{5,6},{6,7},{8,9},{9,10},{10,11},{11... | collective-permute-start | bytes 393224 | tf_op jit(solution)/shard_map/ppermute | solution.py:363
  18.0 3.6 %collective-permute-start.1 = (bf16[4,64,256]{2,1,0:T(8,128)(2,1)S(1)}, bf16[4,64,256]{2,1,0:T(8,128)(2,1)S(1)}, u32[]{:S(2)}, u32[]{:S(2)}) collective-permute-start(bf16[4,64,256]{2,1,0:T(8,128)(2,1)S(1)} %get-tuple-element.14), channel_id=1, source_target_pairs={{1,0},{2,1},{3,2},{4,3},{5,4},{6,5},{7,6},{9,8},{10,9},{11,10},{12... | collective-permute-start | bytes 393224 | tf_op jit(solution)/shard_map/ppermute | solution.py:364
  21.6 0.7 collective-permute-done.above
  22.3 1.8 %collective-permute-done.1.below = bf16[4,64,256]{2,1,0:T(8,128)(2,1)S(1)} collective-permute-done((bf16[4,64,256]{2,1,0:T(8,128)(2,1)S(1)}, bf16[4,64,256]{2,1,0:T(8,128)(2,1)S(1)}, u32[]{:S(2)}, u32[]{:S(2)}) %collective-permute-start.1) | collective-permute-done | bytes 131104 | tf_op jit(solution)/shard_map/ppermute | solution.py:364
  24.1 6.7 %shard_map.105 = (bf16[32,4,16,256]{3,2,1,0:T(8,128)(2,1)}, bf16[32,4,16,256]{3,2,1,0:T(8,128)(2,1)}) custom-call(s32[32]{0:T(128)} %frame_count.7, s32[8]{0:T(128)} %row_count.9, bf16[4,8,64,256]{3,2,1,0:T(8,128)(2,1)} %field.3, bf16[4,64,256]{2,1,0:T(8,128)(2,1)S(1)} %collective-permute-done.above, bf16[4,64,256]{2,1,0:T(8,128)(2,1)S(1)} %collective-permute-done.1.below, ...), custom_call_target="tpu_custom_call" | custom-call | flops 2415919104 | bytes 4194304 | tf_op jit(solution)/shard_map/pallas_call | solution.py:394
  30.8 0.0 copy-start.3
  30.8 11.6 %all-to-all-done.1 = bf16[32,4,16,256]{3,2,1,0:T(8,128)(2,1)S(1)} async-done(((bf16[32,4,16,256]{3,2,1,0:T(8,128)(2,1)}), bf16[32,4,16,256]{3,2,1,0:T(8,128)(2,1)S(1)}, u32[]{:S(2)}, u32[]{:S(2)}) %all-to-all-start.1) | async-done | bytes 1048608 | tf_op jit(solution)/shard_map/all_to_all | solution.py:369
  42.4 5.6 %all-to-all-start = ((bf16[32,4,16,256]{3,2,1,0:T(8,128)(2,1)}), bf16[32,4,16,256]{3,2,1,0:T(8,128)(2,1)S(1)}, u32[]{:S(2)}, u32[]{:S(2)}) async-start(bf16[32,4,16,256]{3,2,1,0:T(8,128)(2,1)} %get-tuple-element.16), calls=%async_computation | async-start | bytes 2097152 | tf_op jit(solution)/shard_map/all_to_all | solution.py:369
  48.0 0.0 copy-done.3
  48.0 0.1 fusion
  48.1 0.1 reshape.31
  48.2 0.1 iota.10.used
  48.3 3.5 %shard_map.107 = (bf16[16,128,256]{2,1,0:T(8,128)(2,1)}, bf16[256,256]{1,0:T(8,128)(2,1)}) custom-call(bf16[128,16,256]{2,1,0:T(8,128)(2,1)S(1)} %bitcast.5, f32[128,128]{1,0:T(8,128)S(1)} %iota.10.used, bf16[256,256]{1,0:T(8,128)(2,1)} %w_out.3, bf16[256,256]{1,0:T(8,128)(2,1)} %w_query.3, bf16[256,256]{1,0:T(8,128)(2,1)} %w_key.3, bf16[256,256]{1,0:T(8,128)(2,1)} %w_value.3), custom_call_target="tpu_custom_call" | custom-call | flops 536870912 | bytes 2097152 | tf_op jit(solution)/shard_map/pallas_call | solution.py:394
  51.7 23.3 %all-to-all-done = bf16[32,4,16,256]{3,2,1,0:T(8,128)(2,1)S(1)} async-done(((bf16[32,4,16,256]{3,2,1,0:T(8,128)(2,1)}), bf16[32,4,16,256]{3,2,1,0:T(8,128)(2,1)S(1)}, u32[]{:S(2)}, u32[]{:S(2)}) %all-to-all-start) | async-done | bytes 1048608 | tf_op jit(solution)/shard_map/all_to_all | solution.py:369
  75.0 5.8 %shard_map.108 = (bf16[128,16,256]{2,1,0:T(8,128)(2,1)}, bf16[2048,256]{1,0:T(8,128)(2,1)}) custom-call(bf16[128,16,256]{2,1,0:T(8,128)(2,1)S(1)} %bitcast.6, bf16[16,128,256]{2,1,0:T(8,128)(2,1)} %get-tuple-element.17.folded, f32[128,128]{1,0:T(8,128)S(1)} %iota.10.used, bf16[256,256]{1,0:T(8,128)(2,1)} %get-tuple-element.18.mixed), custom_call_target="tpu_custom_call" | custom-call | flops 1207959552 | bytes 4194304 | tf_op jit(solution)/shard_map/pallas_call | solution.py:394
  80.8 5.6 %all-to-all-start.3 = ((bf16[32,4,16,256]{3,2,1,0:T(8,128)(2,1)}), bf16[32,4,16,256]{3,2,1,0:T(8,128)(2,1)S(1)}, u32[]{:S(2)}, u32[]{:S(2)}) async-start(bf16[32,4,16,256]{3,2,1,0:T(8,128)(2,1)} %bitcast.9), calls=%async_computation.3 | async-start | bytes 2097152 | tf_op jit(solution)/shard_map/all_to_all | solution.py:369
  86.4 7.6 %shard_map.109 = bf16[128,16,256]{2,1,0:T(8,128)(2,1)} custom-call(bf16[2048,256]{1,0:T(8,128)(2,1)} %get-tuple-element.19.ordered, f32[128,128]{1,0:T(8,128)S(1)} %iota.10.used, bf16[256,256]{1,0:T(8,128)(2,1)} %w_query.3, bf16[256,256]{1,0:T(8,128)(2,1)} %w_key.3, bf16[256,256]{1,0:T(8,128)(2,1)} %w_value.3, bf16[256,256]{1,0:T(8,128)(2,1)} %w_out.3), custom_call_target="tpu_custom_call" | custom-call | flops 1342177280 | bytes 2097152 | tf_op jit(solution)/shard_map/pallas_call | solution.py:394
  94.0 19.0 %all-to-all-done.3.grad_normed = bf16[32,4,16,256]{3,2,1,0:T(8,128)(2,1)S(1)} async-done(((bf16[32,4,16,256]{3,2,1,0:T(8,128)(2,1)}), bf16[32,4,16,256]{3,2,1,0:T(8,128)(2,1)S(1)}, u32[]{:S(2)}, u32[]{:S(2)}) %all-to-all-start.3) | async-done | bytes 1048608 | tf_op jit(solution)/shard_map/all_to_all | solution.py:369
  113.0 0.0 copy-start.1
  113.0 1.0 copy-done.1
  114.0 0.0 copy-start.2
  114.0 5.7 %all-to-all-start.2 = ((bf16[32,4,16,256]{3,2,1,0:T(8,128)(2,1)}), bf16[32,4,16,256]{3,2,1,0:T(8,128)(2,1)S(1)}, u32[]{:S(2)}, u32[]{:S(2)}) async-start(bf16[32,4,16,256]{3,2,1,0:T(8,128)(2,1)} %bitcast.8), calls=%async_computation.2 | async-start | bytes 2097152 | tf_op jit(solution)/shard_map/all_to_all | solution.py:369
  119.7 0.0 copy-done.2
  119.7 0.0 copy-start
  119.7 4.0 %shard_map.111 = (bf16[4,8,64,256]{3,2,1,0:T(8,128)(2,1)}, bf16[4,64,256]{2,1,0:T(8,128)(2,1)}, bf16[4,64,256]{2,1,0:T(8,128)(2,1)}) custom-call(s32[32]{0:T(128)} %frame_count.7, s32[8]{0:T(128)} %row_count.9, bf16[4,8,64,256]{3,2,1,0:T(8,128)(2,1)} %cotangent.1, bf16[32,4,16,256]{3,2,1,0:T(8,128)(2,1)} %get-tuple-element.15.hidden, ...), custom_call_target="tpu_custom_call" | custom-call | bytes 5242880 | tf_op jit(solution)/shard_map/pallas_call | solution.py:394
  123.7 1.9 %collective-permute-start.2 = (bf16[4,64,256]{2,1,0:T(8,128)(2,1)}, bf16[4,64,256]{2,1,0:T(8,128)(2,1)S(1)}, u32[]{:S(2)}, u32[]{:S(2)}) collective-permute-start(bf16[4,64,256]{2,1,0:T(8,128)(2,1)} %get-tuple-element.22), channel_id=1, source_target_pairs={{0,1},{1,2},{2,3},{3,4},{4,5},{5,6},{6,7},{8,9},{9,10},{10,11},{11... | collective-permute-start | bytes 393224 | tf_op jit(solution)/shard_map/ppermute | solution.py:363
  125.6 3.6 %collective-permute-start.3 = (bf16[4,64,256]{2,1,0:T(8,128)(2,1)}, bf16[4,64,256]{2,1,0:T(8,128)(2,1)S(1)}, u32[]{:S(2)}, u32[]{:S(2)}) collective-permute-start(bf16[4,64,256]{2,1,0:T(8,128)(2,1)} %get-tuple-element.23), channel_id=1, source_target_pairs={{1,0},{2,1},{3,2},{4,3},{5,4},{6,5},{7,6},{9,8},{10,9},{11,10},{12... | collective-permute-start | bytes 393224 | tf_op jit(solution)/shard_map/ppermute | solution.py:364
  129.3 16.9 %all-to-all-done.2.projected = bf16[32,4,16,256]{3,2,1,0:T(8,128)(2,1)S(1)} async-done(((bf16[32,4,16,256]{3,2,1,0:T(8,128)(2,1)}), bf16[32,4,16,256]{3,2,1,0:T(8,128)(2,1)S(1)}, u32[]{:S(2)}, u32[]{:S(2)}) %all-to-all-start.2) | async-done | bytes 1048608 | tf_op jit(solution)/shard_map/all_to_all | solution.py:369
  146.2 0.0 copy-done
  146.2 1.8 %shard_map.110 = bf16[4,8,64,256]{3,2,1,0:T(8,128)(2,1)} custom-call(s32[32]{0:T(128)} %frame_count.7, s32[8]{0:T(128)} %row_count.9, bf16[32,4,16,256]{3,2,1,0:T(8,128)(2,1)S(1)} %copy-done, bf16[32,4,16,256]{3,2,1,0:T(8,128)(2,1)S(1)} %all-to-all-done.2.projected), custom_call_target="tpu_custom_call" | custom-call | bytes 3145728 | tf_op jit(solution)/shard_map/pallas_call | solution.py:394
  148.0 0.0 collective-permute-done.2.above
  148.0 0.0 collective-permute-done.3.below
  148.0 6.0 %shard_map.112 = bf16[4,8,64,256]{3,2,1,0:T(8,128)(2,1)} custom-call(s32[32]{0:T(128)} %frame_count.7, s32[8]{0:T(128)} %row_count.9, bf16[4,8,64,256]{3,2,1,0:T(8,128)(2,1)} %get-tuple-element.21.field, bf16[4,64,256]{2,1,0:T(8,128)(2,1)S(1)} %collective-permute-done.2.above, bf16[4,64,256]{2,1,0:T(8,128)(2,1)S(1)} %collective-permute-done.3.below, ...), custom_call_target="tpu_custom_call" | custom-call | flops 2415919104 | bytes 3145728 | tf_op jit(solution)/shard_map/pallas_call | solution.py:394
Async XLA Ops:
  2.6 39.8 %all-to-all-start.1 = ((bf16[32,4,16,256]{3,2,1,0:T(8,128)(2,1)}), bf16[32,4,16,256]{3,2,1,0:T(8,128)(2,1)S(1)}, u32[]{:S(2)}, u32[]{:S(2)}) async-start(bf16[32,4,16,256]{3,2,1,0:T(8,128)(2,1)} %shard_map.106), calls=%async_computation.1 | async-start | bytes 2097152 | tf_op jit(solution)/shard_map/all_to_all | solution.py:369
  16.0 6.3 %collective-permute-start = (bf16[4,64,256]{2,1,0:T(8,128)(2,1)S(1)}, bf16[4,64,256]{2,1,0:T(8,128)(2,1)S(1)}, u32[]{:S(2)}, u32[]{:S(2)}) collective-permute-start(bf16[4,64,256]{2,1,0:T(8,128)(2,1)S(1)} %get-tuple-element.13), channel_id=1, source_target_pairs={{0,1},{1,2},{2,3},{3,4},{4,5},{5,6},{6,7},{8,9},{9,10},{10,11},{11... | collective-permute-start | bytes 393224 | tf_op jit(solution)/shard_map/ppermute | solution.py:363
  18.0 6.1 %collective-permute-start.1 = (bf16[4,64,256]{2,1,0:T(8,128)(2,1)S(1)}, bf16[4,64,256]{2,1,0:T(8,128)(2,1)S(1)}, u32[]{:S(2)}, u32[]{:S(2)}) collective-permute-start(bf16[4,64,256]{2,1,0:T(8,128)(2,1)S(1)} %get-tuple-element.14), channel_id=1, source_target_pairs={{1,0},{2,1},{3,2},{4,3},{5,4},{6,5},{7,6},{9,8},{10,9},{11,10},{12... | collective-permute-start | bytes 393224 | tf_op jit(solution)/shard_map/ppermute | solution.py:364
  30.8 17.2 %copy-start.3 = (s32[32]{0:T(128)S(1)}, s32[32]{0:T(128)}, u32[]{:S(2)}) copy-start(s32[32]{0:T(128)} %frame_count.7) | copy-start | bytes 388
  42.4 32.6 %all-to-all-start = ((bf16[32,4,16,256]{3,2,1,0:T(8,128)(2,1)}), bf16[32,4,16,256]{3,2,1,0:T(8,128)(2,1)S(1)}, u32[]{:S(2)}, u32[]{:S(2)}) async-start(bf16[32,4,16,256]{3,2,1,0:T(8,128)(2,1)} %get-tuple-element.16), calls=%async_computation | async-start | bytes 2097152 | tf_op jit(solution)/shard_map/all_to_all | solution.py:369
  80.8 32.2 %all-to-all-start.3 = ((bf16[32,4,16,256]{3,2,1,0:T(8,128)(2,1)}), bf16[32,4,16,256]{3,2,1,0:T(8,128)(2,1)S(1)}, u32[]{:S(2)}, u32[]{:S(2)}) async-start(bf16[32,4,16,256]{3,2,1,0:T(8,128)(2,1)} %bitcast.9), calls=%async_computation.3 | async-start | bytes 2097152 | tf_op jit(solution)/shard_map/all_to_all | solution.py:369
  113.0 1.0 copy-start.1
  114.0 5.7 %copy-start.2 = (bf16[32,4,16,256]{3,2,1,0:T(8,128)(2,1)S(1)}, bf16[32,4,16,256]{3,2,1,0:T(8,128)(2,1)}, u32[]{:S(2)}) copy-start(bf16[32,4,16,256]{3,2,1,0:T(8,128)(2,1)} %copy-done.1) | copy-start | bytes 3145732
  114.0 32.2 %all-to-all-start.2 = ((bf16[32,4,16,256]{3,2,1,0:T(8,128)(2,1)}), bf16[32,4,16,256]{3,2,1,0:T(8,128)(2,1)S(1)}, u32[]{:S(2)}, u32[]{:S(2)}) async-start(bf16[32,4,16,256]{3,2,1,0:T(8,128)(2,1)} %bitcast.8), calls=%async_computation.2 | async-start | bytes 2097152 | tf_op jit(solution)/shard_map/all_to_all | solution.py:369
  119.7 26.5 %copy-start = (bf16[32,4,16,256]{3,2,1,0:T(8,128)(2,1)S(1)}, bf16[32,4,16,256]{3,2,1,0:T(8,128)(2,1)}, u32[]{:S(2)}) copy-start(bf16[32,4,16,256]{3,2,1,0:T(8,128)(2,1)} %get-tuple-element.15.hidden) | copy-start | bytes 3145732
  123.7 24.3 %collective-permute-start.2 = (bf16[4,64,256]{2,1,0:T(8,128)(2,1)}, bf16[4,64,256]{2,1,0:T(8,128)(2,1)S(1)}, u32[]{:S(2)}, u32[]{:S(2)}) collective-permute-start(bf16[4,64,256]{2,1,0:T(8,128)(2,1)} %get-tuple-element.22), channel_id=1, source_target_pairs={{0,1},{1,2},{2,3},{3,4},{4,5},{5,6},{6,7},{8,9},{9,10},{10,11},{11... | collective-permute-start | bytes 393224 | tf_op jit(solution)/shard_map/ppermute | solution.py:363
  125.6 22.4 %collective-permute-start.3 = (bf16[4,64,256]{2,1,0:T(8,128)(2,1)}, bf16[4,64,256]{2,1,0:T(8,128)(2,1)S(1)}, u32[]{:S(2)}, u32[]{:S(2)}) collective-permute-start(bf16[4,64,256]{2,1,0:T(8,128)(2,1)} %get-tuple-element.23), channel_id=1, source_target_pairs={{1,0},{2,1},{3,2},{4,3},{5,4},{6,5},{7,6},{9,8},{10,9},{11,10},{12... | collective-permute-start | bytes 393224 | tf_op jit(solution)/shard_map/ppermute | solution.py:364

commit v5 on v4

--- a/solution.py
+++ b/solution.py
@@ -10,6 +10,7 @@
 F32 = jnp.float32
 GROUP = 4
 LANES = 128
+TILE = 16
 VMEM = pltpu.VMEM
 SMEM = pltpu.SMEM
 HBM = pltpu.HBM
@@ -121,24 +122,6 @@
         spread[h] = part.reshape(spread.shape[1], LANES)
 
 
-def narrow(spread, held, target, sems):
-    frames, positions, _ = held.shape
-    pieces = 4
-    size = frames // pieces
-    copies = []
-    for i in range(pieces):
-        here = slice(i * size, (i + 1) * size)
-        for h in range(spread.shape[0]):
-            part = spread[h, i * size * positions : (i + 1) * size * positions]
-            part = part.reshape(size, positions, LANES)
-            held[here, :, h * LANES : (h + 1) * LANES] = part.astype(BF16)
-        copy = pltpu.make_async_copy(held.at[here], target.at[here], sems.at[i])
-        copy.start()
-        copies.append(copy)
-    for copy in copies:
-        copy.wait()
-
-
 def send_kernel(field, out, held, sems):
     frames = field.shape[0]
     arrive = [
@@ -187,7 +170,7 @@
 
 def attention_kernel(
     normed, folded, used, mixed, grad_normed, kept,
-    weights, bias, spread, result, out, ordered, sides, products, mix, inner, direct, sems,
+    weights, bias, result, out, ordered, sides, products, mix, inner, direct, sems,
 ):
     all_frames, positions, channels = normed.shape
     pieces = positions // GROUP
@@ -197,9 +180,11 @@
     ]
     for copy in loads:
         copy.start()
-    widen(normed, spread)
+    for f in range(0, all_frames, TILE):
+        ordered[:, f : f + TILE] = jnp.transpose(normed[f : f + TILE], (1, 0, 2))
     bias[...] = jnp.where(allowed_pairs(used), 0.0, -1e30)
-    keeps = []
+    keep = pltpu.make_async_copy(ordered, kept, sems.at[2 * pieces - 1])
+    keep.start()
 
     def rows_of(p):
         return slice(p * all_frames, (p + 1) * all_frames)
@@ -208,19 +193,12 @@
         return slice(first * all_frames, (first + GROUP) * all_frames)
 
     def project_group(first):
-        group = group_of(first)
-        for p in range(first, first + GROUP):
-            ordered[rows_of(p)] = load_position(spread, p, positions)
-        keep = pltpu.make_async_copy(
-            ordered.at[group], kept.at[group], sems.at[pieces + first // GROUP]
-        )
-        keep.start()
-        keeps.append(keep)
-        queries = dot(ordered[group], weights[...]).astype(BF16)
+        rows = ordered[first : first + GROUP].reshape(GROUP * all_frames, channels)
+        queries = dot(rows, weights[...]).astype(BF16)
         sides[first : first + GROUP, :all_frames] = queries.reshape(GROUP, all_frames, channels)
 
     def pair_products(p):
-        products[p] = dot(ordered[rows_of(p)], sides[p], (1, 1))
+        products[p] = dot(ordered[p], sides[p], (1, 1))
 
     def softmax(p):
         logits = products[p, :, :all_frames] + bias[...]
@@ -235,15 +213,12 @@
     def back_products(p):
         here = rows_of(p)
         direct[here] = dot(mix[p], sides[p])
-        inner[here] = dot(mix[p, :, :all_frames], ordered[here], (0, 0)).astype(BF16)
+        inner[here] = dot(mix[p, :, :all_frames], ordered[p], (0, 0)).astype(BF16)
 
     def back_group(first):
         group = group_of(first)
         total = dot(inner[group], weights[...], (1, 1)) + direct[group]
-        total = total.astype(BF16).astype(F32)
-        for j in range(GROUP):
-            part = total[j * all_frames : (j + 1) * all_frames]
-            store_position(result, first + j, positions, part)
+        result[first : first + GROUP] = total.astype(BF16).reshape(GROUP, all_frames, channels)
 
     loads[0].wait()
     project_group(0)
@@ -252,17 +227,27 @@
         group = range(first, first + GROUP)
         for p in group:
             pair_products(p)
+            if first > 0:
+                back_products(p - GROUP)
         if first + GROUP < positions:
             project_group(first + GROUP)
-        for p in group:
-            softmax(p)
         if first > 0:
             back_group(first - GROUP)
         for p in group:
-            back_products(p)
+            softmax(p)
+    for p in range(positions - GROUP, positions):
+        back_products(p)
     back_group(positions - GROUP)
-    narrow(result, out, grad_normed, sems)
-    for copy in keeps:
+    copies = []
+    size = all_frames // pieces
+    for i in range(pieces):
+        for f in range(i * size, (i + 1) * size, TILE):
+            out[f : f + TILE] = jnp.transpose(result[:, f : f + TILE], (1, 0, 2))
+        here = slice(i * size, (i + 1) * size)
+        copy = pltpu.make_async_copy(out.at[here], grad_normed.at[here], sems.at[i])
+        copy.start()
+        copies.append(copy)
+    for copy in copies + [keep]:
         copy.wait()
 
 
@@ -433,11 +418,11 @@
     double = (positions, 2 * all_frames, channels)
     grad_normed, kept = call(
         attention_kernel,
-        [shaped(spread, BF16), shaped((all_frames * positions, channels), BF16)],
+        [shaped(spread, BF16), shaped(ordered, BF16)],
         [ON_CHIP, HBM, ON_CHIP, HBM], [normed_in, folded, used, mixed],
         [
-            VMEM((channels, channels), BF16), VMEM(pairs, F32), wide, wide, VMEM(spread, BF16),
-            flat, VMEM(double, BF16), VMEM((positions, all_frames, 2 * all_frames), F32),
+            VMEM((channels, channels), BF16), VMEM(pairs, F32), VMEM(ordered, BF16), VMEM(spread, BF16),
+            VMEM(ordered, BF16), VMEM(double, BF16), VMEM((positions, all_frames, 2 * all_frames), F32),
             VMEM((positions, all_frames, 2 * all_frames), BF16), flat,
             VMEM((all_frames * positions, channels), F32), dma((2 * positions // GROUP,)),
         ],
@@ -446,7 +431,7 @@
     grad_home = exchange(grad_normed.reshape(sent))
     (projected,) = call(
         project_kernel, [shaped(spread, BF16)], [VMEM, ON_CHIP] + [VMEM] * 4,
-        [kept, used, w_query, w_key, w_value, w_out],
+        [kept.reshape(all_frames * positions, channels), used, w_query, w_key, w_value, w_out],
         [wide] + [part] * 4, 4 * product + 2 * inner, 2 * size,
     )
     projected_home = exchange(projected.reshape(sent))

time: 155 us -> 154 us (level)
  no operation moved by 1% of the time
where the time goes in v5:
time: 154 us; the launch traced here: 153 us
  waiting for transfers between devices  73.3 us (48%)
  starting transfers between devices  39.7 us (26%)
  Pallas kernels  38.1 us (25%)
    all_to_all x4, waiting for transfers between devices, exchange(): return lax.all_to_all(blocks, 'tm', split_axis=0, concat_axis=0, tiled=True)  70.8 us
    pallas_call x9, Pallas kernels, call(): pl.pallas_call(kernel, out_shape=outs, in_specs=specs(*ins), out_specs=sp...  38.1 us
    all_to_all x4, starting transfers between devices, exchange(): return lax.all_to_all(blocks, 'tm', split_axis=0, concat_axis=0, tiled=True)  28.5 us
    ppermute x2, starting transfers between devices, share_rows(): below = lax.ppermute(head, 'space', [(i + 1, i) for i in range(ends)])  7.28 us
    ppermute x2, starting transfers between devices, share_rows(): above = lax.ppermute(tail, 'space', [(i, i + 1) for i in range(ends)])  3.83 us
  transfers between devices with their start and end apart: 8, of which 6 were waited for; matrix products, arithmetic and copies ran while one was open for 0% of the time, Pallas kernels for 16%

profile of v5, /device:TPU:10, one launch (start us, length us, event | category | flops | bytes accessed | tf_op | source)
XLA Modules:
  0.0 153.1 jit_solution(9192278924623828002)
XLA Ops:
  0.6 2.0 %shard_map.106 = bf16[32,4,16,256]{3,2,1,0:T(8,128)(2,1)} custom-call(bf16[4,32,16,256]{3,2,1,0:T(8,128)(2,1)} %bitcast.8), custom_call_target="tpu_custom_call" | custom-call | bytes 1048576 | tf_op jit(solution)/shard_map/pallas_call | solution.py:379
  2.6 11.7 %all-to-all-start.1 = ((bf16[32,4,16,256]{3,2,1,0:T(8,128)(2,1)}), bf16[32,4,16,256]{3,2,1,0:T(8,128)(2,1)S(1)}, u32[]{:S(2)}, u32[]{:S(2)}) async-start(bf16[32,4,16,256]{3,2,1,0:T(8,128)(2,1)} %shard_map.106), calls=%async_computation.1 | async-start | bytes 2097152 | tf_op jit(solution)/shard_map/all_to_all | solution.py:354
  14.4 1.7 %shard_map.104 = (bf16[4,64,256]{2,1,0:T(8,128)(2,1)S(1)}, bf16[4,64,256]{2,1,0:T(8,128)(2,1)S(1)}) custom-call(s32[8]{0:T(128)} %row_count.9, bf16[4,8,64,256]{3,2,1,0:T(8,128)(2,1)} %field.3), custom_call_target="tpu_custom_call" | custom-call | bytes 262144 | tf_op jit(solution)/shard_map/pallas_call | solution.py:379
  16.0 1.9 %collective-permute-start = (bf16[4,64,256]{2,1,0:T(8,128)(2,1)S(1)}, bf16[4,64,256]{2,1,0:T(8,128)(2,1)S(1)}, u32[]{:S(2)}, u32[]{:S(2)}) collective-permute-start(bf16[4,64,256]{2,1,0:T(8,128)(2,1)S(1)} %get-tuple-element.13), channel_id=1, source_target_pairs={{0,1},{1,2},{2,3},{3,4},{4,5},{5,6},{6,7},{8,9},{9,10},{10,11},{11... | collective-permute-start | bytes 393224 | tf_op jit(solution)/shard_map/ppermute | solution.py:348
  18.0 3.6 %collective-permute-start.1 = (bf16[4,64,256]{2,1,0:T(8,128)(2,1)S(1)}, bf16[4,64,256]{2,1,0:T(8,128)(2,1)S(1)}, u32[]{:S(2)}, u32[]{:S(2)}) collective-permute-start(bf16[4,64,256]{2,1,0:T(8,128)(2,1)S(1)} %get-tuple-element.14), channel_id=1, source_target_pairs={{1,0},{2,1},{3,2},{4,3},{5,4},{6,5},{7,6},{9,8},{10,9},{11,10},{12... | collective-permute-start | bytes 393224 | tf_op jit(solution)/shard_map/ppermute | solution.py:349
  21.6 0.7 collective-permute-done.above
  22.3 1.8 %collective-permute-done.1.below = bf16[4,64,256]{2,1,0:T(8,128)(2,1)S(1)} collective-permute-done((bf16[4,64,256]{2,1,0:T(8,128)(2,1)S(1)}, bf16[4,64,256]{2,1,0:T(8,128)(2,1)S(1)}, u32[]{:S(2)}, u32[]{:S(2)}) %collective-permute-start.1) | collective-permute-done | bytes 131104 | tf_op jit(solution)/shard_map/ppermute | solution.py:349
  24.1 6.7 %shard_map.105 = (bf16[32,4,16,256]{3,2,1,0:T(8,128)(2,1)}, bf16[32,4,16,256]{3,2,1,0:T(8,128)(2,1)}) custom-call(s32[32]{0:T(128)} %frame_count.7, s32[8]{0:T(128)} %row_count.9, bf16[4,8,64,256]{3,2,1,0:T(8,128)(2,1)} %field.3, bf16[4,64,256]{2,1,0:T(8,128)(2,1)S(1)} %collective-permute-done.above, bf16[4,64,256]{2,1,0:T(8,128)(2,1)S(1)} %collective-permute-done.1.below, ...), custom_call_target="tpu_custom_call" | custom-call | flops 2415919104 | bytes 4194304 | tf_op jit(solution)/shard_map/pallas_call | solution.py:379
  30.8 0.0 copy-start.3
  30.8 11.6 %all-to-all-done.1 = bf16[32,4,16,256]{3,2,1,0:T(8,128)(2,1)S(1)} async-done(((bf16[32,4,16,256]{3,2,1,0:T(8,128)(2,1)}), bf16[32,4,16,256]{3,2,1,0:T(8,128)(2,1)S(1)}, u32[]{:S(2)}, u32[]{:S(2)}) %all-to-all-start.1) | async-done | bytes 1048608 | tf_op jit(solution)/shard_map/all_to_all | solution.py:354
  42.4 5.6 %all-to-all-start = ((bf16[32,4,16,256]{3,2,1,0:T(8,128)(2,1)}), bf16[32,4,16,256]{3,2,1,0:T(8,128)(2,1)S(1)}, u32[]{:S(2)}, u32[]{:S(2)}) async-start(bf16[32,4,16,256]{3,2,1,0:T(8,128)(2,1)} %get-tuple-element.16), calls=%async_computation | async-start | bytes 2097152 | tf_op jit(solution)/shard_map/all_to_all | solution.py:354
  48.0 0.0 copy-done.3
  48.0 0.1 fusion
  48.1 0.1 reshape.35
  48.2 0.1 iota.10.used
  48.3 3.5 %shard_map.107 = (bf16[16,128,256]{2,1,0:T(8,128)(2,1)}, bf16[256,256]{1,0:T(8,128)(2,1)}) custom-call(bf16[128,16,256]{2,1,0:T(8,128)(2,1)S(1)} %bitcast.6, f32[128,128]{1,0:T(8,128)S(1)} %iota.10.used, bf16[256,256]{1,0:T(8,128)(2,1)} %w_out.3, bf16[256,256]{1,0:T(8,128)(2,1)} %w_query.3, bf16[256,256]{1,0:T(8,128)(2,1)} %w_key.3, bf16[256,256]{1,0:T(8,128)(2,1)} %w_value.3), custom_call_target="tpu_custom_call" | custom-call | flops 536870912 | bytes 2097152 | tf_op jit(solution)/shard_map/pallas_call | solution.py:379
  51.7 23.3 %all-to-all-done = bf16[32,4,16,256]{3,2,1,0:T(8,128)(2,1)S(1)} async-done(((bf16[32,4,16,256]{3,2,1,0:T(8,128)(2,1)}), bf16[32,4,16,256]{3,2,1,0:T(8,128)(2,1)S(1)}, u32[]{:S(2)}, u32[]{:S(2)}) %all-to-all-start) | async-done | bytes 1048608 | tf_op jit(solution)/shard_map/all_to_all | solution.py:354
  75.0 4.9 %shard_map.108 = (bf16[128,16,256]{2,1,0:T(8,128)(2,1)}, bf16[16,128,256]{2,1,0:T(8,128)(2,1)}) custom-call(bf16[128,16,256]{2,1,0:T(8,128)(2,1)S(1)} %bitcast.7, bf16[16,128,256]{2,1,0:T(8,128)(2,1)} %get-tuple-element.17.folded, f32[128,128]{1,0:T(8,128)S(1)} %iota.10.used, bf16[256,256]{1,0:T(8,128)(2,1)} %get-tuple-element.18.mixed), custom_call_target="tpu_custom_call" | custom-call | flops 1207959552 | bytes 4194304 | tf_op jit(solution)/shard_map/pallas_call | solution.py:379
  79.9 5.6 %all-to-all-start.3 = ((bf16[32,4,16,256]{3,2,1,0:T(8,128)(2,1)}), bf16[32,4,16,256]{3,2,1,0:T(8,128)(2,1)S(1)}, u32[]{:S(2)}, u32[]{:S(2)}) async-start(bf16[32,4,16,256]{3,2,1,0:T(8,128)(2,1)} %bitcast.10), calls=%async_computation.3 | async-start | bytes 2097152 | tf_op jit(solution)/shard_map/all_to_all | solution.py:354
  85.5 7.6 %shard_map.109 = bf16[128,16,256]{2,1,0:T(8,128)(2,1)} custom-call(bf16[2048,256]{1,0:T(8,128)(2,1)} %bitcast.11, f32[128,128]{1,0:T(8,128)S(1)} %iota.10.used, bf16[256,256]{1,0:T(8,128)(2,1)} %w_query.3, bf16[256,256]{1,0:T(8,128)(2,1)} %w_key.3, bf16[256,256]{1,0:T(8,128)(2,1)} %w_value.3, bf16[256,256]{1,0:T(8,128)(2,1)} %w_out.3), custom_call_target="tpu_custom_call" | custom-call | flops 1342177280 | bytes 2097152 | tf_op jit(solution)/shard_map/pallas_call | solution.py:379
  93.1 19.0 %all-to-all-done.3.grad_normed = bf16[32,4,16,256]{3,2,1,0:T(8,128)(2,1)S(1)} async-done(((bf16[32,4,16,256]{3,2,1,0:T(8,128)(2,1)}), bf16[32,4,16,256]{3,2,1,0:T(8,128)(2,1)S(1)}, u32[]{:S(2)}, u32[]{:S(2)}) %all-to-all-start.3) | async-done | bytes 1048608 | tf_op jit(solution)/shard_map/all_to_all | solution.py:354
  112.1 0.0 copy-start.1
  112.1 1.0 copy-done.1
  113.1 0.0 copy-start.2
  113.1 5.7 %all-to-all-start.2 = ((bf16[32,4,16,256]{3,2,1,0:T(8,128)(2,1)}), bf16[32,4,16,256]{3,2,1,0:T(8,128)(2,1)S(1)}, u32[]{:S(2)}, u32[]{:S(2)}) async-start(bf16[32,4,16,256]{3,2,1,0:T(8,128)(2,1)} %bitcast.9), calls=%async_computation.2 | async-start | bytes 2097152 | tf_op jit(solution)/shard_map/all_to_all | solution.py:354
  118.8 0.0 copy-done.2
  118.8 0.0 copy-start
  118.8 4.0 %shard_map.111 = (bf16[4,8,64,256]{3,2,1,0:T(8,128)(2,1)}, bf16[4,64,256]{2,1,0:T(8,128)(2,1)}, bf16[4,64,256]{2,1,0:T(8,128)(2,1)}) custom-call(s32[32]{0:T(128)} %frame_count.7, s32[8]{0:T(128)} %row_count.9, bf16[4,8,64,256]{3,2,1,0:T(8,128)(2,1)} %cotangent.1, bf16[32,4,16,256]{3,2,1,0:T(8,128)(2,1)} %get-tuple-element.15.hidden, ...), custom_call_target="tpu_custom_call" | custom-call | bytes 5242880 | tf_op jit(solution)/shard_map/pallas_call | solution.py:379
  122.8 1.9 %collective-permute-start.2 = (bf16[4,64,256]{2,1,0:T(8,128)(2,1)}, bf16[4,64,256]{2,1,0:T(8,128)(2,1)S(1)}, u32[]{:S(2)}, u32[]{:S(2)}) collective-permute-start(bf16[4,64,256]{2,1,0:T(8,128)(2,1)} %get-tuple-element.22), channel_id=1, source_target_pairs={{0,1},{1,2},{2,3},{3,4},{4,5},{5,6},{6,7},{8,9},{9,10},{10,11},{11... | collective-permute-start | bytes 393224 | tf_op jit(solution)/shard_map/ppermute | solution.py:348
  124.7 3.6 %collective-permute-start.3 = (bf16[4,64,256]{2,1,0:T(8,128)(2,1)}, bf16[4,64,256]{2,1,0:T(8,128)(2,1)S(1)}, u32[]{:S(2)}, u32[]{:S(2)}) collective-permute-start(bf16[4,64,256]{2,1,0:T(8,128)(2,1)} %get-tuple-element.23), channel_id=1, source_target_pairs={{1,0},{2,1},{3,2},{4,3},{5,4},{6,5},{7,6},{9,8},{10,9},{11,10},{12... | collective-permute-start | bytes 393224 | tf_op jit(solution)/shard_map/ppermute | solution.py:349
  128.3 16.9 %all-to-all-done.2.projected = bf16[32,4,16,256]{3,2,1,0:T(8,128)(2,1)S(1)} async-done(((bf16[32,4,16,256]{3,2,1,0:T(8,128)(2,1)}), bf16[32,4,16,256]{3,2,1,0:T(8,128)(2,1)S(1)}, u32[]{:S(2)}, u32[]{:S(2)}) %all-to-all-start.2) | async-done | bytes 1048608 | tf_op jit(solution)/shard_map/all_to_all | solution.py:354
  145.3 0.0 copy-done
  145.3 1.8 %shard_map.110 = bf16[4,8,64,256]{3,2,1,0:T(8,128)(2,1)} custom-call(s32[32]{0:T(128)} %frame_count.7, s32[8]{0:T(128)} %row_count.9, bf16[32,4,16,256]{3,2,1,0:T(8,128)(2,1)S(1)} %copy-done, bf16[32,4,16,256]{3,2,1,0:T(8,128)(2,1)S(1)} %all-to-all-done.2.projected), custom_call_target="tpu_custom_call" | custom-call | bytes 3145728 | tf_op jit(solution)/shard_map/pallas_call | solution.py:379
  147.1 0.0 collective-permute-done.2.above
  147.1 0.0 collective-permute-done.3.below
  147.1 6.0 %shard_map.112 = bf16[4,8,64,256]{3,2,1,0:T(8,128)(2,1)} custom-call(s32[32]{0:T(128)} %frame_count.7, s32[8]{0:T(128)} %row_count.9, bf16[4,8,64,256]{3,2,1,0:T(8,128)(2,1)} %get-tuple-element.21.field, bf16[4,64,256]{2,1,0:T(8,128)(2,1)S(1)} %collective-permute-done.2.above, bf16[4,64,256]{2,1,0:T(8,128)(2,1)S(1)} %collective-permute-done.3.below, ...), custom_call_target="tpu_custom_call" | custom-call | flops 2415919104 | bytes 3145728 | tf_op jit(solution)/shard_map/pallas_call | solution.py:379
Async XLA Ops:
  2.6 39.8 %all-to-all-start.1 = ((bf16[32,4,16,256]{3,2,1,0:T(8,128)(2,1)}), bf16[32,4,16,256]{3,2,1,0:T(8,128)(2,1)S(1)}, u32[]{:S(2)}, u32[]{:S(2)}) async-start(bf16[32,4,16,256]{3,2,1,0:T(8,128)(2,1)} %shard_map.106), calls=%async_computation.1 | async-start | bytes 2097152 | tf_op jit(solution)/shard_map/all_to_all | solution.py:354
  16.0 6.3 %collective-permute-start = (bf16[4,64,256]{2,1,0:T(8,128)(2,1)S(1)}, bf16[4,64,256]{2,1,0:T(8,128)(2,1)S(1)}, u32[]{:S(2)}, u32[]{:S(2)}) collective-permute-start(bf16[4,64,256]{2,1,0:T(8,128)(2,1)S(1)} %get-tuple-element.13), channel_id=1, source_target_pairs={{0,1},{1,2},{2,3},{3,4},{4,5},{5,6},{6,7},{8,9},{9,10},{10,11},{11... | collective-permute-start | bytes 393224 | tf_op jit(solution)/shard_map/ppermute | solution.py:348
  18.0 6.1 %collective-permute-start.1 = (bf16[4,64,256]{2,1,0:T(8,128)(2,1)S(1)}, bf16[4,64,256]{2,1,0:T(8,128)(2,1)S(1)}, u32[]{:S(2)}, u32[]{:S(2)}) collective-permute-start(bf16[4,64,256]{2,1,0:T(8,128)(2,1)S(1)} %get-tuple-element.14), channel_id=1, source_target_pairs={{1,0},{2,1},{3,2},{4,3},{5,4},{6,5},{7,6},{9,8},{10,9},{11,10},{12... | collective-permute-start | bytes 393224 | tf_op jit(solution)/shard_map/ppermute | solution.py:349
  30.8 17.2 %copy-start.3 = (s32[32]{0:T(128)S(1)}, s32[32]{0:T(128)}, u32[]{:S(2)}) copy-start(s32[32]{0:T(128)} %frame_count.7) | copy-start | bytes 388
  42.4 32.6 %all-to-all-start = ((bf16[32,4,16,256]{3,2,1,0:T(8,128)(2,1)}), bf16[32,4,16,256]{3,2,1,0:T(8,128)(2,1)S(1)}, u32[]{:S(2)}, u32[]{:S(2)}) async-start(bf16[32,4,16,256]{3,2,1,0:T(8,128)(2,1)} %get-tuple-element.16), calls=%async_computation | async-start | bytes 2097152 | tf_op jit(solution)/shard_map/all_to_all | solution.py:354
  79.9 32.2 %all-to-all-start.3 = ((bf16[32,4,16,256]{3,2,1,0:T(8,128)(2,1)}), bf16[32,4,16,256]{3,2,1,0:T(8,128)(2,1)S(1)}, u32[]{:S(2)}, u32[]{:S(2)}) async-start(bf16[32,4,16,256]{3,2,1,0:T(8,128)(2,1)} %bitcast.10), calls=%async_computation.3 | async-start | bytes 2097152 | tf_op jit(solution)/shard_map/all_to_all | solution.py:354
  112.1 1.0 copy-start.1
  113.1 5.7 %copy-start.2 = (bf16[32,4,16,256]{3,2,1,0:T(8,128)(2,1)S(1)}, bf16[32,4,16,256]{3,2,1,0:T(8,128)(2,1)}, u32[]{:S(2)}) copy-start(bf16[32,4,16,256]{3,2,1,0:T(8,128)(2,1)} %copy-done.1) | copy-start | bytes 3145732
  113.1 32.2 %all-to-all-start.2 = ((bf16[32,4,16,256]{3,2,1,0:T(8,128)(2,1)}), bf16[32,4,16,256]{3,2,1,0:T(8,128)(2,1)S(1)}, u32[]{:S(2)}, u32[]{:S(2)}) async-start(bf16[32,4,16,256]{3,2,1,0:T(8,128)(2,1)} %bitcast.9), calls=%async_computation.2 | async-start | bytes 2097152 | tf_op jit(solution)/shard_map/all_to_all | solution.py:354
  118.8 26.5 %copy-start = (bf16[32,4,16,256]{3,2,1,0:T(8,128)(2,1)S(1)}, bf16[32,4,16,256]{3,2,1,0:T(8,128)(2,1)}, u32[]{:S(2)}) copy-start(bf16[32,4,16,256]{3,2,1,0:T(8,128)(2,1)} %get-tuple-element.15.hidden) | copy-start | bytes 3145732
  122.8 24.3 %collective-permute-start.2 = (bf16[4,64,256]{2,1,0:T(8,128)(2,1)}, bf16[4,64,256]{2,1,0:T(8,128)(2,1)S(1)}, u32[]{:S(2)}, u32[]{:S(2)}) collective-permute-start(bf16[4,64,256]{2,1,0:T(8,128)(2,1)} %get-tuple-element.22), channel_id=1, source_target_pairs={{0,1},{1,2},{2,3},{3,4},{4,5},{5,6},{6,7},{8,9},{9,10},{10,11},{11... | collective-permute-start | bytes 393224 | tf_op jit(solution)/shard_map/ppermute | solution.py:348
  124.7 22.4 %collective-permute-start.3 = (bf16[4,64,256]{2,1,0:T(8,128)(2,1)}, bf16[4,64,256]{2,1,0:T(8,128)(2,1)S(1)}, u32[]{:S(2)}, u32[]{:S(2)}) collective-permute-start(bf16[4,64,256]{2,1,0:T(8,128)(2,1)} %get-tuple-element.23), channel_id=1, source_target_pairs={{1,0},{2,1},{3,2},{4,3},{5,4},{6,5},{7,6},{9,8},{10,9},{11,10},{12... | collective-permute-start | bytes 393224 | tf_op jit(solution)/shard_map/ppermute | solution.py:349

commit v6 on v5

--- a/solution.py
+++ b/solution.py
@@ -11,6 +11,7 @@
 GROUP = 4
 LANES = 128
 TILE = 16
+PIECES = 4
 VMEM = pltpu.VMEM
 SMEM = pltpu.SMEM
 HBM = pltpu.HBM
@@ -123,18 +124,22 @@
 
 
 def send_kernel(field, out, held, sems):
-    frames = field.shape[0]
+    frames, blocks = field.shape[:2]
+    size = blocks // PIECES
+    pieces = [(f, pl.ds(i * size, size), i) for f in range(frames) for i in range(PIECES)]
     arrive = [
-        pltpu.make_async_copy(field.at[f], held.at[f], sems.at[0, f]) for f in range(frames)
+        pltpu.make_async_copy(field.at[f, at], held.at[f, at], sems.at[0, f, i])
+        for f, at, i in pieces
     ]
     leave = [
-        pltpu.make_async_copy(held.at[f], out.at[:, f], sems.at[1, f]) for f in range(frames)
+        pltpu.make_async_copy(held.at[f, at], out.at[at, f], sems.at[1, f, i])
+        for f, at, i in pieces
     ]
     for copy in arrive:
         copy.start()
-    for f in range(frames):
-        arrive[f].wait()
-        leave[f].start()
+    for first, second in zip(arrive, leave):
+        first.wait()
+        second.start()
     for copy in leave:
         copy.wait()
 
@@ -285,17 +290,24 @@
     frames_here = frame_count[lax.axis_index("tm")]
     rows_here = row_count[lax.axis_index("space")]
     frames, slots, columns, channels = encoded.shape
-    tokens = slots * columns
+    half = slots // 2
+    groups = hidden.shape[0] // 2
+    tokens = half * columns
     copies = []
     for frame in range(frames):
-        total = hidden[:, frame].astype(F32) + projected[:, frame].astype(F32)
-        total = total.reshape(tokens, channels)
-        used = token_mask(frame, frames_here, rows_here, columns, total.shape)
-        total = jnp.where(used, total, 0.0).astype(BF16)
-        held[frame] = total.reshape(slots, columns, channels)
-        copy = pltpu.make_async_copy(held.at[frame], encoded.at[frame], sems.at[frame])
-        copy.start()
-        copies.append(copy)
+        for i in range(2):
+            source = slice(i * groups, (i + 1) * groups)
+            rows = slice(i * half, (i + 1) * half)
+            total = hidden[source, frame].astype(F32) + projected[source, frame].astype(F32)
+            total = total.reshape(tokens, channels)
+            used = token_mask(frame, frames_here, rows_here - i * half, columns, total.shape)
+            total = jnp.where(used, total, 0.0).astype(BF16)
+            held[frame, rows] = total.reshape(half, columns, channels)
+            copy = pltpu.make_async_copy(
+                held.at[frame, rows], encoded.at[frame, rows], sems.at[frame, i]
+            )
+            copy.start()
+            copies.append(copy)
     for copy in copies:
         copy.wait()
 
@@ -393,7 +405,7 @@
 
     (outgoing,) = call(
         send_kernel, [shaped(sent, BF16)], [HBM], [cotangent.reshape(chunked)],
-        [VMEM(chunked, BF16), dma((2, frames))], 0, size, [HBM],
+        [VMEM(chunked, BF16), dma((2, frames, PIECES))], 0, size, [HBM],
     )
     grads_in = exchange(outgoing).reshape(spread)
     head, tail = call(
@@ -449,7 +461,7 @@
     (encoded,) = call(
         encode_kernel, [shaped(home, BF16)], [SMEM, SMEM, ON_CHIP, ON_CHIP],
         [frame_count, row_count, hidden, projected_home],
-        [VMEM(home, BF16), dma((frames,))], 0, 3 * size, [HBM],
+        [VMEM(home, BF16), dma((frames, 2))], 0, 3 * size, [HBM],
     )
     return encoded, video_grad
 

time: 154 us -> 154 us (level)
  transfers between devices with their start and end apart: 8 -> 8, of which waited for: 6 -> 6; matrix products, arithmetic and copies ran while one was open for 0% -> 0% of each run, Pallas kernels for 16% -> 17%
where the time goes in v6:
time: 154 us; the launch traced here: 153 us
  waiting for transfers between devices  73.3 us (48%)
  starting transfers between devices  39.7 us (26%)
  Pallas kernels  38.4 us (25%)
    all_to_all x4, waiting for transfers between devices, exchange(): return lax.all_to_all(blocks, 'tm', split_axis=0, concat_axis=0, tiled=True)  70.8 us
    pallas_call x9, Pallas kernels, call(): pl.pallas_call(kernel, out_shape=outs, in_specs=specs(*ins), out_specs=sp...  38.4 us
    all_to_all x4, starting transfers between devices, exchange(): return lax.all_to_all(blocks, 'tm', split_axis=0, concat_axis=0, tiled=True)  28.5 us
    ppermute x2, starting transfers between devices, share_rows(): below = lax.ppermute(head, 'space', [(i + 1, i) for i in range(ends)])  7.28 us
    ppermute x2, starting transfers between devices, share_rows(): above = lax.ppermute(tail, 'space', [(i, i + 1) for i in range(ends)])  3.83 us
  transfers between devices with their start and end apart: 8, of which 6 were waited for; matrix products, arithmetic and copies ran while one was open for 0% of the time, Pallas kernels for 17%

profile of v6, /device:TPU:10, one launch (start us, length us, event | category | flops | bytes accessed | tf_op | source)
XLA Modules:
  0.0 153.4 jit_solution(8141765733349291980)
XLA Ops:
  0.6 2.2 %shard_map.106 = bf16[32,4,16,256]{3,2,1,0:T(8,128)(2,1)} custom-call(bf16[4,32,16,256]{3,2,1,0:T(8,128)(2,1)} %bitcast.8), custom_call_target="tpu_custom_call" | custom-call | bytes 1048576 | tf_op jit(solution)/shard_map/pallas_call | solution.py:391
  2.8 11.7 %all-to-all-start.1 = ((bf16[32,4,16,256]{3,2,1,0:T(8,128)(2,1)}), bf16[32,4,16,256]{3,2,1,0:T(8,128)(2,1)S(1)}, u32[]{:S(2)}, u32[]{:S(2)}) async-start(bf16[32,4,16,256]{3,2,1,0:T(8,128)(2,1)} %shard_map.106), calls=%async_computation.1 | async-start | bytes 2097152 | tf_op jit(solution)/shard_map/all_to_all | solution.py:366
  14.6 1.7 %shard_map.104 = (bf16[4,64,256]{2,1,0:T(8,128)(2,1)S(1)}, bf16[4,64,256]{2,1,0:T(8,128)(2,1)S(1)}) custom-call(s32[8]{0:T(128)} %row_count.9, bf16[4,8,64,256]{3,2,1,0:T(8,128)(2,1)} %field.3), custom_call_target="tpu_custom_call" | custom-call | bytes 262144 | tf_op jit(solution)/shard_map/pallas_call | solution.py:391
  16.2 1.9 %collective-permute-start = (bf16[4,64,256]{2,1,0:T(8,128)(2,1)S(1)}, bf16[4,64,256]{2,1,0:T(8,128)(2,1)S(1)}, u32[]{:S(2)}, u32[]{:S(2)}) collective-permute-start(bf16[4,64,256]{2,1,0:T(8,128)(2,1)S(1)} %get-tuple-element.13), channel_id=1, source_target_pairs={{0,1},{1,2},{2,3},{3,4},{4,5},{5,6},{6,7},{8,9},{9,10},{10,11},{11... | collective-permute-start | bytes 393224 | tf_op jit(solution)/shard_map/ppermute | solution.py:360
  18.1 3.6 %collective-permute-start.1 = (bf16[4,64,256]{2,1,0:T(8,128)(2,1)S(1)}, bf16[4,64,256]{2,1,0:T(8,128)(2,1)S(1)}, u32[]{:S(2)}, u32[]{:S(2)}) collective-permute-start(bf16[4,64,256]{2,1,0:T(8,128)(2,1)S(1)} %get-tuple-element.14), channel_id=1, source_target_pairs={{1,0},{2,1},{3,2},{4,3},{5,4},{6,5},{7,6},{9,8},{10,9},{11,10},{12... | collective-permute-start | bytes 393224 | tf_op jit(solution)/shard_map/ppermute | solution.py:361
  21.8 0.7 collective-permute-done.above
  22.5 1.8 %collective-permute-done.1.below = bf16[4,64,256]{2,1,0:T(8,128)(2,1)S(1)} collective-permute-done((bf16[4,64,256]{2,1,0:T(8,128)(2,1)S(1)}, bf16[4,64,256]{2,1,0:T(8,128)(2,1)S(1)}, u32[]{:S(2)}, u32[]{:S(2)}) %collective-permute-start.1) | collective-permute-done | bytes 131104 | tf_op jit(solution)/shard_map/ppermute | solution.py:361
  24.3 6.7 %shard_map.105 = (bf16[32,4,16,256]{3,2,1,0:T(8,128)(2,1)}, bf16[32,4,16,256]{3,2,1,0:T(8,128)(2,1)}) custom-call(s32[32]{0:T(128)} %frame_count.7, s32[8]{0:T(128)} %row_count.9, bf16[4,8,64,256]{3,2,1,0:T(8,128)(2,1)} %field.3, bf16[4,64,256]{2,1,0:T(8,128)(2,1)S(1)} %collective-permute-done.above, bf16[4,64,256]{2,1,0:T(8,128)(2,1)S(1)} %collective-permute-done.1.below, ...), custom_call_target="tpu_custom_call" | custom-call | flops 2415919104 | bytes 4194304 | tf_op jit(solution)/shard_map/pallas_call | solution.py:391
  31.0 0.0 copy-start.3
  31.0 11.6 %all-to-all-done.1 = bf16[32,4,16,256]{3,2,1,0:T(8,128)(2,1)S(1)} async-done(((bf16[32,4,16,256]{3,2,1,0:T(8,128)(2,1)}), bf16[32,4,16,256]{3,2,1,0:T(8,128)(2,1)S(1)}, u32[]{:S(2)}, u32[]{:S(2)}) %all-to-all-start.1) | async-done | bytes 1048608 | tf_op jit(solution)/shard_map/all_to_all | solution.py:366
  42.6 5.6 %all-to-all-start = ((bf16[32,4,16,256]{3,2,1,0:T(8,128)(2,1)}), bf16[32,4,16,256]{3,2,1,0:T(8,128)(2,1)S(1)}, u32[]{:S(2)}, u32[]{:S(2)}) async-start(bf16[32,4,16,256]{3,2,1,0:T(8,128)(2,1)} %get-tuple-element.16), calls=%async_computation | async-start | bytes 2097152 | tf_op jit(solution)/shard_map/all_to_all | solution.py:366
  48.2 0.0 copy-done.3
  48.2 0.1 fusion
  48.3 0.1 reshape.35
  48.4 0.1 iota.10.used
  48.5 3.5 %shard_map.107 = (bf16[16,128,256]{2,1,0:T(8,128)(2,1)}, bf16[256,256]{1,0:T(8,128)(2,1)}) custom-call(bf16[128,16,256]{2,1,0:T(8,128)(2,1)S(1)} %bitcast.6, f32[128,128]{1,0:T(8,128)S(1)} %iota.10.used, bf16[256,256]{1,0:T(8,128)(2,1)} %w_out.3, bf16[256,256]{1,0:T(8,128)(2,1)} %w_query.3, bf16[256,256]{1,0:T(8,128)(2,1)} %w_key.3, bf16[256,256]{1,0:T(8,128)(2,1)} %w_value.3), custom_call_target="tpu_custom_call" | custom-call | flops 536870912 | bytes 2097152 | tf_op jit(solution)/shard_map/pallas_call | solution.py:391
  51.9 23.3 %all-to-all-done = bf16[32,4,16,256]{3,2,1,0:T(8,128)(2,1)S(1)} async-done(((bf16[32,4,16,256]{3,2,1,0:T(8,128)(2,1)}), bf16[32,4,16,256]{3,2,1,0:T(8,128)(2,1)S(1)}, u32[]{:S(2)}, u32[]{:S(2)}) %all-to-all-start) | async-done | bytes 1048608 | tf_op jit(solution)/shard_map/all_to_all | solution.py:366
  75.2 4.9 %shard_map.108 = (bf16[128,16,256]{2,1,0:T(8,128)(2,1)}, bf16[16,128,256]{2,1,0:T(8,128)(2,1)}) custom-call(bf16[128,16,256]{2,1,0:T(8,128)(2,1)S(1)} %bitcast.7, bf16[16,128,256]{2,1,0:T(8,128)(2,1)} %get-tuple-element.17.folded, f32[128,128]{1,0:T(8,128)S(1)} %iota.10.used, bf16[256,256]{1,0:T(8,128)(2,1)} %get-tuple-element.18.mixed), custom_call_target="tpu_custom_call" | custom-call | flops 1207959552 | bytes 4194304 | tf_op jit(solution)/shard_map/pallas_call | solution.py:391
  80.1 5.6 %all-to-all-start.3 = ((bf16[32,4,16,256]{3,2,1,0:T(8,128)(2,1)}), bf16[32,4,16,256]{3,2,1,0:T(8,128)(2,1)S(1)}, u32[]{:S(2)}, u32[]{:S(2)}) async-start(bf16[32,4,16,256]{3,2,1,0:T(8,128)(2,1)} %bitcast.10), calls=%async_computation.3 | async-start | bytes 2097152 | tf_op jit(solution)/shard_map/all_to_all | solution.py:366
  85.7 7.6 %shard_map.109 = bf16[128,16,256]{2,1,0:T(8,128)(2,1)} custom-call(bf16[2048,256]{1,0:T(8,128)(2,1)} %bitcast.11, f32[128,128]{1,0:T(8,128)S(1)} %iota.10.used, bf16[256,256]{1,0:T(8,128)(2,1)} %w_query.3, bf16[256,256]{1,0:T(8,128)(2,1)} %w_key.3, bf16[256,256]{1,0:T(8,128)(2,1)} %w_value.3, bf16[256,256]{1,0:T(8,128)(2,1)} %w_out.3), custom_call_target="tpu_custom_call" | custom-call | flops 1342177280 | bytes 2097152 | tf_op jit(solution)/shard_map/pallas_call | solution.py:391
  93.3 19.0 %all-to-all-done.3.grad_normed = bf16[32,4,16,256]{3,2,1,0:T(8,128)(2,1)S(1)} async-done(((bf16[32,4,16,256]{3,2,1,0:T(8,128)(2,1)}), bf16[32,4,16,256]{3,2,1,0:T(8,128)(2,1)S(1)}, u32[]{:S(2)}, u32[]{:S(2)}) %all-to-all-start.3) | async-done | bytes 1048608 | tf_op jit(solution)/shard_map/all_to_all | solution.py:366
  112.3 0.0 copy-start.1
  112.3 1.0 copy-done.1
  113.3 0.0 copy-start.2
  113.3 5.7 %all-to-all-start.2 = ((bf16[32,4,16,256]{3,2,1,0:T(8,128)(2,1)}), bf16[32,4,16,256]{3,2,1,0:T(8,128)(2,1)S(1)}, u32[]{:S(2)}, u32[]{:S(2)}) async-start(bf16[32,4,16,256]{3,2,1,0:T(8,128)(2,1)} %bitcast.9), calls=%async_computation.2 | async-start | bytes 2097152 | tf_op jit(solution)/shard_map/all_to_all | solution.py:366
  119.0 0.0 copy-done.2
  119.0 0.0 copy-start
  119.0 4.0 %shard_map.111 = (bf16[4,8,64,256]{3,2,1,0:T(8,128)(2,1)}, bf16[4,64,256]{2,1,0:T(8,128)(2,1)}, bf16[4,64,256]{2,1,0:T(8,128)(2,1)}) custom-call(s32[32]{0:T(128)} %frame_count.7, s32[8]{0:T(128)} %row_count.9, bf16[4,8,64,256]{3,2,1,0:T(8,128)(2,1)} %cotangent.1, bf16[32,4,16,256]{3,2,1,0:T(8,128)(2,1)} %get-tuple-element.15.hidden, ...), custom_call_target="tpu_custom_call" | custom-call | bytes 5242880 | tf_op jit(solution)/shard_map/pallas_call | solution.py:391
  123.0 1.9 %collective-permute-start.2 = (bf16[4,64,256]{2,1,0:T(8,128)(2,1)}, bf16[4,64,256]{2,1,0:T(8,128)(2,1)S(1)}, u32[]{:S(2)}, u32[]{:S(2)}) collective-permute-start(bf16[4,64,256]{2,1,0:T(8,128)(2,1)} %get-tuple-element.22), channel_id=1, source_target_pairs={{0,1},{1,2},{2,3},{3,4},{4,5},{5,6},{6,7},{8,9},{9,10},{10,11},{11... | collective-permute-start | bytes 393224 | tf_op jit(solution)/shard_map/ppermute | solution.py:360
  124.9 3.6 %collective-permute-start.3 = (bf16[4,64,256]{2,1,0:T(8,128)(2,1)}, bf16[4,64,256]{2,1,0:T(8,128)(2,1)S(1)}, u32[]{:S(2)}, u32[]{:S(2)}) collective-permute-start(bf16[4,64,256]{2,1,0:T(8,128)(2,1)} %get-tuple-element.23), channel_id=1, source_target_pairs={{1,0},{2,1},{3,2},{4,3},{5,4},{6,5},{7,6},{9,8},{10,9},{11,10},{12... | collective-permute-start | bytes 393224 | tf_op jit(solution)/shard_map/ppermute | solution.py:361
  128.5 16.9 %all-to-all-done.2.projected = bf16[32,4,16,256]{3,2,1,0:T(8,128)(2,1)S(1)} async-done(((bf16[32,4,16,256]{3,2,1,0:T(8,128)(2,1)}), bf16[32,4,16,256]{3,2,1,0:T(8,128)(2,1)S(1)}, u32[]{:S(2)}, u32[]{:S(2)}) %all-to-all-start.2) | async-done | bytes 1048608 | tf_op jit(solution)/shard_map/all_to_all | solution.py:366
  145.5 0.0 copy-done
  145.5 1.9 %shard_map.110 = bf16[4,8,64,256]{3,2,1,0:T(8,128)(2,1)} custom-call(s32[32]{0:T(128)} %frame_count.7, s32[8]{0:T(128)} %row_count.9, bf16[32,4,16,256]{3,2,1,0:T(8,128)(2,1)S(1)} %copy-done, bf16[32,4,16,256]{3,2,1,0:T(8,128)(2,1)S(1)} %all-to-all-done.2.projected), custom_call_target="tpu_custom_call" | custom-call | bytes 3145728 | tf_op jit(solution)/shard_map/pallas_call | solution.py:391
  147.4 0.0 collective-permute-done.2.above
  147.4 0.0 collective-permute-done.3.below
  147.4 6.0 %shard_map.112 = bf16[4,8,64,256]{3,2,1,0:T(8,128)(2,1)} custom-call(s32[32]{0:T(128)} %frame_count.7, s32[8]{0:T(128)} %row_count.9, bf16[4,8,64,256]{3,2,1,0:T(8,128)(2,1)} %get-tuple-element.21.field, bf16[4,64,256]{2,1,0:T(8,128)(2,1)S(1)} %collective-permute-done.2.above, bf16[4,64,256]{2,1,0:T(8,128)(2,1)S(1)} %collective-permute-done.3.below, ...), custom_call_target="tpu_custom_call" | custom-call | flops 2415919104 | bytes 3145728 | tf_op jit(solution)/shard_map/pallas_call | solution.py:391
Async XLA Ops:
  2.8 39.8 %all-to-all-start.1 = ((bf16[32,4,16,256]{3,2,1,0:T(8,128)(2,1)}), bf16[32,4,16,256]{3,2,1,0:T(8,128)(2,1)S(1)}, u32[]{:S(2)}, u32[]{:S(2)}) async-start(bf16[32,4,16,256]{3,2,1,0:T(8,128)(2,1)} %shard_map.106), calls=%async_computation.1 | async-start | bytes 2097152 | tf_op jit(solution)/shard_map/all_to_all | solution.py:366
  16.2 6.3 %collective-permute-start = (bf16[4,64,256]{2,1,0:T(8,128)(2,1)S(1)}, bf16[4,64,256]{2,1,0:T(8,128)(2,1)S(1)}, u32[]{:S(2)}, u32[]{:S(2)}) collective-permute-start(bf16[4,64,256]{2,1,0:T(8,128)(2,1)S(1)} %get-tuple-element.13), channel_id=1, source_target_pairs={{0,1},{1,2},{2,3},{3,4},{4,5},{5,6},{6,7},{8,9},{9,10},{10,11},{11... | collective-permute-start | bytes 393224 | tf_op jit(solution)/shard_map/ppermute | solution.py:360
  18.1 6.1 %collective-permute-start.1 = (bf16[4,64,256]{2,1,0:T(8,128)(2,1)S(1)}, bf16[4,64,256]{2,1,0:T(8,128)(2,1)S(1)}, u32[]{:S(2)}, u32[]{:S(2)}) collective-permute-start(bf16[4,64,256]{2,1,0:T(8,128)(2,1)S(1)} %get-tuple-element.14), channel_id=1, source_target_pairs={{1,0},{2,1},{3,2},{4,3},{5,4},{6,5},{7,6},{9,8},{10,9},{11,10},{12... | collective-permute-start | bytes 393224 | tf_op jit(solution)/shard_map/ppermute | solution.py:361
  31.0 17.2 %copy-start.3 = (s32[32]{0:T(128)S(1)}, s32[32]{0:T(128)}, u32[]{:S(2)}) copy-start(s32[32]{0:T(128)} %frame_count.7) | copy-start | bytes 388
  42.6 32.6 %all-to-all-start = ((bf16[32,4,16,256]{3,2,1,0:T(8,128)(2,1)}), bf16[32,4,16,256]{3,2,1,0:T(8,128)(2,1)S(1)}, u32[]{:S(2)}, u32[]{:S(2)}) async-start(bf16[32,4,16,256]{3,2,1,0:T(8,128)(2,1)} %get-tuple-element.16), calls=%async_computation | async-start | bytes 2097152 | tf_op jit(solution)/shard_map/all_to_all | solution.py:366
  80.1 32.2 %all-to-all-start.3 = ((bf16[32,4,16,256]{3,2,1,0:T(8,128)(2,1)}), bf16[32,4,16,256]{3,2,1,0:T(8,128)(2,1)S(1)}, u32[]{:S(2)}, u32[]{:S(2)}) async-start(bf16[32,4,16,256]{3,2,1,0:T(8,128)(2,1)} %bitcast.10), calls=%async_computation.3 | async-start | bytes 2097152 | tf_op jit(solution)/shard_map/all_to_all | solution.py:366
  112.3 1.0 copy-start.1
  113.3 5.7 %copy-start.2 = (bf16[32,4,16,256]{3,2,1,0:T(8,128)(2,1)S(1)}, bf16[32,4,16,256]{3,2,1,0:T(8,128)(2,1)}, u32[]{:S(2)}) copy-start(bf16[32,4,16,256]{3,2,1,0:T(8,128)(2,1)} %copy-done.1) | copy-start | bytes 3145732
  113.3 32.2 %all-to-all-start.2 = ((bf16[32,4,16,256]{3,2,1,0:T(8,128)(2,1)}), bf16[32,4,16,256]{3,2,1,0:T(8,128)(2,1)S(1)}, u32[]{:S(2)}, u32[]{:S(2)}) async-start(bf16[32,4,16,256]{3,2,1,0:T(8,128)(2,1)} %bitcast.9), calls=%async_computation.2 | async-start | bytes 2097152 | tf_op jit(solution)/shard_map/all_to_all | solution.py:366
  119.0 26.5 %copy-start = (bf16[32,4,16,256]{3,2,1,0:T(8,128)(2,1)S(1)}, bf16[32,4,16,256]{3,2,1,0:T(8,128)(2,1)}, u32[]{:S(2)}) copy-start(bf16[32,4,16,256]{3,2,1,0:T(8,128)(2,1)} %get-tuple-element.15.hidden) | copy-start | bytes 3145732
  123.0 24.4 %collective-permute-start.2 = (bf16[4,64,256]{2,1,0:T(8,128)(2,1)}, bf16[4,64,256]{2,1,0:T(8,128)(2,1)S(1)}, u32[]{:S(2)}, u32[]{:S(2)}) collective-permute-start(bf16[4,64,256]{2,1,0:T(8,128)(2,1)} %get-tuple-element.22), channel_id=1, source_target_pairs={{0,1},{1,2},{2,3},{3,4},{4,5},{5,6},{6,7},{8,9},{9,10},{10,11},{11... | collective-permute-start | bytes 393224 | tf_op jit(solution)/shard_map/ppermute | solution.py:360
  124.9 22.5 %collective-permute-start.3 = (bf16[4,64,256]{2,1,0:T(8,128)(2,1)}, bf16[4,64,256]{2,1,0:T(8,128)(2,1)S(1)}, u32[]{:S(2)}, u32[]{:S(2)}) collective-permute-start(bf16[4,64,256]{2,1,0:T(8,128)(2,1)} %get-tuple-element.23), channel_id=1, source_target_pairs={{1,0},{2,1},{3,2},{4,3},{5,4},{6,5},{7,6},{9,8},{10,9},{11,10},{12... | collective-permute-start | bytes 393224 | tf_op jit(solution)/shard_map/ppermute | solution.py:361
